TPU v7x, 512 devices: a whole 4x8x8 slice. The times are simulated.
512 devices in a mesh: fsdp: 32 (over z_hi, x, core), seq: 16 (over z_lo, y).
Axes of the slice: x: 4, y: 8, z: 8 (z_hi: 4, z_lo: 2; z = z_hi * 2 + z_lo), core: 2. Of those that a mesh axis runs over, the one named last changes fastest.
Arguments:
- video_qkv: bfloat16 [32, 2048, 3, 4096], P('fsdp', 'seq'), may hold values from -6 to 6
- reference_rows: bfloat16 [32, 64, 5120], P('fsdp', 'seq'), may hold values from -150 to 150
- kv_weight: bfloat16 [5120, 2, 4096], P('fsdp', None, 'seq'), may hold values from -0.125 to 0.125
- pose_table: bfloat16 [256, 4096], P('fsdp', 'seq'), may hold values from -6 to 6
- pose_ids: int32 [32, 2048], P('fsdp', 'seq'), may hold values from 0 to 255
- frame_counts: int32 [32], P('fsdp'), may hold values from 1 to 4, as said below
Outputs:
- attended: bfloat16 [32, 2048, 4096], P('fsdp', 'seq')
Inputs may be any that keep to these rules, and one draw needn't show every extreme that they name: `frame_counts`: every clip has 1 to 4 reference frames in the window, each making 16 slots live; in every draw some clip has exactly 4 and another exactly 1.
All inputs are finite; a program needn't handle non-finite values.
Results may differ from a plain program's by a relative error of at most 0.011.
Values may be sent and summed in bfloat16 or wider, within the bound.
No kernel may reach another device: no remote copies, remote signals or barrier semaphores. Data moves between devices by JAX's collectives and lax.ppermute only.
A program may use at most 64 MiB of HBM per device.

v0:
```python
import math

import jax
import jax.numpy as jnp
from jax import lax
from jax.sharding import PartitionSpec as P

HD = 128
TPF = 16
POSE = 256


def layer_norm(row_block):
    row_mean = jnp.mean(row_block, axis=-1, keepdims=True)
    centered = row_block - row_mean
    row_var = jnp.mean(centered * centered, axis=-1, keepdims=True)
    return centered * lax.rsqrt(row_var + 1e-06)


def pose_lookup(token_ids, codebook):
    onehot = (token_ids[:, None] == jnp.arange(POSE, dtype=jnp.int32)[None, :]).astype(jnp.bfloat16)
    return jnp.dot(onehot, codebook, preferred_element_type=jnp.float32)


def shards(video_qkv, reference_rows, kv_weight, pose_table, pose_ids, frame_counts):
    score_scale = 1.0 / math.sqrt(HD)
    query_part = video_qkv[:, :, 0:1, :]
    pair_part = video_qkv[:, :, 1:3, :]
    codebook_cols = lax.all_gather(pose_table, "seq", axis=1, tiled=True)
    codebook = lax.all_gather(codebook_cols, "fsdp", axis=0, tiled=True)
    lookup = pose_lookup(pose_ids[0], codebook)
    query_part = (query_part.astype(jnp.float32) + lookup[None, :, None, :]).astype(jnp.bfloat16)
    query_heads, pair_heads = (
        lax.all_to_all(query_part, "seq", split_axis=3, concat_axis=1, tiled=True),
        lax.all_to_all(pair_part, "seq", split_axis=3, concat_axis=1, tiled=True),
    )
    normed = layer_norm(reference_rows[0].astype(jnp.float32)).astype(jnp.bfloat16)
    all_rows = lax.all_gather(normed, "seq", axis=0, tiled=True)
    ref_count = all_rows.shape[0]
    head_width = kv_weight.shape[2]
    piece = lax.all_gather(kv_weight, "fsdp", axis=0, tiled=True)
    kv_sum = jnp.dot(
        all_rows, piece.reshape(piece.shape[0], 2 * head_width), preferred_element_type=jnp.float32
    )
    ref_kv = kv_sum.astype(jnp.bfloat16).reshape(ref_count, 2, head_width)
    video_len = query_heads.shape[1]
    heads_here = head_width // HD
    key_total = video_len + ref_count
    key_rows = jnp.concatenate([pair_heads[0, :, 0, :], ref_kv[:, 0, :]], axis=0).reshape(
        key_total, heads_here, HD
    )
    value_rows = jnp.concatenate([pair_heads[0, :, 1, :], ref_kv[:, 1, :]], axis=0).reshape(
        key_total, heads_here, HD
    )
    live_keys = jnp.arange(key_total, dtype=jnp.int32) < video_len + TPF * frame_counts[0]
    block_rows = min(512, video_len)
    block_count = video_len // block_rows

    def attend(query_block):
        scores = (
            jnp.einsum("bhd,khd->hbk", query_block, key_rows, preferred_element_type=jnp.float32)
            * score_scale
        )
        scores = jnp.where(live_keys[None, None, :], scores, -1e30)
        row_max = jnp.max(scores, axis=-1, keepdims=True)
        expo = jnp.where(live_keys[None, None, :], jnp.exp(scores - row_max), 0.0)
        row_total = jnp.sum(expo, axis=-1, keepdims=True)
        weights = (expo / row_total).astype(jnp.bfloat16)
        mixed = jnp.einsum("hbk,khd->bhd", weights, value_rows, preferred_element_type=jnp.float32)
        return mixed.astype(jnp.bfloat16)

    query_blocks = query_heads.reshape(block_count, block_rows, heads_here, HD)
    attended = lax.map(attend, query_blocks).reshape(1, video_len, head_width)
    return lax.all_to_all(attended, "seq", split_axis=1, concat_axis=2, tiled=True)


def solution(mesh):
    placed = (
        P("fsdp", "seq", None, None),
        P("fsdp", "seq", None),
        P("fsdp", None, "seq"),
        P("fsdp", "seq"),
        P("fsdp", "seq"),
        P("fsdp"),
    )
    return jax.shard_map(
        shards, mesh=mesh, in_specs=placed, out_specs=P("fsdp", "seq", None), check_vma=False
    )
```

profile of v0, /device:TPU:4, one launch (start us, length us, event | category | flops | bytes accessed | tf_op | source)
XLA Modules:
  0.0 340.3 jit_solution(14495082860246076433)
XLA Ops:
  6.5 37.7 %all_gather.12 = bf16[8,4096]{1,0:T(8,128)(2,1)} all-gather(bf16[8,256]{1,0:T(8,128)(2,1)} %param.11), channel_id=1, replica_groups=mesh['fsdp'=32,'seq'=16] {'seq'}, dimensions={1}, use_global_device_ids=true | all-gather | bytes 69632 | tf_op jit(solution)/shard_map/all_gather | solution.py:29
  44.3 0.7 all-gather.6.cloned.1.call-update
  45.0 1.6 slice-done
  46.6 3.8 %copy.76 = bf16[1,128,2,4096]{1,2,0,3:T(2,128)(2,1)} copy(bf16[1,128,2,4096]{3,1,2,0:T(8,128)(2,1)S(1)} %slice-done) | data formatting | bytes 4194304
  50.3 3.8 %all-to-all-start.1 = ((bf16[1,128,2,4096]{1,2,0,3:T(2,128)(2,1)}), bf16[1,128,2,4096]{1,2,0,3:T(2,128)(2,1)S(1)}, u32[]{:S(2)}, u32[]{:S(2)}) async-start(bf16[1,128,2,4096]{1,2,0,3:T(2,128)(2,1)} %copy.76), calls=%async_computation.1 | async-start | bytes 4194304 | tf_op jit(solution)/shard_map/all_to_all | solution.py:35
  54.4 0.2 fusion.20
  54.6 53.1 %all-gather.4.cloned.1.call-done = bf16[256,4096]{1,0:T(8,128)(2,1)} async-done(((bf16[8,4096]{1,0:T(8,128)(2,1)}), bf16[256,4096]{1,0:T(8,128)(2,1)}) %all-gather.4.cloned.1.call-update) | async-done | bytes 2097168 | tf_op jit(solution)/shard_map/all_gather | solution.py:30
  107.7 2.3 fusion.16
  110.1 3.9 %copy.51 = bf16[1,128,1,4096]{1,2,0,3:T(2,128)(2,1)} copy(bf16[1,128,1,4096]{3,1,2,0:T(8,128)(2,1)S(1)} %fusion.16) | data formatting | bytes 2097152 | tf_op jit(solution)/shard_map/convert_element_type | solution.py:32
  114.0 0.6 broadcast.42
  114.6 23.4 %reduce.1 = bf16[4096,128]{1,0:T(8,128)(2,1)S(1)} reduce(bf16[4096,1,1,128]{3,2,1,0:T(2,128)(2,1)} %bitcast.78, bf16[]{:T(256)} %broadcast.42), dimensions={1,2}, to_apply=%bitcast.56.reduce_sub_computation | reduce | bytes 2097154
  138.0 1.1 reshape.51
  139.2 9.9 %all-to-all-start = ((bf16[16,2,16384]{2,1,0:T(2,128)(2,1)}), bf16[16,2,16384]{2,1,0:T(2,128)(2,1)S(1)}, u32[]{:S(2)}, u32[]{:S(2)}) async-start(bf16[16,2,16384]{2,1,0:T(2,128)(2,1)} %reshape.51), calls=%async_computation | async-start | bytes 2097152 | tf_op jit(solution)/shard_map/all_to_all | solution.py:34
  149.2 58.6 %all-gather = bf16[16,4,5120]{2,1,0:T(4,128)(2,1)} all-gather(bf16[1,4,5120]{2,1,0:T(4,128)(2,1)S(1)} %fusion.23), channel_id=1, replica_groups=mesh['fsdp'=32,'seq'=16] {'seq'}, dimensions={0}, use_global_device_ids=true | all-gather | bytes 696320 | tf_op jit(solution)/shard_map/all_gather | solution.py:38
  207.8 2.3 reshape.49
  210.7 1.6 copy.54
  212.3 2.9 copy.55
  215.2 1.5 fusion.25
  216.7 2.3 copy.56
  219.1 1.4 copy.59
  220.5 1.0 reshape.52
  221.7 1.4 copy.52
  223.0 1.3 reshape.44
  224.4 3.4 %copy.81 = bf16[640,8,2,256]{3,1,2,0:T(8,128)(2,1)S(1)} copy(bf16[640,8,2,256]{3,2,1,0:T(2,128)(2,1)} %bitcast.82) | data formatting | bytes 10485760
  227.9 1.0 convolution_convert_fusion
  229.2 1.4 pad_maximum_fusion
  230.6 1.4 copy.63
  232.2 1.4 copy.64
  233.6 55.6 %while.11 = (s32[]{:T(128)}, bf16[4,512,2,128]{3,2,1,0:T(2,128)(2,1)}, bf16[4,512,2,128]{3,2,1,0:T(2,128)(2,1)S(1)}, bf16[2112,2,128]{2,0,1:T(8,128)(2,1)S(1)}, ...) while((s32[]{:T(128)}, bf16[4,512,2,128]{3,2,1,0:T(2,128)(2,1)}, ...), condition=%wide.region_5.6_spmd.clone, body=%wide.region_2.5_spmd.clone.sunk | while | flops 1122570368 | bytes 25375472 | solution.py:73
  233.8 7.4 %fusion.38 = (f32[2,512]{1,0:T(2,128)S(1)}, f32[2,512,2112]{1,2,0:T(8,128)}) fusion(pred[2112]{0:T(1024)(128)(4,1)S(1)} %iota_compare_fusion.4, bf16[2112,2,128]{2,0,1:T(8,128)(2,1)S(1)} %get-tuple-element.153, bf16[1,512,2,128]{3,2,1,0:T(2,128)(2,1)S(1)} %constant_dynamic-slice_fusion.2), kind=kOutput, calls=%fused_computation.38.clone.1 | convolution fusion | flops 564463680 | bytes 10000448 | tf_op jit(solution)/shard_map/while/body/eval_jaxpr/sub | solution.py:66
  241.2 5.3 %fusion.39 = bf16[1,512,2,128]{3,1,2,0:T(8,128)(2,1)S(1)} fusion(bf16[2112,2,128]{2,0,1:T(8,128)(2,1)S(1)} %copy-done.4, f32[2,512,2112]{1,2,0:T(8,128)} %get-tuple-element.134, f32[2,512]{1,0:T(2,128)S(1)} %get-tuple-element.135), kind=kOutput, calls=%fused_computation.11.clone.1 | convolution fusion | flops 558104576 | bytes 9998336 | tf_op jit(solution)/shard_map/while/body/eval_jaxpr/hbk,khd->bhd/dot_general | solution.py:69
  246.5 1.0 copy_dynamic-update-slice_fusion.2
  247.7 7.4 %fusion.38 = (f32[2,512]{1,0:T(2,128)S(1)}, f32[2,512,2112]{1,2,0:T(8,128)}) fusion(pred[2112]{0:T(1024)(128)(4,1)S(1)} %iota_compare_fusion.4, bf16[2112,2,128]{2,0,1:T(8,128)(2,1)S(1)} %get-tuple-element.153, bf16[1,512,2,128]{3,2,1,0:T(2,128)(2,1)S(1)} %constant_dynamic-slice_fusion.2), kind=kOutput, calls=%fused_computation.38.clone.1 | convolution fusion | flops 564463680 | bytes 10000448 | tf_op jit(solution)/shard_map/while/body/eval_jaxpr/sub | solution.py:66
  255.1 5.3 %fusion.39 = bf16[1,512,2,128]{3,1,2,0:T(8,128)(2,1)S(1)} fusion(bf16[2112,2,128]{2,0,1:T(8,128)(2,1)S(1)} %copy-done.4, f32[2,512,2112]{1,2,0:T(8,128)} %get-tuple-element.134, f32[2,512]{1,0:T(2,128)S(1)} %get-tuple-element.135), kind=kOutput, calls=%fused_computation.11.clone.1 | convolution fusion | flops 558104576 | bytes 9998336 | tf_op jit(solution)/shard_map/while/body/eval_jaxpr/hbk,khd->bhd/dot_general | solution.py:69
  260.4 1.0 copy_dynamic-update-slice_fusion.2
  261.6 7.4 %fusion.38 = (f32[2,512]{1,0:T(2,128)S(1)}, f32[2,512,2112]{1,2,0:T(8,128)}) fusion(pred[2112]{0:T(1024)(128)(4,1)S(1)} %iota_compare_fusion.4, bf16[2112,2,128]{2,0,1:T(8,128)(2,1)S(1)} %get-tuple-element.153, bf16[1,512,2,128]{3,2,1,0:T(2,128)(2,1)S(1)} %constant_dynamic-slice_fusion.2), kind=kOutput, calls=%fused_computation.38.clone.1 | convolution fusion | flops 564463680 | bytes 10000448 | tf_op jit(solution)/shard_map/while/body/eval_jaxpr/sub | solution.py:66
  269.0 5.3 %fusion.39 = bf16[1,512,2,128]{3,1,2,0:T(8,128)(2,1)S(1)} fusion(bf16[2112,2,128]{2,0,1:T(8,128)(2,1)S(1)} %copy-done.4, f32[2,512,2112]{1,2,0:T(8,128)} %get-tuple-element.134, f32[2,512]{1,0:T(2,128)S(1)} %get-tuple-element.135), kind=kOutput, calls=%fused_computation.11.clone.1 | convolution fusion | flops 558104576 | bytes 9998336 | tf_op jit(solution)/shard_map/while/body/eval_jaxpr/hbk,khd->bhd/dot_general | solution.py:69
  274.3 1.0 copy_dynamic-update-slice_fusion.2
  275.5 7.4 %fusion.38 = (f32[2,512]{1,0:T(2,128)S(1)}, f32[2,512,2112]{1,2,0:T(8,128)}) fusion(pred[2112]{0:T(1024)(128)(4,1)S(1)} %iota_compare_fusion.4, bf16[2112,2,128]{2,0,1:T(8,128)(2,1)S(1)} %get-tuple-element.153, bf16[1,512,2,128]{3,2,1,0:T(2,128)(2,1)S(1)} %constant_dynamic-slice_fusion.2), kind=kOutput, calls=%fused_computation.38.clone.1 | convolution fusion | flops 564463680 | bytes 10000448 | tf_op jit(solution)/shard_map/while/body/eval_jaxpr/sub | solution.py:66
  282.9 5.3 %fusion.39 = bf16[1,512,2,128]{3,1,2,0:T(8,128)(2,1)S(1)} fusion(bf16[2112,2,128]{2,0,1:T(8,128)(2,1)S(1)} %copy-done.4, f32[2,512,2112]{1,2,0:T(8,128)} %get-tuple-element.134, f32[2,512]{1,0:T(2,128)S(1)} %get-tuple-element.135), kind=kOutput, calls=%fused_computation.11.clone.1 | convolution fusion | flops 558104576 | bytes 9998336 | tf_op jit(solution)/shard_map/while/body/eval_jaxpr/hbk,khd->bhd/dot_general | solution.py:69
  288.2 1.0 copy_dynamic-update-slice_fusion.2
  289.2 6.6 %reshape.50 = bf16[1,2048,256]{2,0,1:T(2,128)(2,1)S(1)} reshape(bf16[4,512,2,128]{3,2,1,0:T(2,128)(2,1)} %get-tuple-element.37) | data formatting | bytes 2097152 | tf_op jit(solution)/shard_map/reshape | solution.py:73
  295.8 10.6 %reduce.2 = bf16[2048,256]{1,0:T(8,128)(2,1)S(1)} reduce(bf16[2048,1,256]{2,1,0:T(2,128)(2,1)S(1)} %bitcast.80, bf16[]{:T(256)} %broadcast.42), dimensions={1}, to_apply=%bitcast.58.reduce_sub_computation | reduce | bytes 2097154
  306.4 0.3 reshape.53
  306.7 23.5 %all_to_all.51 = bf16[16,2,16384]{2,1,0:T(2,128)(2,1)S(1)} all-to-all(bf16[16,2,16384]{2,1,0:T(2,128)(2,1)S(1)} %reshape.53), channel_id=1, replica_groups=mesh['fsdp'=32,'seq'=16] {'seq'}, dimensions={0} | all-to-all | bytes 2097152 | tf_op jit(solution)/shard_map/all_to_all | solution.py:74
  330.2 1.0 reshape.54
  331.4 0.7 copy.67
  332.1 1.3 copy.68
  (47 shorter events, 1.9 us)
Async XLA Ops:
  6.5 101.2 %all-gather.4.cloned.1.call-start = ((), (), s32[]{:S(2)}) async-start(), calls=%async_computation.3 | async-start | bytes 2162688 | tf_op jit(solution)/shard_map/all_gather | solution.py:30
  44.2 180.2 %all-gather.6.cloned.1.call-start = ((), (), s32[]{:S(2)}) async-start(), calls=%async_computation.4 | async-start | bytes 5406720 | tf_op jit(solution)/shard_map/all_gather | solution.py:41
  45.0 1.6 slice-start
  50.3 3.9 %copy-start.5 = (bf16[1,4,5120]{2,1,0:T(4,128)(2,1)S(1)}, bf16[1,4,5120]{2,1,0:T(4,128)(2,1)}, u32[]{:S(2)}) copy-start(bf16[1,4,5120]{2,1,0:T(4,128)(2,1)} %param.9) | copy-start | bytes 122884
  50.3 57.4 %copy-start.6 = (s32[1,128]{1,0:T(1,128)S(1)}, s32[1,128]{1,0:T(1,128)}, u32[]{:S(2)}) copy-start(s32[1,128]{1,0:T(1,128)} %param.12) | copy-start | bytes 1540
  50.3 88.8 %all-to-all-start.1 = ((bf16[1,128,2,4096]{1,2,0,3:T(2,128)(2,1)}), bf16[1,128,2,4096]{1,2,0,3:T(2,128)(2,1)S(1)}, u32[]{:S(2)}, u32[]{:S(2)}) async-start(bf16[1,128,2,4096]{1,2,0,3:T(2,128)(2,1)} %copy.76), calls=%async_computation.1 | async-start | bytes 4194304 | tf_op jit(solution)/shard_map/all_to_all | solution.py:35
  139.2 81.3 %all-to-all-start = ((bf16[16,2,16384]{2,1,0:T(2,128)(2,1)}), bf16[16,2,16384]{2,1,0:T(2,128)(2,1)S(1)}, u32[]{:S(2)}, u32[]{:S(2)}) async-start(bf16[16,2,16384]{2,1,0:T(2,128)(2,1)} %reshape.51), calls=%async_computation | async-start | bytes 2097152 | tf_op jit(solution)/shard_map/all_to_all | solution.py:34
  216.7 2.3 copy-start.1
  224.4 3.4 %copy-start.2 = (bf16[64,5120]{1,0:T(8,128)(2,1)S(1)}, bf16[64,5120]{1,0:T(8,128)(2,1)}, u32[]{:S(2)}) copy-start(bf16[64,5120]{1,0:T(8,128)(2,1)} %reshape.49) | copy-start | bytes 1966084
  229.2 2.9 copy-start
  232.2 1.4 copy-start.3
  233.8 7.4 %copy-start.4 = (bf16[2112,2,128]{2,0,1:T(8,128)(2,1)S(1)}, bf16[2112,2,128]{2,0,1:T(8,128)(2,1)}, u32[]{:S(2)}) copy-start(bf16[2112,2,128]{2,0,1:T(8,128)(2,1)} %get-tuple-element.154) | copy-start | bytes 3244036 | tf_op jit(solution)/shard_map/while
  247.7 7.4 %copy-start.4 = (bf16[2112,2,128]{2,0,1:T(8,128)(2,1)S(1)}, bf16[2112,2,128]{2,0,1:T(8,128)(2,1)}, u32[]{:S(2)}) copy-start(bf16[2112,2,128]{2,0,1:T(8,128)(2,1)} %get-tuple-element.154) | copy-start | bytes 3244036 | tf_op jit(solution)/shard_map/while
  261.6 7.4 %copy-start.4 = (bf16[2112,2,128]{2,0,1:T(8,128)(2,1)S(1)}, bf16[2112,2,128]{2,0,1:T(8,128)(2,1)}, u32[]{:S(2)}) copy-start(bf16[2112,2,128]{2,0,1:T(8,128)(2,1)} %get-tuple-element.154) | copy-start | bytes 3244036 | tf_op jit(solution)/shard_map/while
  275.5 7.4 %copy-start.4 = (bf16[2112,2,128]{2,0,1:T(8,128)(2,1)S(1)}, bf16[2112,2,128]{2,0,1:T(8,128)(2,1)}, u32[]{:S(2)}) copy-start(bf16[2112,2,128]{2,0,1:T(8,128)(2,1)} %get-tuple-element.154) | copy-start | bytes 3244036 | tf_op jit(solution)/shard_map/while
Sparse Core Ops, SparseCore 0:
  44.3 63.3 all-gather.3
  110.9 82.3 all-gather.5
where the time goes:
time: 341 us; the launch traced here: 340 us
  blocking collectives  120 us (35%)
  matrix products  54.2 us (16%)
  waiting for transfers between devices  53.9 us (16%)
  local copies, waits for them, and re-layouts  48.2 us (14%)
  other arithmetic  36 us (11%)
  between operations  14.3 us (4%)
  starting transfers between devices  13.8 us (4%)
    all_gather x1, blocking collectives, shards(): all_rows = lax.all_gather(normed, 'seq', axis=0, tiled=True)  58.6 us
    all_gather x1, waiting for transfers between devices, shards(): codebook = lax.all_gather(codebook_cols, 'fsdp', axis=0, tiled=True)  53.1 us
    all_gather x1, blocking collectives, shards(): codebook_cols = lax.all_gather(pose_table, 'seq', axis=1, tiled=True)  37.7 us
    unnamed x3, other arithmetic  34.1 us
    sub x4, matrix products, attend(): expo = jnp.where(live_keys[None, None, :], jnp.exp(scores - row_max), 0.0)  29.5 us
    all_to_all x1, blocking collectives, shards(): lax.all_to_all(attended, 'seq', split_axis=1, concat_axis=2, tiled=True)  23.5 us
    dot_general x4, matrix products, attend(): jnp.einsum('hbk,khd->bhd', weights, value_rows, preferred_element_type=jn...  21.3 us
    unnamed x24, local copies, waits for them, and re-layouts  16.6 us
  transfers between devices with their start and end apart: 4, of which 1 were waited for; matrix products, arithmetic and copies ran while one was open for 15% of the time, Pallas kernels for 0%

commit v1 on v0

v1 whole, which is shorter than its diff:
```python
import math

import jax
import jax.numpy as jnp
from jax import lax
from jax.experimental import pallas as pl
from jax.experimental.pallas import tpu as pltpu
from jax.sharding import PartitionSpec as P

HD = 128
TPF = 16
WROWS = 176
IDROWS = 16


def fsdp_perm(move):
    pairs = []
    for i in range(32):
        z, x, c = move(i // 8, i // 2 % 4, i % 2)
        pairs.append((i, z % 4 * 8 + x % 4 * 2 + c))
    return pairs


def direction(core):
    return 1 - 2 * core


Z_RING = fsdp_perm(lambda z, x, c: (z + direction(c), x, c))
X_RING = fsdp_perm(lambda z, x, c: (z, x + direction(c), c))
CORE_SWAP = fsdp_perm(lambda z, x, c: (z, x, 1 - c))


def pack_kernel(tokens, group, x_ref, rows_ref, ids_ref, first_ref, second_ref, normed):
    @pl.when(pl.program_id(0) == 0)
    def _():
        x = rows_ref[...].astype(jnp.float32)
        mean = jnp.mean(x, axis=-1, keepdims=True)
        centered = x - mean
        var = jnp.mean(centered * centered, axis=-1, keepdims=True)
        out = centered * lax.rsqrt(var + 1e-06)
        r = x.shape[0]
        for c in range(x.shape[1] // HD):
            normed[c * r : (c + 1) * r, :] = out[:, c * HD : (c + 1) * HD]

    ids = jnp.broadcast_to(ids_ref[...].astype(jnp.float32), (IDROWS, tokens)).astype(jnp.bfloat16)
    norm = normed[...].astype(jnp.bfloat16)
    for d in range(group):
        for k in range(3):
            col = d * 2 * HD
            first_ref[d, k * tokens : (k + 1) * tokens, :] = x_ref[k, :, col : col + HD]
            second_ref[d, k * tokens : (k + 1) * tokens, :] = x_ref[k, :, col + HD : col + 2 * HD]
        first_ref[d, 3 * tokens : 3 * tokens + IDROWS, :] = ids
        first_ref[d, 3 * tokens + IDROWS :, :] = norm


def pack(video, rows, ids):
    tokens, width = video.shape[1], video.shape[2]
    n = width // (2 * HD)
    nrows = rows.shape[0] * rows.shape[1] // HD
    group = 2
    long = 3 * tokens + IDROWS + nrows
    return pl.pallas_call(
        lambda *refs: pack_kernel(tokens, group, *refs),
        grid=(n // group,),
        out_shape=(
            jax.ShapeDtypeStruct((n, long, HD), jnp.bfloat16),
            jax.ShapeDtypeStruct((n, 3 * tokens, HD), jnp.bfloat16),
        ),
        in_specs=[
            pl.BlockSpec((3, tokens, group * 2 * HD), lambda i: (0, 0, i)),
            pl.BlockSpec(rows.shape, lambda i: (0, 0)),
            pl.BlockSpec(ids.shape, lambda i: (0, 0)),
        ],
        out_specs=(
            pl.BlockSpec((group, long, HD), lambda i: (i, 0, 0)),
            pl.BlockSpec((group, 3 * tokens, HD), lambda i: (i, 0, 0)),
        ),
        scratch_shapes=[pltpu.VMEM((nrows, HD), jnp.float32)],
        cost_estimate=pl.CostEstimate(flops=1 << 20, bytes_accessed=7 << 20, transcendentals=0),
        name="pack",
    )(video, rows, ids)


def ref_kernel(x_ref, own_ref, other_ref, kv_ref, book_ref, weight, codes, sem):
    me = lax.axis_index("fsdp")
    mz, mx, mc = me // 8, me // 2 % 4, me % 2
    kdim = weight.shape[0] // 32
    copies = []
    for side, src in ((0, own_ref), (1, other_ref)):
        core = mc if side == 0 else 1 - mc
        sign = 1 - 2 * core
        for kx in range(4):
            for kz in range(4):
                z = (mz - sign * kz + 4) % 4
                x = (mx - sign * kx + 4) % 4
                f = z * 8 + x * 2 + core
                row = (kx * 4 + kz) * WROWS
                copies.append(
                    pltpu.make_async_copy(
                        src.at[pl.ds(row, kdim), :],
                        weight.at[pl.ds(pl.multiple_of(f * kdim, 16), kdim), :],
                        sem.at[len(copies)],
                    )
                )
                copies.append(
                    pltpu.make_async_copy(
                        src.at[pl.ds(row + kdim, 16), pl.ds(0, 2 * HD)],
                        codes.at[pl.ds(pl.multiple_of(f * 16, 16), 16), :],
                        sem.at[len(copies)],
                    )
                )
    for c in copies:
        c.start()
    for c in copies:
        c.wait()
    kv_ref[...] = jnp.dot(x_ref[...], weight[...], preferred_element_type=jnp.float32).astype(jnp.bfloat16)
    for f in range(32):
        book_ref[f * 8 : (f + 1) * 8, :] = codes[f * 16 : f * 16 + 8, :]


def ref_project(rows, own, other):
    n = own.shape[1]
    return pl.pallas_call(
        ref_kernel,
        out_shape=(
            jax.ShapeDtypeStruct((rows.shape[0], n), jnp.bfloat16),
            jax.ShapeDtypeStruct((256, 2 * HD), jnp.bfloat16),
        ),
        in_specs=[
            pl.BlockSpec(memory_space=pltpu.VMEM),
            pl.BlockSpec(memory_space=pl.ANY),
            pl.BlockSpec(memory_space=pl.ANY),
        ],
        out_specs=(pl.BlockSpec(memory_space=pltpu.VMEM), pl.BlockSpec(memory_space=pltpu.VMEM)),
        scratch_shapes=[
            pltpu.VMEM((rows.shape[1], n), jnp.bfloat16),
            pltpu.VMEM((512, 2 * HD), jnp.bfloat16),
            pltpu.SemaphoreType.DMA((64,)),
        ],
        cost_estimate=pl.CostEstimate(flops=1 << 29, bytes_accessed=7 << 20, transcendentals=0),
        name="ref_project",
    )(rows, own, other)


def attend_kernel(tokens, count_ref, q_ref, k_ref, v_ref, ids_ref, book_ref, rk_ref, rv_ref, o_ref):
    per = q_ref.shape[0]
    entries = book_ref.shape[0]
    parts = []
    for j in range(per):
        ids = ids_ref[j, 0:1, :].astype(jnp.float32).astype(jnp.int32)
        entry = lax.broadcasted_iota(jnp.int32, (entries, tokens), 0)
        onehot = jnp.where(entry == ids, 1.0, 0.0).astype(jnp.bfloat16)
        lookup = lax.dot_general(onehot, book_ref[...], (((0,), (0,)), ((), ())), preferred_element_type=jnp.float32)
        parts.append((q_ref[j].astype(jnp.float32) + lookup).astype(jnp.bfloat16))
    q = jnp.concatenate(parts, axis=0)
    keys = k_ref[...].reshape(-1, HD)
    values = v_ref[...].reshape(-1, HD)
    scale = math.log2(math.e) / math.sqrt(HD)
    nt = (((1,), (1,)), ((), ()))
    s1 = lax.dot_general(q, keys, nt, preferred_element_type=jnp.float32)
    s2 = lax.dot_general(q, rk_ref[...], nt, preferred_element_type=jnp.float32)
    slot = lax.broadcasted_iota(jnp.int32, s2.shape, 1)
    live = slot < TPF * count_ref[0]
    s2 = jnp.where(live, s2, -1e30)
    top = jnp.maximum(jnp.max(s1, axis=-1, keepdims=True), jnp.max(s2, axis=-1, keepdims=True))
    p1 = jnp.exp2((s1 - top) * scale)
    p2 = jnp.where(live, jnp.exp2((s2 - top) * scale), 0.0)
    total = jnp.sum(p1, axis=-1, keepdims=True) + jnp.sum(p2, axis=-1, keepdims=True)
    out = jnp.dot(p1.astype(jnp.bfloat16), values, preferred_element_type=jnp.float32)
    out = out + jnp.dot(p2.astype(jnp.bfloat16), rv_ref[...], preferred_element_type=jnp.float32)
    out = out / total
    o_ref[...] = out.astype(jnp.bfloat16).reshape(o_ref.shape)


def attend(head, tokens, count, block, id_block, book, ref_kv):
    n = block.shape[0]
    per = 2
    slots = ref_kv.shape[0]
    pairs = 2048 * 2112
    return pl.pallas_call(
        lambda *refs: attend_kernel(tokens, *refs),
        grid_spec=pltpu.PrefetchScalarGridSpec(
            num_scalar_prefetch=1,
            grid=(n // per,),
            in_specs=[
                pl.BlockSpec((per, tokens, HD), lambda i, c: (i, 0, 0)),
                pl.BlockSpec((n, tokens, HD), lambda i, c: (0, 1, 0)),
                pl.BlockSpec((n, tokens, HD), lambda i, c: (0, 2, 0)),
                pl.BlockSpec((per, IDROWS, HD), lambda i, c: (i, 3 * tokens // IDROWS, 0)),
                pl.BlockSpec((book.shape[0], HD), lambda i, c: (0, head)),
                pl.BlockSpec((slots, HD), lambda i, c: (0, head)),
                pl.BlockSpec((slots, HD), lambda i, c: (0, 2 + head)),
            ],
            out_specs=pl.BlockSpec((per, tokens, HD), lambda i, c: (i, 0, 0)),
        ),
        out_shape=jax.ShapeDtypeStruct((n, tokens, HD), jnp.bfloat16),
        cost_estimate=pl.CostEstimate(flops=pairs * HD * 4, bytes_accessed=2 << 20, transcendentals=pairs),
        name="attend",
    )(count, block, block, block, id_block, book, ref_kv, ref_kv)


def unpack_kernel(first_ref, second_ref, o_ref):
    for d in range(first_ref.shape[0]):
        col = d * 2 * HD
        o_ref[:, col : col + HD] = first_ref[d]
        o_ref[:, col + HD : col + 2 * HD] = second_ref[d]


def unpack(first, second):
    n, tokens, _ = first.shape
    group = 4
    spec = pl.BlockSpec((group, tokens, HD), lambda i: (i, 0, 0))
    return pl.pallas_call(
        unpack_kernel,
        grid=(n // group,),
        out_shape=jax.ShapeDtypeStruct((tokens, n * 2 * HD), jnp.bfloat16),
        in_specs=[spec, spec],
        out_specs=pl.BlockSpec((tokens, group * 2 * HD), lambda i: (0, i)),
        cost_estimate=pl.CostEstimate(flops=0, bytes_accessed=2 << 20, transcendentals=0),
        name="unpack",
    )(first, second)


def exchange(x):
    return lax.all_to_all(x, "seq", 0, 0, tiled=True)


def ring(block, pairs):
    parts = [block]
    for _ in range(3):
        parts.append(lax.ppermute(parts[-1], "fsdp", pairs))
    return jnp.concatenate(parts, axis=0)


def shards(video_qkv, reference_rows, kv_weight, pose_table, pose_ids, frame_counts):
    tokens = video_qkv.shape[1]
    video = jnp.transpose(video_qkv[0], (1, 0, 2))
    depth = kv_weight.shape[0]
    first, second = pack(video, reference_rows[0], pose_ids)
    first = exchange(first)
    codes = jnp.pad(pose_table, ((0, WROWS - depth - pose_table.shape[0]), (0, kv_weight.shape[2])))
    packed = jnp.concatenate([kv_weight.reshape(depth, -1), codes], axis=0)
    own = ring(ring(packed, Z_RING), X_RING)
    other = lax.ppermute(own, "fsdp", CORE_SWAP)
    second = exchange(second)
    n = first.shape[0]
    r = reference_rows.shape[1]
    rows = first[:, 3 * tokens + IDROWS :, :].reshape(n, -1, r, HD)
    rows = jnp.transpose(rows, (0, 2, 1, 3)).reshape(n * r, -1)
    ref_kv, book = ref_project(rows, own, other)
    out0 = attend(0, tokens, frame_counts, first, first, book, ref_kv)
    out1 = attend(1, tokens, frame_counts, second, first, book, ref_kv)
    return unpack(exchange(out0), exchange(out1))[None]


def solution(mesh):
    placed = (
        P("fsdp", "seq", None, None),
        P("fsdp", "seq", None),
        P("fsdp", None, "seq"),
        P("fsdp", "seq"),
        P("fsdp", "seq"),
        P("fsdp"),
    )
    return jax.shard_map(
        shards, mesh=mesh, in_specs=placed, out_specs=P("fsdp", "seq", None), check_vma=False
    )
```

time: 341 us -> 209 us (0.61)
  the two profiles are of different devices: /device:TPU:4 before, /device:TPU:8 now
where the time goes in v1:
time: 209 us; the launch traced here: 208 us
  waiting for transfers between devices  86 us (41%)
  starting transfers between devices  51.1 us (24%)
  Pallas kernels  42.5 us (20%)
  blocking collectives  20.8 us (10%)
  local copies, waits for them, and re-layouts  7.24 us (3%)
    ppermute x6, waiting for transfers between devices, ring(): parts.append(lax.ppermute(parts[-1], 'fsdp', pairs))  67.3 us
    all_to_all x3, starting transfers between devices, exchange(): return lax.all_to_all(x, 'seq', 0, 0, tiled=True)  28.5 us
    pallas_call x2, Pallas kernels, attend(): pl.pallas_call(lambda *refs: attend_kernel(tokens, *refs), grid_spec=pltp...  26.2 us
    all_to_all x1, blocking collectives, exchange(): return lax.all_to_all(x, 'seq', 0, 0, tiled=True)  20.8 us
    ppermute x6, starting transfers between devices, ring(): parts.append(lax.ppermute(parts[-1], 'fsdp', pairs))  20.7 us
    all_to_all x3, waiting for transfers between devices, exchange(): return lax.all_to_all(x, 'seq', 0, 0, tiled=True)  18.7 us
    pallas_call x1, Pallas kernels, pack(): pl.pallas_call(lambda *refs: pack_kernel(tokens, group, *refs), grid=(n /...  6.77 us
    pallas_call x1, Pallas kernels, ref_project(): pl.pallas_call(ref_kernel, out_shape=(jax.ShapeDtypeStruct((rows.shape[0]...  6.05 us
  transfers between devices with their start and end apart: 10, of which 8 were waited for; matrix products, arithmetic and copies ran while one was open for 3% of the time, Pallas kernels for 15%

profile of v1, /device:TPU:8, one launch (start us, length us, event | category | flops | bytes accessed | tf_op | source)
XLA Modules:
  0.0 208.4 jit_solution(16774640309666125142)
XLA Ops:
  0.0 6.8 %pack.1 = (bf16[16,560,128]{2,1,0:T(8,128)(2,1)}, bf16[16,384,128]{2,1,0:T(8,128)(2,1)}) custom-call(bf16[3,128,4096]{2,1,0:T(8,128)(2,1)} %bitcast.15, bf16[4,5120]{1,0:T(4,128)(2,1)} %bitcast.22, s32[1,128]{1,0:T(1,128)} %refs_2_.1), custom_call_target="tpu_custom_call" | custom-call | flops 1048576 | bytes 7340032 | tf_op jit(solution)/shard_map/pack/pallas_call | solution.py:62
  6.8 0.0 copy-start.2
  6.8 0.0 copy-start.3
  6.8 9.5 %all-to-all-start = ((bf16[16,560,128]{2,1,0:T(8,128)(2,1)}), bf16[16,560,128]{2,1,0:T(8,128)(2,1)S(1)}, u32[]{:S(2)}, u32[]{:S(2)}) async-start(bf16[16,560,128]{2,1,0:T(8,128)(2,1)} %get-tuple-element.9), calls=%async_computation | async-start | bytes 4587520 | tf_op jit(solution)/shard_map/all_to_all | solution.py:225
  16.3 0.0 copy-done.2
  16.3 0.7 constant_dynamic-update-slice_fusion.4
  17.0 0.0 copy-done.3
  17.0 0.6 constant_dynamic-update-slice_fusion.3
  17.6 6.1 %collective-permute-start = (bf16[176,512]{1,0:T(8,128)(2,1)S(1)}, bf16[176,512]{1,0:T(8,128)(2,1)S(1)}, u32[]{:S(2)}, u32[]{:S(2)}) collective-permute-start(bf16[176,512]{1,0:T(8,128)(2,1)S(1)} %pad_maximum_fusion), channel_id=1, source_target_pairs={{0,128},{16,400},{32,160},{48,432},{64,192},{80,464},{96,224},{112... | collective-permute-start | bytes 540680 | tf_op jit(solution)/shard_map/ppermute | solution.py:231
  23.7 12.5 %collective-permute-done = bf16[176,512]{1,0:T(8,128)(2,1)S(1)} collective-permute-done((bf16[176,512]{1,0:T(8,128)(2,1)S(1)}, bf16[176,512]{1,0:T(8,128)(2,1)S(1)}, u32[]{:S(2)}, u32[]{:S(2)}) %collective-permute-start) | collective-permute-done | bytes 180256 | tf_op jit(solution)/shard_map/ppermute | solution.py:231
  36.2 1.9 collective-permute-start.1
  38.1 17.8 %collective-permute-done.1 = bf16[176,512]{1,0:T(8,128)(2,1)S(1)} collective-permute-done((bf16[176,512]{1,0:T(8,128)(2,1)S(1)}, bf16[176,512]{1,0:T(8,128)(2,1)S(1)}, u32[]{:S(2)}, u32[]{:S(2)}) %collective-permute-start.1) | collective-permute-done | bytes 180256 | tf_op jit(solution)/shard_map/ppermute | solution.py:231
  55.9 5.3 %collective-permute-start.2 = (bf16[176,512]{1,0:T(8,128)(2,1)S(1)}, bf16[176,512]{1,0:T(8,128)(2,1)S(1)}, u32[]{:S(2)}, u32[]{:S(2)}) collective-permute-start(bf16[176,512]{1,0:T(8,128)(2,1)S(1)} %collective-permute-done.1), channel_id=1, source_target_pairs={{0,128},{16,400},{32,160},{48,432},{64,192},{80,464},{96,224},{112... | collective-permute-start | bytes 540680 | tf_op jit(solution)/shard_map/ppermute | solution.py:231
  61.2 0.7 constant_dynamic-update-slice_fusion.2
  61.9 0.7 constant_dynamic-update-slice_fusion.1
  62.6 3.1 %collective-permute-done.2 = bf16[176,512]{1,0:T(8,128)(2,1)S(1)} collective-permute-done((bf16[176,512]{1,0:T(8,128)(2,1)S(1)}, bf16[176,512]{1,0:T(8,128)(2,1)S(1)}, u32[]{:S(2)}, u32[]{:S(2)}) %collective-permute-start.2) | collective-permute-done | bytes 180256 | tf_op jit(solution)/shard_map/ppermute | solution.py:231
  65.7 0.7 constant_dynamic-update-slice_fusion
  66.4 3.4 %collective-permute-start.3 = (bf16[704,512]{1,0:T(8,128)(2,1)S(1)}, bf16[704,512]{1,0:T(8,128)(2,1)S(1)}, u32[]{:S(2)}, u32[]{:S(2)}) collective-permute-start(bf16[704,512]{1,0:T(8,128)(2,1)S(1)} %get-tuple-element.13), channel_id=1, source_target_pairs={{0,32},{16,112},{32,64},{48,16},{64,96},{80,48},{96,0},{112,80},{1... | collective-permute-start | bytes 2162696 | tf_op jit(solution)/shard_map/ppermute | solution.py:231
  69.8 11.0 %collective-permute-done.3 = bf16[704,512]{1,0:T(8,128)(2,1)S(1)} collective-permute-done((bf16[704,512]{1,0:T(8,128)(2,1)S(1)}, bf16[704,512]{1,0:T(8,128)(2,1)S(1)}, u32[]{:S(2)}, u32[]{:S(2)}) %collective-permute-start.3) | collective-permute-done | bytes 720928 | tf_op jit(solution)/shard_map/ppermute | solution.py:231
  80.8 2.1 %collective-permute-start.4 = (bf16[704,512]{1,0:T(8,128)(2,1)S(1)}, bf16[704,512]{1,0:T(8,128)(2,1)S(1)}, u32[]{:S(2)}, u32[]{:S(2)}) collective-permute-start(bf16[704,512]{1,0:T(8,128)(2,1)S(1)} %collective-permute-done.3), channel_id=1, source_target_pairs={{0,32},{16,112},{32,64},{48,16},{64,96},{80,48},{96,0},{112,80},{1... | collective-permute-start | bytes 2162696 | tf_op jit(solution)/shard_map/ppermute | solution.py:231
  83.0 12.2 %collective-permute-done.4 = bf16[704,512]{1,0:T(8,128)(2,1)S(1)} collective-permute-done((bf16[704,512]{1,0:T(8,128)(2,1)S(1)}, bf16[704,512]{1,0:T(8,128)(2,1)S(1)}, u32[]{:S(2)}, u32[]{:S(2)}) %collective-permute-start.4) | collective-permute-done | bytes 720928 | tf_op jit(solution)/shard_map/ppermute | solution.py:231
  95.2 1.9 collective-permute-start.5
  97.1 0.9 constant_dynamic-update-slice_fusion.7
  98.0 0.9 constant_dynamic-update-slice_fusion.6
  98.9 10.6 %collective-permute-done.5 = bf16[704,512]{1,0:T(8,128)(2,1)S(1)} collective-permute-done((bf16[704,512]{1,0:T(8,128)(2,1)S(1)}, bf16[704,512]{1,0:T(8,128)(2,1)S(1)}, u32[]{:S(2)}, u32[]{:S(2)}) %collective-permute-start.5) | collective-permute-done | bytes 720928 | tf_op jit(solution)/shard_map/ppermute | solution.py:231
  109.6 0.9 constant_dynamic-update-slice_fusion.5.own_ref
  110.5 1.9 collective-permute-start.6
  112.4 0.0 all-to-all-done.refs_1_.refs_2_.refs_3_.refs_4_
  112.4 0.0 copy-start
  112.4 11.9 %all-to-all-start.2 = ((bf16[16,384,128]{2,1,0:T(8,128)(2,1)}), bf16[16,384,128]{2,1,0:T(8,128)(2,1)}, u32[]{:S(2)}, u32[]{:S(2)}) async-start(bf16[16,384,128]{2,1,0:T(8,128)(2,1)} %get-tuple-element.12), calls=%async_computation.2 | async-start | bytes 3145728 | tf_op jit(solution)/shard_map/all_to_all | solution.py:225
  125.1 0.1 copy.7
  125.2 0.0 copy-done
  125.2 0.9 copy.11
  126.1 0.0 collective-permute-done.6.other_ref
  126.1 6.1 %ref_project.1 = (bf16[64,512]{1,0:T(8,128)(2,1)}, bf16[256,256]{1,0:T(8,128)(2,1)}) custom-call(bf16[64,5120]{1,0:T(8,128)(2,1)} %bitcast.16, bf16[2816,512]{1,0:T(8,128)(2,1)} %constant_dynamic-update-slice_fusion.5.own_ref, bf16[2816,512]{1,0:T(8,128)(2,1)} %collective-permute-done.6.other_ref), custom_call_target="tpu_custom_call" | custom-call | flops 536870912 | bytes 7340032 | tf_op jit(solution)/shard_map/ref_project/pallas_call | solution.py:123
  132.2 13.1 %attend.2 = bf16[16,128,128]{2,1,0:T(8,128)(2,1)} custom-call(s32[1]{0:T(128)S(6)} %copy.23.refs_0_, bf16[16,560,128]{2,1,0:T(8,128)(2,1)} %copy-done, bf16[16,560,128]{2,1,0:T(8,128)(2,1)} %copy-done, bf16[16,560,128]{2,1,0:T(8,128)(2,1)} %copy-done, bf16[16,560,128]{2,1,0:T(8,128)(2,1)} %copy-done, bf16[256,256]{1,0:T(8,128)(2,1)} %get-tuple-element.10.refs_5_, ...), custom_call_target="tpu_custom_call" | custom-call | flops 2214592512 | bytes 2097152 | tf_op jit(solution)/shard_map/attend/pallas_call | solution.py:180
  145.3 16.5 %all-to-all-done.2.refs_1_.refs_2_.refs_3_ = bf16[16,384,128]{2,1,0:T(8,128)(2,1)} async-done(((bf16[16,384,128]{2,1,0:T(8,128)(2,1)}), bf16[16,384,128]{2,1,0:T(8,128)(2,1)}, u32[]{:S(2)}, u32[]{:S(2)}) %all-to-all-start.2) | async-done | bytes 1572896 | tf_op jit(solution)/shard_map/all_to_all | solution.py:225
  161.8 7.0 %all-to-all-start.1 = ((bf16[16,128,128]{2,1,0:T(8,128)(2,1)}), bf16[16,128,128]{2,1,0:T(8,128)(2,1)S(1)}, u32[]{:S(2)}, u32[]{:S(2)}) async-start(bf16[16,128,128]{2,1,0:T(8,128)(2,1)} %attend.2), calls=%async_computation.1 | async-start | bytes 1048576 | tf_op jit(solution)/shard_map/all_to_all | solution.py:225
  168.9 13.1 %attend.3 = bf16[16,128,128]{2,1,0:T(8,128)(2,1)} custom-call(s32[1]{0:T(128)S(6)} %copy.23.refs_0_, bf16[16,384,128]{2,1,0:T(8,128)(2,1)} %all-to-all-done.2.refs_1_.refs_2_.refs_3_, bf16[16,384,128]{2,1,0:T(8,128)(2,1)} %all-to-all-done.2.refs_1_.refs_2_.refs_3_, bf16[16,384,128]{2,1,0:T(8,128)(2,1)} %all-to-all-done.2.refs_1_.refs_2_.refs_3_, ...), custom_call_target="tpu_custom_call" | custom-call | flops 2214592512 | bytes 2097152 | tf_op jit(solution)/shard_map/attend/pallas_call | solution.py:180
  181.9 2.2 %all-to-all-done.1.first_ref = bf16[16,128,128]{2,1,0:T(8,128)(2,1)S(1)} async-done(((bf16[16,128,128]{2,1,0:T(8,128)(2,1)}), bf16[16,128,128]{2,1,0:T(8,128)(2,1)S(1)}, u32[]{:S(2)}, u32[]{:S(2)}) %all-to-all-start.1) | async-done | bytes 524320 | tf_op jit(solution)/shard_map/all_to_all | solution.py:225
  184.1 0.0 copy-start.1
  184.1 20.8 %all_to_all.20.second_ref = bf16[16,128,128]{2,1,0:T(8,128)(2,1)} all-to-all(bf16[16,128,128]{2,1,0:T(8,128)(2,1)} %attend.3), channel_id=1, replica_groups=mesh['fsdp'=32,'seq'=16] {'seq'}, dimensions={0} | all-to-all | bytes 1048576 | tf_op jit(solution)/shard_map/all_to_all | solution.py:225
  204.9 0.0 copy-done.1
  204.9 3.5 %unpack.1 = bf16[128,4096]{1,0:T(8,128)(2,1)} custom-call(bf16[16,128,128]{2,1,0:T(8,128)(2,1)} %copy-done.1, bf16[16,128,128]{2,1,0:T(8,128)(2,1)} %all_to_all.20.second_ref), custom_call_target="tpu_custom_call" | custom-call | bytes 2097152 | tf_op jit(solution)/shard_map/unpack/pallas_call | solution.py:213
  (3 shorter events, 0.1 us)
Async XLA Ops:
  6.8 9.5 %copy-start.2 = (bf16[160,2,256]{2,1,0:T(2,128)(2,1)S(1)}, bf16[160,2,256]{2,1,0:T(2,128)(2,1)}, u32[]{:S(2)}) copy-start(bf16[160,2,256]{2,1,0:T(2,128)(2,1)} %param.8) | copy-start | bytes 491524
  6.8 10.2 %copy-start.3 = (bf16[8,256]{1,0:T(8,128)(2,1)S(1)}, bf16[8,256]{1,0:T(8,128)(2,1)}, u32[]{:S(2)}) copy-start(bf16[8,256]{1,0:T(8,128)(2,1)} %param.9) | copy-start | bytes 12292
  6.8 105.7 %all-to-all-start = ((bf16[16,560,128]{2,1,0:T(8,128)(2,1)}), bf16[16,560,128]{2,1,0:T(8,128)(2,1)S(1)}, u32[]{:S(2)}, u32[]{:S(2)}) async-start(bf16[16,560,128]{2,1,0:T(8,128)(2,1)} %get-tuple-element.9), calls=%async_computation | async-start | bytes 4587520 | tf_op jit(solution)/shard_map/all_to_all | solution.py:225
  17.6 18.6 %collective-permute-start = (bf16[176,512]{1,0:T(8,128)(2,1)S(1)}, bf16[176,512]{1,0:T(8,128)(2,1)S(1)}, u32[]{:S(2)}, u32[]{:S(2)}) collective-permute-start(bf16[176,512]{1,0:T(8,128)(2,1)S(1)} %pad_maximum_fusion), channel_id=1, source_target_pairs={{0,128},{16,400},{32,160},{48,432},{64,192},{80,464},{96,224},{112... | collective-permute-start | bytes 540680 | tf_op jit(solution)/shard_map/ppermute | solution.py:231
  36.2 19.7 %collective-permute-start.1 = (bf16[176,512]{1,0:T(8,128)(2,1)S(1)}, bf16[176,512]{1,0:T(8,128)(2,1)S(1)}, u32[]{:S(2)}, u32[]{:S(2)}) collective-permute-start(bf16[176,512]{1,0:T(8,128)(2,1)S(1)} %collective-permute-done), channel_id=1, source_target_pairs={{0,128},{16,400},{32,160},{48,432},{64,192},{80,464},{96,224},{112... | collective-permute-start | bytes 540680 | tf_op jit(solution)/shard_map/ppermute | solution.py:231
  55.9 9.9 %collective-permute-start.2 = (bf16[176,512]{1,0:T(8,128)(2,1)S(1)}, bf16[176,512]{1,0:T(8,128)(2,1)S(1)}, u32[]{:S(2)}, u32[]{:S(2)}) collective-permute-start(bf16[176,512]{1,0:T(8,128)(2,1)S(1)} %collective-permute-done.1), channel_id=1, source_target_pairs={{0,128},{16,400},{32,160},{48,432},{64,192},{80,464},{96,224},{112... | collective-permute-start | bytes 540680 | tf_op jit(solution)/shard_map/ppermute | solution.py:231
  66.4 14.4 %collective-permute-start.3 = (bf16[704,512]{1,0:T(8,128)(2,1)S(1)}, bf16[704,512]{1,0:T(8,128)(2,1)S(1)}, u32[]{:S(2)}, u32[]{:S(2)}) collective-permute-start(bf16[704,512]{1,0:T(8,128)(2,1)S(1)} %get-tuple-element.13), channel_id=1, source_target_pairs={{0,32},{16,112},{32,64},{48,16},{64,96},{80,48},{96,0},{112,80},{1... | collective-permute-start | bytes 2162696 | tf_op jit(solution)/shard_map/ppermute | solution.py:231
  80.8 14.4 %collective-permute-start.4 = (bf16[704,512]{1,0:T(8,128)(2,1)S(1)}, bf16[704,512]{1,0:T(8,128)(2,1)S(1)}, u32[]{:S(2)}, u32[]{:S(2)}) collective-permute-start(bf16[704,512]{1,0:T(8,128)(2,1)S(1)} %collective-permute-done.3), channel_id=1, source_target_pairs={{0,32},{16,112},{32,64},{48,16},{64,96},{80,48},{96,0},{112,80},{1... | collective-permute-start | bytes 2162696 | tf_op jit(solution)/shard_map/ppermute | solution.py:231
  95.2 14.4 %collective-permute-start.5 = (bf16[704,512]{1,0:T(8,128)(2,1)S(1)}, bf16[704,512]{1,0:T(8,128)(2,1)S(1)}, u32[]{:S(2)}, u32[]{:S(2)}) collective-permute-start(bf16[704,512]{1,0:T(8,128)(2,1)S(1)} %collective-permute-done.4), channel_id=1, source_target_pairs={{0,32},{16,112},{32,64},{48,16},{64,96},{80,48},{96,0},{112,80},{1... | collective-permute-start | bytes 2162696 | tf_op jit(solution)/shard_map/ppermute | solution.py:231
  110.5 15.6 %collective-permute-start.6 = (bf16[2816,512]{1,0:T(8,128)(2,1)}, bf16[2816,512]{1,0:T(8,128)(2,1)}, u32[]{:S(2)}, u32[]{:S(2)}) collective-permute-start(bf16[2816,512]{1,0:T(8,128)(2,1)} %constant_dynamic-update-slice_fusion.5.own_ref), channel_id=1, source_target_pairs={{0,16},{16,0},{32,48},{48,32},{64,80},{80,64},{96,112},{112,96},{1... | collective-permute-start | bytes 8650760 | tf_op jit(solution)/shard_map/ppermute | solution.py:244
  112.4 12.7 %copy-start = (bf16[16,560,128]{2,1,0:T(8,128)(2,1)}, bf16[16,560,128]{2,1,0:T(8,128)(2,1)S(1)}, u32[]{:S(2)}) copy-start(bf16[16,560,128]{2,1,0:T(8,128)(2,1)S(1)} %all-to-all-done.refs_1_.refs_2_.refs_3_.refs_4_) | copy-start | bytes 6881284
  112.4 49.4 %all-to-all-start.2 = ((bf16[16,384,128]{2,1,0:T(8,128)(2,1)}), bf16[16,384,128]{2,1,0:T(8,128)(2,1)}, u32[]{:S(2)}, u32[]{:S(2)}) async-start(bf16[16,384,128]{2,1,0:T(8,128)(2,1)} %get-tuple-element.12), calls=%async_computation.2 | async-start | bytes 3145728 | tf_op jit(solution)/shard_map/all_to_all | solution.py:225
  161.8 22.3 %all-to-all-start.1 = ((bf16[16,128,128]{2,1,0:T(8,128)(2,1)}), bf16[16,128,128]{2,1,0:T(8,128)(2,1)S(1)}, u32[]{:S(2)}, u32[]{:S(2)}) async-start(bf16[16,128,128]{2,1,0:T(8,128)(2,1)} %attend.2), calls=%async_computation.1 | async-start | bytes 1048576 | tf_op jit(solution)/shard_map/all_to_all | solution.py:225
  184.1 20.8 %copy-start.1 = (bf16[16,128,128]{2,1,0:T(8,128)(2,1)}, bf16[16,128,128]{2,1,0:T(8,128)(2,1)S(1)}, u32[]{:S(2)}) copy-start(bf16[16,128,128]{2,1,0:T(8,128)(2,1)S(1)} %all-to-all-done.1.first_ref) | copy-start | bytes 1572868

commit v2 on v1

v2 whole, which is shorter than its diff:
```python
import math

import jax
import jax.numpy as jnp
from jax import lax
from jax.experimental import pallas as pl
from jax.experimental.pallas import tpu as pltpu
from jax.sharding import PartitionSpec as P

HD = 128
TPF = 16
WROWS = 176
IDROWS = 16


def fsdp_perm(move):
    pairs = []
    for i in range(32):
        z, x, c = move(i // 8, i // 2 % 4, i % 2)
        pairs.append((i, z % 4 * 8 + x % 4 * 2 + c))
    return pairs


def direction(core):
    return 1 - 2 * core


Z_MOVES = [fsdp_perm(lambda z, x, c, k=k: (z + k * direction(c), x, c)) for k in (1, 2, 3)]
X_AHEAD = fsdp_perm(lambda z, x, c: (z, x + direction(c), c))
X_BEHIND = fsdp_perm(lambda z, x, c: (z, x - direction(c), c))
CORE_SWAP = fsdp_perm(lambda z, x, c: (z, x, 1 - c))
LAG = 6000


def pack_first_kernel(tokens, group, x_ref, rows_ref, ids_ref, o_ref, normed):
    @pl.when(pl.program_id(0) == 0)
    def _():
        x = rows_ref[...].astype(jnp.float32)
        mean = jnp.mean(x, axis=-1, keepdims=True)
        centered = x - mean
        var = jnp.mean(centered * centered, axis=-1, keepdims=True)
        out = centered * lax.rsqrt(var + 1e-06)
        r = x.shape[0]
        for c in range(x.shape[1] // HD):
            normed[c * r : (c + 1) * r, :] = out[:, c * HD : (c + 1) * HD]

    ids = jnp.broadcast_to(ids_ref[...].astype(jnp.float32), (IDROWS, tokens)).astype(jnp.bfloat16)
    norm = normed[...].astype(jnp.bfloat16)
    for d in range(group):
        for k in range(3):
            o_ref[d, k * tokens : (k + 1) * tokens, :] = x_ref[k, :, d * 2 * HD : d * 2 * HD + HD]
        o_ref[d, 3 * tokens : 3 * tokens + IDROWS, :] = ids
        o_ref[d, 3 * tokens + IDROWS :, :] = norm

    if LAG:
        @pl.when((pl.program_id(0) == 0) & (lax.axis_index("fsdp") % 2 == 1))
        def _():
            pl.delay(LAG)


def pack_second_kernel(tokens, group, x_ref, o_ref):
    for d in range(group):
        for k in range(3):
            o_ref[d, k * tokens : (k + 1) * tokens, :] = x_ref[k, :, d * 2 * HD + HD : (d + 1) * 2 * HD]


def pack_first(video, rows, ids):
    tokens, width = video.shape[1], video.shape[2]
    n = width // (2 * HD)
    nrows = rows.shape[0] * rows.shape[1] // HD
    group = 4
    long = 3 * tokens + IDROWS + nrows
    return pl.pallas_call(
        lambda *refs: pack_first_kernel(tokens, group, *refs),
        grid=(n // group,),
        out_shape=jax.ShapeDtypeStruct((n, long, HD), jnp.bfloat16),
        in_specs=[
            pl.BlockSpec((3, tokens, group * 2 * HD), lambda i: (0, 0, i)),
            pl.BlockSpec(rows.shape, lambda i: (0, 0)),
            pl.BlockSpec(ids.shape, lambda i: (0, 0)),
        ],
        out_specs=pl.BlockSpec((group, long, HD), lambda i: (i, 0, 0)),
        scratch_shapes=[pltpu.VMEM((nrows, HD), jnp.float32)],
        cost_estimate=pl.CostEstimate(flops=1 << 20, bytes_accessed=5 << 20, transcendentals=0),
        name="pack_first",
    )(video, rows, ids)


def pack_second(video):
    tokens, width = video.shape[1], video.shape[2]
    n = width // (2 * HD)
    group = 4
    return pl.pallas_call(
        lambda *refs: pack_second_kernel(tokens, group, *refs),
        grid=(n // group,),
        out_shape=jax.ShapeDtypeStruct((n, 3 * tokens, HD), jnp.bfloat16),
        in_specs=[pl.BlockSpec((3, tokens, group * 2 * HD), lambda i: (0, 0, i))],
        out_specs=pl.BlockSpec((group, 3 * tokens, HD), lambda i: (i, 0, 0)),
        cost_estimate=pl.CostEstimate(flops=0, bytes_accessed=5 << 20, transcendentals=0),
        name="pack_second",
    )(video)


def ref_kernel(x_ref, own_ref, other_ref, kv_ref, book_ref, weight, codes, sem):
    me = lax.axis_index("fsdp")
    mz, mx, mc = me // 8, me // 2 % 4, me % 2
    kdim = weight.shape[0] // 32
    copies = []
    for side, src in ((0, own_ref), (1, other_ref)):
        core = mc if side == 0 else 1 - mc
        sign = 1 - 2 * core
        for kx in range(4):
            for kz in range(4):
                z = (mz - sign * kz + 4) % 4
                x = (mx - sign * kx + 4) % 4
                f = z * 8 + x * 2 + core
                row = (kx * 4 + kz) * WROWS
                copies.append(
                    pltpu.make_async_copy(
                        src.at[pl.ds(row, kdim), :],
                        weight.at[pl.ds(pl.multiple_of(f * kdim, 16), kdim), :],
                        sem.at[len(copies)],
                    )
                )
                copies.append(
                    pltpu.make_async_copy(
                        src.at[pl.ds(row + kdim, 16), pl.ds(0, 2 * HD)],
                        codes.at[pl.ds(pl.multiple_of(f * 16, 16), 16), :],
                        sem.at[len(copies)],
                    )
                )
    for c in copies:
        c.start()
    for c in copies:
        c.wait()
    kv_ref[...] = jnp.dot(x_ref[...], weight[...], preferred_element_type=jnp.float32).astype(jnp.bfloat16)
    for f in range(32):
        book_ref[f * 8 : (f + 1) * 8, :] = codes[f * 16 : f * 16 + 8, :]


def ref_project(rows, own, other):
    n = own.shape[1]
    return pl.pallas_call(
        ref_kernel,
        out_shape=(
            jax.ShapeDtypeStruct((rows.shape[0], n), jnp.bfloat16),
            jax.ShapeDtypeStruct((256, 2 * HD), jnp.bfloat16),
        ),
        in_specs=[
            pl.BlockSpec(memory_space=pltpu.VMEM),
            pl.BlockSpec(memory_space=pl.ANY),
            pl.BlockSpec(memory_space=pl.ANY),
        ],
        out_specs=(pl.BlockSpec(memory_space=pltpu.VMEM), pl.BlockSpec(memory_space=pltpu.VMEM)),
        scratch_shapes=[
            pltpu.VMEM((rows.shape[1], n), jnp.bfloat16),
            pltpu.VMEM((512, 2 * HD), jnp.bfloat16),
            pltpu.SemaphoreType.DMA((64,)),
        ],
        cost_estimate=pl.CostEstimate(flops=1 << 10, bytes_accessed=1 << 10, transcendentals=0),
        compiler_params=pltpu.CompilerParams(vmem_limit_bytes=10 << 20),
        name="ref_project",
    )(rows, own, other)


def attend_kernel(tokens, sub, count_ref, q_ref, k_ref, v_ref, ids_ref, book_ref, rk_ref, rv_ref, o_ref):
    entries = book_ref.shape[0]
    keys = k_ref[...].reshape(-1, HD)
    values = v_ref[...].reshape(-1, HD)
    ref_values = rv_ref[...]
    values = jnp.concatenate([values, jnp.ones_like(values)], axis=1)
    ref_values = jnp.concatenate([ref_values, jnp.ones_like(ref_values)], axis=1)
    scale = math.log2(math.e) / math.sqrt(HD)
    nt = (((1,), (1,)), ((), ()))
    for b in range(q_ref.shape[0] // sub):
        parts = []
        for j in range(b * sub, (b + 1) * sub):
            ids = ids_ref[j, 0:1, :].astype(jnp.float32).astype(jnp.int32)
            entry = lax.broadcasted_iota(jnp.int32, (entries, tokens), 0)
            onehot = jnp.where(entry == ids, 1.0, 0.0).astype(jnp.bfloat16)
            lookup = lax.dot_general(
                onehot, book_ref[...], (((0,), (0,)), ((), ())), preferred_element_type=jnp.float32
            )
            parts.append((q_ref[j].astype(jnp.float32) + lookup).astype(jnp.bfloat16))
        q = jnp.concatenate(parts, axis=0)
        s1 = lax.dot_general(q, keys, nt, preferred_element_type=jnp.float32)
        s2 = lax.dot_general(q, rk_ref[...], nt, preferred_element_type=jnp.float32)
        live = lax.broadcasted_iota(jnp.int32, s2.shape, 1) < TPF * count_ref[0]
        s2 = jnp.where(live, s2, -1e30)
        top = jnp.maximum(jnp.max(s1, axis=-1, keepdims=True), jnp.max(s2, axis=-1, keepdims=True)) * scale
        p1 = jnp.exp2(s1 * scale - top).astype(jnp.bfloat16)
        p2 = jnp.where(live, jnp.exp2(s2 * scale - top), 0.0).astype(jnp.bfloat16)
        both = jnp.dot(p1, values, preferred_element_type=jnp.float32)
        both = both + jnp.dot(p2, ref_values, preferred_element_type=jnp.float32)
        out = both[:, :HD] / both[:, HD:]
        o_ref[b * sub : (b + 1) * sub] = out.astype(jnp.bfloat16).reshape(sub, tokens, HD)


def attend(head, tokens, count, block, id_block, book, ref_kv):
    n = block.shape[0]
    per, sub = 8, 4
    slots = ref_kv.shape[0]
    return pl.pallas_call(
        lambda *refs: attend_kernel(tokens, sub, *refs),
        grid_spec=pltpu.PrefetchScalarGridSpec(
            num_scalar_prefetch=1,
            grid=(n // per,),
            in_specs=[
                pl.BlockSpec((per, tokens, HD), lambda i, c: (i, 0, 0)),
                pl.BlockSpec((n, tokens, HD), lambda i, c: (0, 1, 0)),
                pl.BlockSpec((n, tokens, HD), lambda i, c: (0, 2, 0)),
                pl.BlockSpec((per, IDROWS, HD), lambda i, c: (i, 3 * tokens // IDROWS, 0)),
                pl.BlockSpec((book.shape[0], HD), lambda i, c: (0, head)),
                pl.BlockSpec((slots, HD), lambda i, c: (0, head)),
                pl.BlockSpec((slots, HD), lambda i, c: (0, 2 + head)),
            ],
            out_specs=pl.BlockSpec((per, tokens, HD), lambda i, c: (i, 0, 0)),
        ),
        out_shape=jax.ShapeDtypeStruct((n, tokens, HD), jnp.bfloat16),
        cost_estimate=pl.CostEstimate(flops=1 << 10, bytes_accessed=1 << 10, transcendentals=0),
        compiler_params=pltpu.CompilerParams(vmem_limit_bytes=24 << 20),
        name="attend",
    )(count, block, block, block, id_block, book, ref_kv, ref_kv)


def unpack_kernel(head, r_ref, *refs):
    o_ref, sem = refs[-2:]
    copies = []
    for d in range(r_ref.shape[0]):
        col = d * 2 * HD + head * HD
        copies.append(pltpu.make_async_copy(r_ref.at[d], o_ref.at[:, pl.ds(col, HD)], sem.at[d]))
    for c in copies:
        c.start()
    for c in copies:
        c.wait()


def unpack(head, received, partial=None):
    n, tokens, _ = received.shape
    operands = (received,) if partial is None else (received, partial)
    specs = [pl.BlockSpec(memory_space=pl.ANY)] * len(operands)
    return pl.pallas_call(
        lambda *refs: unpack_kernel(head, *refs),
        out_shape=jax.ShapeDtypeStruct((tokens, n * 2 * HD), jnp.bfloat16),
        in_specs=specs,
        out_specs=pl.BlockSpec(memory_space=pl.ANY),
        input_output_aliases={} if partial is None else {1: 0},
        scratch_shapes=[pltpu.SemaphoreType.DMA((n,))],
        cost_estimate=pl.CostEstimate(flops=0, bytes_accessed=2 << 20, transcendentals=0),
        compiler_params=pltpu.CompilerParams(vmem_limit_bytes=1 << 20),
        name="unpack",
    )(*operands)


def exchange(x):
    return lax.all_to_all(x, "seq", 0, 0, tiled=True)


def move(block, pairs):
    return lax.ppermute(block, "fsdp", pairs)


def shards(video_qkv, reference_rows, kv_weight, pose_table, pose_ids, frame_counts):
    tokens = video_qkv.shape[1]
    video = jnp.transpose(video_qkv[0], (1, 0, 2))
    depth = kv_weight.shape[0]
    first = exchange(pack_first(video, reference_rows[0], pose_ids))
    second = pack_second(video)
    codes = jnp.pad(pose_table, ((0, WROWS - depth - pose_table.shape[0]), (0, kv_weight.shape[2])))
    packed = jnp.concatenate([kv_weight.reshape(depth, -1), codes], axis=0)
    column = jnp.concatenate([packed] + [move(packed, pairs) for pairs in Z_MOVES], axis=0)
    column, second = lax.optimization_barrier((column, second))
    ahead = move(column, X_AHEAD)
    behind = move(column, X_BEHIND)
    first, ahead = lax.optimization_barrier((first, ahead))
    far = move(ahead, X_AHEAD)
    own = jnp.concatenate([column, ahead, far, behind], axis=0)
    other = move(own, CORE_SWAP)
    second = exchange(second)
    n = first.shape[0]
    r = reference_rows.shape[1]
    rows = first[:, 3 * tokens + IDROWS :, :].reshape(n, -1, r, HD)
    rows = jnp.transpose(rows, (0, 2, 1, 3)).reshape(n * r, -1)
    ref_kv, book = ref_project(rows, own, other)
    out0 = attend(0, tokens, frame_counts, first, first, book, ref_kv)
    out1 = attend(1, tokens, frame_counts, second, first, book, ref_kv)
    result = unpack(0, exchange(out0))
    return unpack(1, exchange(out1), result)[None]


def solution(mesh):
    placed = (
        P("fsdp", "seq", None, None),
        P("fsdp", "seq", None),
        P("fsdp", None, "seq"),
        P("fsdp", "seq"),
        P("fsdp", "seq"),
        P("fsdp"),
    )
    return jax.shard_map(
        shards, mesh=mesh, in_specs=placed, out_specs=P("fsdp", "seq", None), check_vma=False
    )
```

time: 209 us -> 171 us (0.82)
  the two profiles are of different devices: /device:TPU:8 before, /device:TPU:14 now
where the time goes in v2:
time: 171 us
  starting transfers between devices  77 us (45%)
  waiting for transfers between devices  47.6 us (28%)
  Pallas kernels  40.1 us (23%)
  local copies, waits for them, and re-layouts  4.75 us (3%)
    all_to_all x4, starting transfers between devices, exchange(): return lax.all_to_all(x, 'seq', 0, 0, tiled=True)  43.7 us
    ppermute x7, starting transfers between devices, move(): return lax.ppermute(block, 'fsdp', pairs)  33.3 us
    ppermute x7, waiting for transfers between devices, move(): return lax.ppermute(block, 'fsdp', pairs)  27.1 us
    all_to_all x4, waiting for transfers between devices, exchange(): return lax.all_to_all(x, 'seq', 0, 0, tiled=True)  20.5 us
    pallas_call x2, Pallas kernels, attend(): pl.pallas_call(lambda *refs: attend_kernel(tokens, sub, *refs), grid_spec...  20.4 us
    pallas_call x1, Pallas kernels, ref_project(): pl.pallas_call(ref_kernel, out_shape=(jax.ShapeDtypeStruct((rows.shape[0]...  9.47 us
    pallas_call x1, Pallas kernels, pack_first(): pl.pallas_call(lambda *refs: pack_first_kernel(tokens, group, *refs), gri...  4.38 us
    pallas_call x1, Pallas kernels, pack_second(): pl.pallas_call(lambda *refs: pack_second_kernel(tokens, group, *refs), gr...  4 us
  transfers between devices with their start and end apart: 11, of which 6 were waited for; matrix products, arithmetic and copies ran while one was open for 3% of the time, Pallas kernels for 20%

profile of v2, /device:TPU:14, one launch (start us, length us, event | category | flops | bytes accessed | tf_op | source)
XLA Modules:
  0.0 170.5 jit_solution(15646345373726619079)
XLA Ops:
  0.0 4.4 %pack_first.1 = bf16[16,560,128]{2,1,0:T(8,128)(2,1)} custom-call(bf16[3,128,4096]{2,1,0:T(8,128)(2,1)} %bitcast.16, bf16[4,5120]{1,0:T(4,128)(2,1)} %bitcast.23, s32[1,128]{1,0:T(1,128)} %refs_2_.1), custom_call_target="tpu_custom_call" | custom-call | flops 1048576 | bytes 5242880 | tf_op jit(solution)/shard_map/pack_first/pallas_call | solution.py:73
  4.4 0.0 copy-start
  4.4 0.0 copy-start.1
  4.4 9.5 %all-to-all-start.1 = ((bf16[16,560,128]{2,1,0:T(8,128)(2,1)}), bf16[16,560,128]{2,1,0:T(8,128)(2,1)S(1)}, u32[]{:S(2)}, u32[]{:S(2)}) async-start(bf16[16,560,128]{2,1,0:T(8,128)(2,1)} %pack_first.1), calls=%async_computation.1 | async-start | bytes 4587520 | tf_op jit(solution)/shard_map/all_to_all | solution.py:256
  13.9 0.0 copy-done
  13.9 0.0 copy-done.1
  14.0 6.1 %collective-permute-start = (bf16[176,512]{1,0:T(8,128)(2,1)S(1)}, bf16[176,512]{1,0:T(8,128)(2,1)}, u32[]{:S(2)}, u32[]{:S(2)}) collective-permute-start(bf16[176,512]{1,0:T(8,128)(2,1)S(1)} %pad_maximum_fusion), channel_id=1, source_target_pairs={{0,128},{16,400},{32,160},{48,432},{64,192},{80,464},{96,224},{112... | collective-permute-start | bytes 540680 | tf_op jit(solution)/shard_map/ppermute | solution.py:260
  20.1 8.2 %collective-permute-start.1 = (bf16[176,512]{1,0:T(8,128)(2,1)S(1)}, bf16[176,512]{1,0:T(8,128)(2,1)S(1)}, u32[]{:S(2)}, u32[]{:S(2)}) collective-permute-start(bf16[176,512]{1,0:T(8,128)(2,1)S(1)} %pad_maximum_fusion), channel_id=1, source_target_pairs={{0,256},{16,272},{32,288},{48,304},{64,320},{80,336},{96,352},{112... | collective-permute-start | bytes 540680 | tf_op jit(solution)/shard_map/ppermute | solution.py:260
  28.3 3.7 %collective-permute-start.2 = (bf16[176,512]{1,0:T(8,128)(2,1)S(1)}, bf16[176,512]{1,0:T(8,128)(2,1)S(1)}, u32[]{:S(2)}, u32[]{:S(2)}) collective-permute-start(bf16[176,512]{1,0:T(8,128)(2,1)S(1)} %pad_maximum_fusion), channel_id=1, source_target_pairs={{0,384},{16,144},{32,416},{48,176},{64,448},{80,208},{96,480},{112... | collective-permute-start | bytes 540680 | tf_op jit(solution)/shard_map/ppermute | solution.py:260
  32.0 4.0 %pack_second.1 = bf16[16,384,128]{2,1,0:T(8,128)(2,1)} custom-call(bf16[3,128,4096]{2,1,0:T(8,128)(2,1)} %bitcast.17), custom_call_target="tpu_custom_call" | custom-call | bytes 5242880 | tf_op jit(solution)/shard_map/pack_second/pallas_call | solution.py:93
  36.0 0.0 collective-permute-done
  36.0 0.9 constant_dynamic-update-slice_fusion.2
  36.9 12.2 %collective-permute-done.1 = bf16[176,512]{1,0:T(8,128)(2,1)S(1)} collective-permute-done((bf16[176,512]{1,0:T(8,128)(2,1)S(1)}, bf16[176,512]{1,0:T(8,128)(2,1)S(1)}, u32[]{:S(2)}, u32[]{:S(2)}) %collective-permute-start.1) | collective-permute-done | bytes 180256 | tf_op jit(solution)/shard_map/ppermute | solution.py:260
  49.2 0.0 collective-permute-done.2
  49.2 2.4 %collective-permute-start.3 = (bf16[704,512]{1,0:T(8,128)(2,1)S(1)}, bf16[704,512]{1,0:T(8,128)(2,1)}, u32[]{:S(2)}, u32[]{:S(2)}) collective-permute-start(bf16[704,512]{1,0:T(8,128)(2,1)S(1)} %constant_dynamic-update-slice_fusion), channel_id=1, source_target_pairs={{0,32},{16,112},{32,64},{48,16},{64,96},{80,48},{96,0},{112,80},{1... | collective-permute-start | bytes 2162696 | tf_op jit(solution)/shard_map/ppermute | solution.py:260
  51.6 10.9 %collective-permute-done.3 = bf16[704,512]{1,0:T(8,128)(2,1)} collective-permute-done((bf16[704,512]{1,0:T(8,128)(2,1)S(1)}, bf16[704,512]{1,0:T(8,128)(2,1)}, u32[]{:S(2)}, u32[]{:S(2)}) %collective-permute-start.3) | collective-permute-done | bytes 720928 | tf_op jit(solution)/shard_map/ppermute | solution.py:260
  62.5 1.1 all-to-all-done.1.refs_4_.refs_1_.refs_2_.refs_3_
  63.6 2.5 %collective-permute-start.4 = (bf16[704,512]{1,0:T(8,128)(2,1)}, bf16[704,512]{1,0:T(8,128)(2,1)}, u32[]{:S(2)}, u32[]{:S(2)}) collective-permute-start(bf16[704,512]{1,0:T(8,128)(2,1)} %collective-permute-done.3), channel_id=1, source_target_pairs={{0,32},{16,112},{32,64},{48,16},{64,96},{80,48},{96,0},{112,80},{1... | collective-permute-start | bytes 2162696 | tf_op jit(solution)/shard_map/ppermute | solution.py:260
  66.1 3.3 %collective-permute-start.5 = (bf16[704,512]{1,0:T(8,128)(2,1)S(1)}, bf16[704,512]{1,0:T(8,128)(2,1)}, u32[]{:S(2)}, u32[]{:S(2)}) collective-permute-start(bf16[704,512]{1,0:T(8,128)(2,1)S(1)} %constant_dynamic-update-slice_fusion), channel_id=1, source_target_pairs={{0,96},{16,48},{32,0},{48,80},{64,32},{80,112},{96,64},{112,16},{1... | collective-permute-start | bytes 2162696 | tf_op jit(solution)/shard_map/ppermute | solution.py:260
  69.4 15.7 %all-to-all-start = ((bf16[16,384,128]{2,1,0:T(8,128)(2,1)}), bf16[16,384,128]{2,1,0:T(8,128)(2,1)}, u32[]{:S(2)}, u32[]{:S(2)}) async-start(bf16[16,384,128]{2,1,0:T(8,128)(2,1)} %pack_second.1), calls=%async_computation | async-start | bytes 3145728 | tf_op jit(solution)/shard_map/all_to_all | solution.py:256
  85.1 1.2 constant_dynamic-update-slice_fusion.7
  86.3 0.0 collective-permute-done.4
  86.3 1.2 constant_dynamic-update-slice_fusion.6
  87.5 0.0 collective-permute-done.5
  87.5 1.2 constant_dynamic-update-slice_fusion.5.own_ref
  88.6 7.1 %collective-permute-start.6 = (bf16[2816,512]{1,0:T(8,128)(2,1)S(1)}, bf16[2816,512]{1,0:T(8,128)(2,1)S(1)}, u32[]{:S(2)}, u32[]{:S(2)}) collective-permute-start(bf16[2816,512]{1,0:T(8,128)(2,1)S(1)} %constant_dynamic-update-slice_fusion.5.own_ref), channel_id=1, source_target_pairs={{0,16},{16,0},{32,48},{48,32},{64,80},{80,64},{96,112},{112,96},{1... | collective-permute-start | bytes 8650760 | tf_op jit(solution)/shard_map/ppermute | solution.py:260
  96.4 0.1 copy.8
  96.5 0.1 copy.12
  96.6 4.0 %collective-permute-done.6.other_ref = bf16[2816,512]{1,0:T(8,128)(2,1)S(1)} collective-permute-done((bf16[2816,512]{1,0:T(8,128)(2,1)S(1)}, bf16[2816,512]{1,0:T(8,128)(2,1)S(1)}, u32[]{:S(2)}, u32[]{:S(2)}) %collective-permute-start.6) | collective-permute-done | bytes 2883616 | tf_op jit(solution)/shard_map/ppermute | solution.py:260
  100.6 9.5 %ref_project.1 = (bf16[64,512]{1,0:T(8,128)(2,1)S(1)}, bf16[256,256]{1,0:T(8,128)(2,1)S(1)}) custom-call(bf16[64,5120]{1,0:T(8,128)(2,1)S(1)} %bitcast.15, bf16[2816,512]{1,0:T(8,128)(2,1)S(1)} %constant_dynamic-update-slice_fusion.5.own_ref, bf16[2816,512]{1,0:T(8,128)(2,1)S(1)} %collective-permute-done.6.other_ref), custom_call_target="tpu_custom_call" | custom-call | flops 1024 | bytes 1024 | tf_op jit(solution)/shard_map/ref_project/pallas_call | solution.py:143
  110.1 9.6 %attend.3 = bf16[16,128,128]{2,1,0:T(8,128)(2,1)} custom-call(s32[1]{0:T(128)S(6)} %copy.21.refs_0_, bf16[16,560,128]{2,1,0:T(8,128)(2,1)S(1)} %all-to-all-done.1.refs_4_.refs_1_.refs_2_.refs_3_, bf16[16,560,128]{2,1,0:T(8,128)(2,1)S(1)} %all-to-all-done.1.refs_4_.refs_1_.refs_2_.refs_3_, ...), custom_call_target="tpu_custom_call" | custom-call | flops 1024 | bytes 1024 | tf_op jit(solution)/shard_map/attend/pallas_call | solution.py:203
  119.7 0.0 all-to-all-done.refs_1_.refs_2_.refs_3_
  119.7 13.7 %all-to-all-start.3 = ((bf16[16,128,128]{2,1,0:T(8,128)(2,1)}), bf16[16,128,128]{2,1,0:T(8,128)(2,1)S(1)}, u32[]{:S(2)}, u32[]{:S(2)}) async-start(bf16[16,128,128]{2,1,0:T(8,128)(2,1)} %attend.3), calls=%async_computation.3 | async-start | bytes 1048576 | tf_op jit(solution)/shard_map/all_to_all | solution.py:256
  133.4 10.8 %attend.2 = bf16[16,128,128]{2,1,0:T(8,128)(2,1)} custom-call(s32[1]{0:T(128)S(6)} %copy.21.refs_0_, bf16[16,384,128]{2,1,0:T(8,128)(2,1)} %all-to-all-done.refs_1_.refs_2_.refs_3_, bf16[16,384,128]{2,1,0:T(8,128)(2,1)} %all-to-all-done.refs_1_.refs_2_.refs_3_, bf16[16,384,128]{2,1,0:T(8,128)(2,1)} %all-to-all-done.refs_1_.refs_2_.refs_3_, ...), custom_call_target="tpu_custom_call" | custom-call | flops 1024 | bytes 1024 | tf_op jit(solution)/shard_map/attend/pallas_call | solution.py:203
  144.2 5.1 %all-to-all-done.3.refs_0_ = bf16[16,128,128]{2,1,0:T(8,128)(2,1)S(1)} async-done(((bf16[16,128,128]{2,1,0:T(8,128)(2,1)}), bf16[16,128,128]{2,1,0:T(8,128)(2,1)S(1)}, u32[]{:S(2)}, u32[]{:S(2)}) %all-to-all-start.3) | async-done | bytes 524320 | tf_op jit(solution)/shard_map/all_to_all | solution.py:256
  149.3 4.9 %all-to-all-start.2 = ((bf16[16,128,128]{2,1,0:T(8,128)(2,1)}), bf16[16,128,128]{2,1,0:T(8,128)(2,1)S(1)}, u32[]{:S(2)}, u32[]{:S(2)}) async-start(bf16[16,128,128]{2,1,0:T(8,128)(2,1)} %attend.2), calls=%async_computation.2 | async-start | bytes 1048576 | tf_op jit(solution)/shard_map/all_to_all | solution.py:256
  154.2 0.9 unpack.2.refs_1_
  155.1 14.3 %all-to-all-done.2.refs_0_ = bf16[16,128,128]{2,1,0:T(8,128)(2,1)S(1)} async-done(((bf16[16,128,128]{2,1,0:T(8,128)(2,1)}), bf16[16,128,128]{2,1,0:T(8,128)(2,1)S(1)}, u32[]{:S(2)}, u32[]{:S(2)}) %all-to-all-start.2) | async-done | bytes 524320 | tf_op jit(solution)/shard_map/all_to_all | solution.py:256
  169.5 0.9 unpack.3
  (8 shorter events, 0.2 us)
Async XLA Ops:
  4.4 9.5 %copy-start = (bf16[160,2,256]{2,1,0:T(2,128)(2,1)S(1)}, bf16[160,2,256]{2,1,0:T(2,128)(2,1)}, u32[]{:S(2)}) copy-start(bf16[160,2,256]{2,1,0:T(2,128)(2,1)} %param.8) | copy-start | bytes 491524
  4.4 9.6 %copy-start.1 = (bf16[8,256]{1,0:T(8,128)(2,1)S(1)}, bf16[8,256]{1,0:T(8,128)(2,1)}, u32[]{:S(2)}) copy-start(bf16[8,256]{1,0:T(8,128)(2,1)} %param.9) | copy-start | bytes 12292
  4.4 59.2 %all-to-all-start.1 = ((bf16[16,560,128]{2,1,0:T(8,128)(2,1)}), bf16[16,560,128]{2,1,0:T(8,128)(2,1)S(1)}, u32[]{:S(2)}, u32[]{:S(2)}) async-start(bf16[16,560,128]{2,1,0:T(8,128)(2,1)} %pack_first.1), calls=%async_computation.1 | async-start | bytes 4587520 | tf_op jit(solution)/shard_map/all_to_all | solution.py:256
  14.0 22.0 %collective-permute-start = (bf16[176,512]{1,0:T(8,128)(2,1)S(1)}, bf16[176,512]{1,0:T(8,128)(2,1)}, u32[]{:S(2)}, u32[]{:S(2)}) collective-permute-start(bf16[176,512]{1,0:T(8,128)(2,1)S(1)} %pad_maximum_fusion), channel_id=1, source_target_pairs={{0,128},{16,400},{32,160},{48,432},{64,192},{80,464},{96,224},{112... | collective-permute-start | bytes 540680 | tf_op jit(solution)/shard_map/ppermute | solution.py:260
  20.1 29.0 %collective-permute-start.1 = (bf16[176,512]{1,0:T(8,128)(2,1)S(1)}, bf16[176,512]{1,0:T(8,128)(2,1)S(1)}, u32[]{:S(2)}, u32[]{:S(2)}) collective-permute-start(bf16[176,512]{1,0:T(8,128)(2,1)S(1)} %pad_maximum_fusion), channel_id=1, source_target_pairs={{0,256},{16,272},{32,288},{48,304},{64,320},{80,336},{96,352},{112... | collective-permute-start | bytes 540680 | tf_op jit(solution)/shard_map/ppermute | solution.py:260
  28.3 20.8 %collective-permute-start.2 = (bf16[176,512]{1,0:T(8,128)(2,1)S(1)}, bf16[176,512]{1,0:T(8,128)(2,1)S(1)}, u32[]{:S(2)}, u32[]{:S(2)}) collective-permute-start(bf16[176,512]{1,0:T(8,128)(2,1)S(1)} %pad_maximum_fusion), channel_id=1, source_target_pairs={{0,384},{16,144},{32,416},{48,176},{64,448},{80,208},{96,480},{112... | collective-permute-start | bytes 540680 | tf_op jit(solution)/shard_map/ppermute | solution.py:260
  49.2 13.3 %collective-permute-start.3 = (bf16[704,512]{1,0:T(8,128)(2,1)S(1)}, bf16[704,512]{1,0:T(8,128)(2,1)}, u32[]{:S(2)}, u32[]{:S(2)}) collective-permute-start(bf16[704,512]{1,0:T(8,128)(2,1)S(1)} %constant_dynamic-update-slice_fusion), channel_id=1, source_target_pairs={{0,32},{16,112},{32,64},{48,16},{64,96},{80,48},{96,0},{112,80},{1... | collective-permute-start | bytes 2162696 | tf_op jit(solution)/shard_map/ppermute | solution.py:260
  63.6 22.7 %collective-permute-start.4 = (bf16[704,512]{1,0:T(8,128)(2,1)}, bf16[704,512]{1,0:T(8,128)(2,1)}, u32[]{:S(2)}, u32[]{:S(2)}) collective-permute-start(bf16[704,512]{1,0:T(8,128)(2,1)} %collective-permute-done.3), channel_id=1, source_target_pairs={{0,32},{16,112},{32,64},{48,16},{64,96},{80,48},{96,0},{112,80},{1... | collective-permute-start | bytes 2162696 | tf_op jit(solution)/shard_map/ppermute | solution.py:260
  66.1 21.4 %collective-permute-start.5 = (bf16[704,512]{1,0:T(8,128)(2,1)S(1)}, bf16[704,512]{1,0:T(8,128)(2,1)}, u32[]{:S(2)}, u32[]{:S(2)}) collective-permute-start(bf16[704,512]{1,0:T(8,128)(2,1)S(1)} %constant_dynamic-update-slice_fusion), channel_id=1, source_target_pairs={{0,96},{16,48},{32,0},{48,80},{64,32},{80,112},{96,64},{112,16},{1... | collective-permute-start | bytes 2162696 | tf_op jit(solution)/shard_map/ppermute | solution.py:260
  69.4 50.3 %all-to-all-start = ((bf16[16,384,128]{2,1,0:T(8,128)(2,1)}), bf16[16,384,128]{2,1,0:T(8,128)(2,1)}, u32[]{:S(2)}, u32[]{:S(2)}) async-start(bf16[16,384,128]{2,1,0:T(8,128)(2,1)} %pack_second.1), calls=%async_computation | async-start | bytes 3145728 | tf_op jit(solution)/shard_map/all_to_all | solution.py:256
  88.6 12.0 %collective-permute-start.6 = (bf16[2816,512]{1,0:T(8,128)(2,1)S(1)}, bf16[2816,512]{1,0:T(8,128)(2,1)S(1)}, u32[]{:S(2)}, u32[]{:S(2)}) collective-permute-start(bf16[2816,512]{1,0:T(8,128)(2,1)S(1)} %constant_dynamic-update-slice_fusion.5.own_ref), channel_id=1, source_target_pairs={{0,16},{16,0},{32,48},{48,32},{64,80},{80,64},{96,112},{112,96},{1... | collective-permute-start | bytes 8650760 | tf_op jit(solution)/shard_map/ppermute | solution.py:260
  119.7 29.5 %all-to-all-start.3 = ((bf16[16,128,128]{2,1,0:T(8,128)(2,1)}), bf16[16,128,128]{2,1,0:T(8,128)(2,1)S(1)}, u32[]{:S(2)}, u32[]{:S(2)}) async-start(bf16[16,128,128]{2,1,0:T(8,128)(2,1)} %attend.3), calls=%async_computation.3 | async-start | bytes 1048576 | tf_op jit(solution)/shard_map/all_to_all | solution.py:256
  149.3 20.2 %all-to-all-start.2 = ((bf16[16,128,128]{2,1,0:T(8,128)(2,1)}), bf16[16,128,128]{2,1,0:T(8,128)(2,1)S(1)}, u32[]{:S(2)}, u32[]{:S(2)}) async-start(bf16[16,128,128]{2,1,0:T(8,128)(2,1)} %attend.2), calls=%async_computation.2 | async-start | bytes 1048576 | tf_op jit(solution)/shard_map/all_to_all | solution.py:256

commit v3 on v0

v3 whole, which is shorter than its diff:
```python
import math

import jax
import jax.numpy as jnp
from jax import lax
from jax.experimental import pallas as pl
from jax.experimental.pallas import tpu as pltpu
from jax.sharding import PartitionSpec as P

HD = 128
TPF = 16
WROWS = 176
IDROWS = 16


def fsdp_perm(move):
    pairs = []
    for i in range(32):
        z, x, c = move(i // 8, i // 2 % 4, i % 2)
        pairs.append((i, z % 4 * 8 + x % 4 * 2 + c))
    return pairs


def direction(core):
    return 1 - 2 * core


Z_MOVES = [fsdp_perm(lambda z, x, c, k=k: (z + k * direction(c), x, c)) for k in (1, 2, 3)]
X_AHEAD = fsdp_perm(lambda z, x, c: (z, x + direction(c), c))
X_BEHIND = fsdp_perm(lambda z, x, c: (z, x - direction(c), c))
CORE_SWAP = fsdp_perm(lambda z, x, c: (z, x, 1 - c))
def pack_kernel(tokens, x_ref, ids_ref, o_ref, held, ids, in_sem, out_sem):
    planes, _, width = held.shape
    n = o_ref.shape[0]
    loads = [pltpu.make_async_copy(x_ref.at[k], held.at[k], in_sem.at[k]) for k in range(planes)]
    for load in loads:
        load.start()
    ids[...] = jnp.broadcast_to(ids_ref[...].astype(jnp.float32), (2 * IDROWS, tokens))[0:IDROWS].astype(jnp.bfloat16)
    stores = []
    for d in range(n):
        rows = o_ref.at[d, pl.ds(planes * tokens, IDROWS), pl.ds(0, tokens)]
        stores.append(pltpu.make_async_copy(ids, rows, out_sem.at[len(stores)]))
    for k in range(planes):
        loads[k].wait()
        for d in range(n):
            part = held.at[k, :, pl.ds(d * 2 * HD, 2 * HD)]
            rows = o_ref.at[d, pl.ds(k * tokens, tokens), :]
            copy = pltpu.make_async_copy(part, rows, out_sem.at[len(stores)])
            copy.start()
            stores.append(copy)
    for copy in stores[:n]:
        copy.start()
    for copy in stores:
        copy.wait()


def pack(video, ids):
    planes, tokens, width = video.shape
    n = width // (2 * HD)
    long = planes * tokens + IDROWS
    return pl.pallas_call(
        lambda *refs: pack_kernel(tokens, *refs),
        out_shape=jax.ShapeDtypeStruct((n, long, 2 * HD), jnp.bfloat16),
        in_specs=[pl.BlockSpec(memory_space=pl.ANY), pl.BlockSpec(memory_space=pltpu.VMEM)],
        out_specs=pl.BlockSpec(memory_space=pl.ANY),
        scratch_shapes=[
            pltpu.VMEM(video.shape, jnp.bfloat16),
            pltpu.VMEM((IDROWS, tokens), jnp.bfloat16),
            pltpu.SemaphoreType.DMA((planes,)),
            pltpu.SemaphoreType.DMA(((planes + 1) * n,)),
        ],
        cost_estimate=pl.CostEstimate(flops=0, bytes_accessed=6 << 20, transcendentals=0),
        name="pack",
    )(video, ids)


def norm_kernel(x_ref, o_ref):
    x = x_ref[...].astype(jnp.float32)
    mean = jnp.mean(x, axis=-1, keepdims=True)
    centered = x - mean
    var = jnp.mean(centered * centered, axis=-1, keepdims=True)
    out = (centered * lax.rsqrt(var + 1e-06)).astype(jnp.bfloat16)
    for d in range(o_ref.shape[0]):
        o_ref[d] = out


def norm(rows, n):
    return pl.pallas_call(
        norm_kernel,
        out_shape=jax.ShapeDtypeStruct((n,) + rows.shape, jnp.bfloat16),
        compiler_params=pltpu.CompilerParams(vmem_limit_bytes=4 << 20),
        cost_estimate=pl.CostEstimate(flops=1 << 10, bytes_accessed=1 << 10, transcendentals=0),
        name="norm",
    )(rows)


def ref_kernel(rows_ref, *refs):
    pieces = refs[:8]
    kv_ref, book_ref, x, split, codes = refs[8:]
    me = lax.axis_index("fsdp")
    mz, mx, mc = me // 8, me // 2 % 4, me % 2
    kdim = split.shape[2]
    n, r, _ = rows_ref.shape
    for d in range(n):
        x[d * r : (d + 1) * r, :] = rows_ref[d].astype(jnp.float32)
    for f in range(32):
        split[f] = x[:, f * kdim : (f + 1) * kdim].astype(jnp.bfloat16)
    total = jnp.zeros(kv_ref.shape, jnp.float32)
    for p in range(8):
        core = mc if p < 4 else 1 - mc
        sign = 1 - 2 * core
        kx = p % 4
        for kz in range(4):
            f = (mz - sign * kz + 4) % 4 * 8 + (mx - sign * kx + 4) % 4 * 2 + core
            row = kz * WROWS
            total = total + jnp.dot(
                split[f], pieces[p][row : row + kdim, :], preferred_element_type=jnp.float32
            )
            codes[pl.ds(pl.multiple_of(f * 8, 8), 8), :] = pieces[p][row + kdim : row + WROWS, 0 : 2 * HD].astype(
                jnp.float32
            )[0:8]
    kv_ref[...] = total.astype(jnp.bfloat16)
    book_ref[...] = codes[...].astype(jnp.bfloat16)


def ref_project(rows, pieces, kdim):
    n = pieces[0].shape[1]
    slots = rows.shape[0] * rows.shape[1]
    return pl.pallas_call(
        ref_kernel,
        out_shape=(
            jax.ShapeDtypeStruct((slots, n), jnp.bfloat16),
            jax.ShapeDtypeStruct((256, 2 * HD), jnp.bfloat16),
        ),
        in_specs=[pl.BlockSpec(memory_space=pltpu.VMEM)] * 9,
        out_specs=(pl.BlockSpec(memory_space=pltpu.VMEM), pl.BlockSpec(memory_space=pltpu.VMEM)),
        scratch_shapes=[
            pltpu.VMEM((slots, rows.shape[2]), jnp.float32),
            pltpu.VMEM((32, slots, kdim), jnp.bfloat16),
            pltpu.VMEM((256, 2 * HD), jnp.float32),
        ],
        compiler_params=pltpu.CompilerParams(vmem_limit_bytes=16 << 20),
        cost_estimate=pl.CostEstimate(flops=1 << 10, bytes_accessed=1 << 10, transcendentals=0),
        name="ref_project",
    )(rows, *pieces)


def attend_kernel(tokens, sub, count_ref, q_ref, k_ref, v_ref, ids_ref, book_ref, rk_ref, rv_ref, o_ref):
    entries = book_ref.shape[0]
    keys = k_ref[...].reshape(-1, HD)
    values = v_ref[...].reshape(-1, HD)
    ref_values = rv_ref[...]
    values = jnp.concatenate([values, jnp.ones_like(values)], axis=1)
    ref_values = jnp.concatenate([ref_values, jnp.ones_like(ref_values)], axis=1)
    scale = math.log2(math.e) / math.sqrt(HD)
    nt = (((1,), (1,)), ((), ()))
    for b in range(q_ref.shape[0] // sub):
        parts = []
        for j in range(b * sub, (b + 1) * sub):
            ids = ids_ref[j, 0:1, :].astype(jnp.float32).astype(jnp.int32)
            entry = lax.broadcasted_iota(jnp.int32, (entries, tokens), 0)
            onehot = jnp.where(entry == ids, 1.0, 0.0).astype(jnp.bfloat16)
            lookup = lax.dot_general(
                onehot, book_ref[...], (((0,), (0,)), ((), ())), preferred_element_type=jnp.float32
            )
            parts.append((q_ref[j].astype(jnp.float32) + lookup).astype(jnp.bfloat16))
        q = jnp.concatenate(parts, axis=0)
        s1 = lax.dot_general(q, keys, nt, preferred_element_type=jnp.float32)
        s2 = lax.dot_general(q, rk_ref[...], nt, preferred_element_type=jnp.float32)
        live = lax.broadcasted_iota(jnp.int32, s2.shape, 1) < TPF * count_ref[0]
        s2 = jnp.where(live, s2, -1e30)
        top = jnp.maximum(jnp.max(s1, axis=-1, keepdims=True), jnp.max(s2, axis=-1, keepdims=True)) * scale
        p1 = jnp.exp2(s1 * scale - top).astype(jnp.bfloat16)
        p2 = jnp.where(live, jnp.exp2(s2 * scale - top), 0.0).astype(jnp.bfloat16)
        both = jnp.dot(p1, values, preferred_element_type=jnp.float32)
        both = both + jnp.dot(p2, ref_values, preferred_element_type=jnp.float32)
        out = both[:, :HD] / both[:, HD:]
        o_ref[b * sub : (b + 1) * sub] = out.astype(jnp.bfloat16).reshape(sub, tokens, HD)


def attend(tokens, block, count, book, ref_kv):
    n = block.shape[0]
    per, sub = 8, 4
    slots = ref_kv.shape[0]
    return pl.pallas_call(
        lambda *refs: attend_kernel(tokens, sub, *refs),
        grid_spec=pltpu.PrefetchScalarGridSpec(
            num_scalar_prefetch=1,
            grid=(2, n // per),
            in_specs=[
                pl.BlockSpec((per, tokens, HD), lambda h, i, c: (i, 0, h)),
                pl.BlockSpec((n, tokens, HD), lambda h, i, c: (0, 1, h)),
                pl.BlockSpec((n, tokens, HD), lambda h, i, c: (0, 2, h)),
                pl.BlockSpec((per, IDROWS, HD), lambda h, i, c: (i, 3 * tokens // IDROWS, 0)),
                pl.BlockSpec((book.shape[0], HD), lambda h, i, c: (0, h)),
                pl.BlockSpec((slots, HD), lambda h, i, c: (0, h)),
                pl.BlockSpec((slots, HD), lambda h, i, c: (0, 2 + h)),
            ],
            out_specs=pl.BlockSpec((per, tokens, HD), lambda h, i, c: (i, 0, h)),
        ),
        out_shape=jax.ShapeDtypeStruct((n, tokens, 2 * HD), jnp.bfloat16),
        compiler_params=pltpu.CompilerParams(vmem_limit_bytes=24 << 20),
        cost_estimate=pl.CostEstimate(flops=1 << 10, bytes_accessed=1 << 10, transcendentals=0),
        name="attend",
    )(count, block, block, block, block, book, ref_kv, ref_kv)


def unpack_kernel(r_ref, o_ref, sem):
    width = r_ref.shape[2]
    copies = [
        pltpu.make_async_copy(r_ref.at[d], o_ref.at[:, pl.ds(d * width, width)], sem.at[d])
        for d in range(r_ref.shape[0])
    ]
    for c in copies:
        c.start()
    for c in copies:
        c.wait()


def unpack(received):
    n, tokens, width = received.shape
    return pl.pallas_call(
        unpack_kernel,
        out_shape=jax.ShapeDtypeStruct((tokens, n * width), jnp.bfloat16),
        in_specs=[pl.BlockSpec(memory_space=pl.ANY)],
        out_specs=pl.BlockSpec(memory_space=pl.ANY),
        scratch_shapes=[pltpu.SemaphoreType.DMA((n,))],
        compiler_params=pltpu.CompilerParams(vmem_limit_bytes=1 << 20),
        cost_estimate=pl.CostEstimate(flops=0, bytes_accessed=1 << 10, transcendentals=0),
        name="unpack",
    )(received)


def exchange(x):
    return lax.all_to_all(x, "seq", 0, 0, tiled=True)


def move(block, pairs):
    return lax.ppermute(block, "fsdp", pairs)


def turn(block, step):
    return lax.ppermute(block, "seq", seq_perm(step))


def shards(video_qkv, reference_rows, kv_weight, pose_table, pose_ids, frame_counts):
    tokens = video_qkv.shape[1]
    depth = kv_weight.shape[0]
    n = lax.axis_size("seq")
    rows = exchange(norm(reference_rows[0], n))
    codes = jnp.pad(pose_table, ((0, WROWS - depth - pose_table.shape[0]), (0, kv_weight.shape[2])))
    packed = jnp.concatenate([kv_weight.reshape(depth, -1), codes], axis=0)
    column = jnp.concatenate([packed] + [move(packed, pairs) for pairs in Z_MOVES], axis=0)
    sent = pack(jnp.transpose(video_qkv[0], (1, 0, 2)), pose_ids)
    sent, column, rows = lax.optimization_barrier((sent, column, rows))
    video = exchange(sent)
    ahead, behind = move(column, X_AHEAD), move(column, X_BEHIND)
    far = move(ahead, X_AHEAD)
    own = [column, ahead, far, behind]
    pieces = own + [move(piece, CORE_SWAP) for piece in own]
    ref_kv, book = ref_project(rows, pieces, depth)
    return unpack(exchange(attend(tokens, video, frame_counts, book, ref_kv)))[None]


def solution(mesh):
    placed = (
        P("fsdp", "seq", None, None),
        P("fsdp", "seq", None),
        P("fsdp", None, "seq"),
        P("fsdp", "seq"),
        P("fsdp", "seq"),
        P("fsdp"),
    )
    return jax.shard_map(
        shards, mesh=mesh, in_specs=placed, out_specs=P("fsdp", "seq", None), check_vma=False
    )
```

time: 341 us -> 181 us (0.53)
  the two profiles are of different devices: /device:TPU:4 before, /device:TPU:2 now
where the time goes in v3:
time: 181 us; the launch traced here: 180 us
  waiting for transfers between devices  63.4 us (35%)
  starting transfers between devices  50.6 us (28%)
  blocking collectives  33.3 us (18%)
  Pallas kernels  26 us (14%)
  local copies, waits for them, and re-layouts  5.71 us (3%)
    ppermute x10, starting transfers between devices, move(): return lax.ppermute(block, 'fsdp', pairs)  34.3 us
    all_to_all x1, blocking collectives, exchange(): return lax.all_to_all(x, 'seq', 0, 0, tiled=True)  33.3 us
    all_to_all x2, waiting for transfers between devices, exchange(): return lax.all_to_all(x, 'seq', 0, 0, tiled=True)  31.9 us
    ppermute x10, waiting for transfers between devices, move(): return lax.ppermute(block, 'fsdp', pairs)  31.4 us
    pallas_call x1, Pallas kernels, attend(): pl.pallas_call(lambda *refs: attend_kernel(tokens, sub, *refs), grid_spec...  18.3 us
    all_to_all x2, starting transfers between devices, exchange(): return lax.all_to_all(x, 'seq', 0, 0, tiled=True)  16.2 us
    unnamed x14, local copies, waits for them, and re-layouts  5 us
    pallas_call x1, Pallas kernels, pack(): pl.pallas_call(lambda *refs: pack_kernel(tokens, *refs), out_shape=jax.Sh...  4.22 us
  transfers between devices with their start and end apart: 12, of which 6 were waited for; matrix products, arithmetic and copies ran while one was open for 1% of the time, Pallas kernels for 3%

profile of v3, /device:TPU:2, one launch (start us, length us, event | category | flops | bytes accessed | tf_op | source)
XLA Modules:
  0.0 179.8 jit_solution(3696750944850053063)
XLA Ops:
  0.0 0.0 copy-start.4
  0.0 0.8 copy-done.4
  0.8 1.1 norm.1
  1.9 9.0 %all-to-all-start = ((bf16[16,4,5120]{2,1,0:T(4,128)(2,1)}), bf16[16,4,5120]{2,1,0:T(4,128)(2,1)S(1)}, u32[]{:S(2)}, u32[]{:S(2)}) async-start(bf16[16,4,5120]{2,1,0:T(4,128)(2,1)} %norm.1), calls=%async_computation | async-start | bytes 1310720 | tf_op jit(solution)/shard_map/all_to_all | solution.py:235
  10.9 0.9 copy.7
  11.9 0.7 fusion
  12.6 6.1 %collective-permute-start = (bf16[176,512]{1,0:T(8,128)(2,1)S(1)}, bf16[176,512]{1,0:T(8,128)(2,1)S(1)}, u32[]{:S(2)}, u32[]{:S(2)}) collective-permute-start(bf16[176,512]{1,0:T(8,128)(2,1)S(1)} %pad_maximum_fusion), channel_id=1, source_target_pairs={{0,128},{16,400},{32,160},{48,432},{64,192},{80,464},{96,224},{112... | collective-permute-start | bytes 540680 | tf_op jit(solution)/shard_map/ppermute | solution.py:239
  18.7 8.2 %collective-permute-start.1 = (bf16[176,512]{1,0:T(8,128)(2,1)S(1)}, bf16[176,512]{1,0:T(8,128)(2,1)S(1)}, u32[]{:S(2)}, u32[]{:S(2)}) collective-permute-start(bf16[176,512]{1,0:T(8,128)(2,1)S(1)} %pad_maximum_fusion), channel_id=1, source_target_pairs={{0,256},{16,272},{32,288},{48,304},{64,320},{80,336},{96,352},{112... | collective-permute-start | bytes 540680 | tf_op jit(solution)/shard_map/ppermute | solution.py:239
  26.9 3.7 %collective-permute-start.2 = (bf16[176,512]{1,0:T(8,128)(2,1)S(1)}, bf16[176,512]{1,0:T(8,128)(2,1)S(1)}, u32[]{:S(2)}, u32[]{:S(2)}) collective-permute-start(bf16[176,512]{1,0:T(8,128)(2,1)S(1)} %pad_maximum_fusion), channel_id=1, source_target_pairs={{0,384},{16,144},{32,416},{48,176},{64,448},{80,208},{96,480},{112... | collective-permute-start | bytes 540680 | tf_op jit(solution)/shard_map/ppermute | solution.py:239
  30.6 4.2 %pack.1 = bf16[16,400,256]{2,1,0:T(8,128)(2,1)} custom-call(bf16[3,128,4096]{2,1,0:T(8,128)(2,1)} %bitcast.8, s32[1,128]{1,0:T(1,128)} %refs_1_.1), custom_call_target="tpu_custom_call" | custom-call | bytes 6291456 | tf_op jit(solution)/shard_map/pack/pallas_call | solution.py:61
  34.8 3.4 %collective-permute-done = bf16[176,512]{1,0:T(8,128)(2,1)S(1)} collective-permute-done((bf16[176,512]{1,0:T(8,128)(2,1)S(1)}, bf16[176,512]{1,0:T(8,128)(2,1)S(1)}, u32[]{:S(2)}, u32[]{:S(2)}) %collective-permute-start) | collective-permute-done | bytes 180256 | tf_op jit(solution)/shard_map/ppermute | solution.py:239
  38.3 6.9 %collective-permute-done.1 = bf16[176,512]{1,0:T(8,128)(2,1)S(1)} collective-permute-done((bf16[176,512]{1,0:T(8,128)(2,1)S(1)}, bf16[176,512]{1,0:T(8,128)(2,1)S(1)}, u32[]{:S(2)}, u32[]{:S(2)}) %collective-permute-start.1) | collective-permute-done | bytes 180256 | tf_op jit(solution)/shard_map/ppermute | solution.py:239
  45.2 0.0 collective-permute-done.2
  45.2 0.0 copy-start.2
  45.3 0.0 all-to-all-done.rows_ref
  45.3 0.0 copy-start
  45.3 0.9 copy-done
  46.1 0.2 copy-done.2
  46.3 7.2 %all-to-all-start.1 = ((bf16[16,400,256]{2,1,0:T(8,128)(2,1)}), bf16[16,400,256]{2,1,0:T(8,128)(2,1)S(1)}, u32[]{:S(2)}, u32[]{:S(2)}) async-start(bf16[16,400,256]{2,1,0:T(8,128)(2,1)} %pack.1), calls=%async_computation.1 | async-start | bytes 6553600 | tf_op jit(solution)/shard_map/all_to_all | solution.py:235
  53.6 3.4 %collective-permute-start.3 = (bf16[704,512]{1,0:T(8,128)(2,1)}, bf16[704,512]{1,0:T(8,128)(2,1)S(1)}, u32[]{:S(2)}, u32[]{:S(2)}) collective-permute-start(bf16[704,512]{1,0:T(8,128)(2,1)} %copy-done.2), channel_id=1, source_target_pairs={{0,32},{16,112},{32,64},{48,16},{64,96},{80,48},{96,0},{112,80},{1... | collective-permute-start | bytes 2162696 | tf_op jit(solution)/shard_map/ppermute | solution.py:239
  57.0 2.4 %collective-permute-start.5 = (bf16[704,512]{1,0:T(8,128)(2,1)}, bf16[704,512]{1,0:T(8,128)(2,1)S(1)}, u32[]{:S(2)}, u32[]{:S(2)}) collective-permute-start(bf16[704,512]{1,0:T(8,128)(2,1)} %copy-done.2), channel_id=1, source_target_pairs={{0,96},{16,48},{32,0},{48,80},{64,32},{80,112},{96,64},{112,16},{1... | collective-permute-start | bytes 2162696 | tf_op jit(solution)/shard_map/ppermute | solution.py:239
  59.4 15.0 %collective-permute-done.3.refs_1_ = bf16[704,512]{1,0:T(8,128)(2,1)S(1)} collective-permute-done((bf16[704,512]{1,0:T(8,128)(2,1)}, bf16[704,512]{1,0:T(8,128)(2,1)S(1)}, u32[]{:S(2)}, u32[]{:S(2)}) %collective-permute-start.3) | collective-permute-done | bytes 720928 | tf_op jit(solution)/shard_map/ppermute | solution.py:239
  74.5 2.4 %collective-permute-start.4 = (bf16[704,512]{1,0:T(8,128)(2,1)S(1)}, bf16[704,512]{1,0:T(8,128)(2,1)S(1)}, u32[]{:S(2)}, u32[]{:S(2)}) collective-permute-start(bf16[704,512]{1,0:T(8,128)(2,1)S(1)} %collective-permute-done.3.refs_1_), channel_id=1, source_target_pairs={{0,32},{16,112},{32,64},{48,16},{64,96},{80,48},{96,0},{112,80},{1... | collective-permute-start | bytes 2162696 | tf_op jit(solution)/shard_map/ppermute | solution.py:239
  76.8 1.9 %collective-permute-start.6 = (bf16[704,512]{1,0:T(8,128)(2,1)}, bf16[704,512]{1,0:T(8,128)(2,1)S(1)}, u32[]{:S(2)}, u32[]{:S(2)}) collective-permute-start(bf16[704,512]{1,0:T(8,128)(2,1)} %copy-done.2), channel_id=1, source_target_pairs={{0,16},{16,0},{32,48},{48,32},{64,80},{80,64},{96,112},{112,96},{1... | collective-permute-start | bytes 2162696 | tf_op jit(solution)/shard_map/ppermute | solution.py:239
  78.8 2.4 %collective-permute-start.7 = (bf16[704,512]{1,0:T(8,128)(2,1)S(1)}, bf16[704,512]{1,0:T(8,128)(2,1)S(1)}, u32[]{:S(2)}, u32[]{:S(2)}) collective-permute-start(bf16[704,512]{1,0:T(8,128)(2,1)S(1)} %collective-permute-done.3.refs_1_), channel_id=1, source_target_pairs={{0,16},{16,0},{32,48},{48,32},{64,80},{80,64},{96,112},{112,96},{1... | collective-permute-start | bytes 2162696 | tf_op jit(solution)/shard_map/ppermute | solution.py:239
  81.2 0.0 collective-permute-done.5.refs_3_
  81.2 1.9 %collective-permute-start.9 = (bf16[704,512]{1,0:T(8,128)(2,1)S(1)}, bf16[704,512]{1,0:T(8,128)(2,1)S(1)}, u32[]{:S(2)}, u32[]{:S(2)}) collective-permute-start(bf16[704,512]{1,0:T(8,128)(2,1)S(1)} %collective-permute-done.5.refs_3_), channel_id=1, source_target_pairs={{0,16},{16,0},{32,48},{48,32},{64,80},{80,64},{96,112},{112,96},{1... | collective-permute-start | bytes 2162696 | tf_op jit(solution)/shard_map/ppermute | solution.py:239
  83.1 4.5 %collective-permute-done.4.refs_2_ = bf16[704,512]{1,0:T(8,128)(2,1)S(1)} collective-permute-done((bf16[704,512]{1,0:T(8,128)(2,1)S(1)}, bf16[704,512]{1,0:T(8,128)(2,1)S(1)}, u32[]{:S(2)}, u32[]{:S(2)}) %collective-permute-start.4) | collective-permute-done | bytes 720928 | tf_op jit(solution)/shard_map/ppermute | solution.py:239
  87.6 1.9 %collective-permute-start.8 = (bf16[704,512]{1,0:T(8,128)(2,1)S(1)}, bf16[704,512]{1,0:T(8,128)(2,1)S(1)}, u32[]{:S(2)}, u32[]{:S(2)}) collective-permute-start(bf16[704,512]{1,0:T(8,128)(2,1)S(1)} %collective-permute-done.4.refs_2_), channel_id=1, source_target_pairs={{0,16},{16,0},{32,48},{48,32},{64,80},{80,64},{96,112},{112,96},{1... | collective-permute-start | bytes 2162696 | tf_op jit(solution)/shard_map/ppermute | solution.py:239
  90.2 0.0 collective-permute-done.6.refs_4_
  90.2 0.0 collective-permute-done.7.refs_5_
  90.2 0.0 collective-permute-done.9.refs_7_
  90.2 1.5 collective-permute-done.8.refs_6_
  91.7 0.0 copy-start.1
  91.7 1.1 copy-done.1
  92.8 0.0 copy-start.3
  92.8 1.1 copy-done.3
  93.9 1.2 ref_project.1
  95.1 31.9 %all-to-all-done.1.refs_1_.refs_2_.refs_3_.refs_4_ = bf16[16,400,256]{2,1,0:T(8,128)(2,1)S(1)} async-done(((bf16[16,400,256]{2,1,0:T(8,128)(2,1)}), bf16[16,400,256]{2,1,0:T(8,128)(2,1)S(1)}, u32[]{:S(2)}, u32[]{:S(2)}) %all-to-all-start.1) | async-done | bytes 3276832 | tf_op jit(solution)/shard_map/all_to_all | solution.py:235
  127.1 18.3 %attend.1 = bf16[16,128,256]{2,1,0:T(8,128)(2,1)S(1)} custom-call(s32[1]{0:T(128)S(6)} %copy.12.refs_0_, bf16[16,400,256]{2,1,0:T(8,128)(2,1)S(1)} %all-to-all-done.1.refs_1_.refs_2_.refs_3_.refs_4_, bf16[16,400,256]{2,1,0:T(8,128)(2,1)S(1)} %all-to-all-done.1.refs_1_.refs_2_.refs_3_.refs_4_, ...), custom_call_target="tpu_custom_call" | custom-call | flops 1024 | bytes 1024 | tf_op jit(solution)/shard_map/attend/pallas_call | solution.py:185
  145.4 33.3 %all_to_all.15.r_ref = bf16[16,128,256]{2,1,0:T(8,128)(2,1)S(1)} all-to-all(bf16[16,128,256]{2,1,0:T(8,128)(2,1)S(1)} %attend.1), channel_id=1, replica_groups=mesh['fsdp'=32,'seq'=16] {'seq'}, dimensions={0} | all-to-all | bytes 2097152 | tf_op jit(solution)/shard_map/all_to_all | solution.py:235
  178.7 1.1 unpack.1
  (5 shorter events, 0.1 us)
Async XLA Ops:
  0.0 0.8 copy-start.4
  1.9 43.3 %all-to-all-start = ((bf16[16,4,5120]{2,1,0:T(4,128)(2,1)}), bf16[16,4,5120]{2,1,0:T(4,128)(2,1)S(1)}, u32[]{:S(2)}, u32[]{:S(2)}) async-start(bf16[16,4,5120]{2,1,0:T(4,128)(2,1)} %norm.1), calls=%async_computation | async-start | bytes 1310720 | tf_op jit(solution)/shard_map/all_to_all | solution.py:235
  12.6 25.6 %collective-permute-start = (bf16[176,512]{1,0:T(8,128)(2,1)S(1)}, bf16[176,512]{1,0:T(8,128)(2,1)S(1)}, u32[]{:S(2)}, u32[]{:S(2)}) collective-permute-start(bf16[176,512]{1,0:T(8,128)(2,1)S(1)} %pad_maximum_fusion), channel_id=1, source_target_pairs={{0,128},{16,400},{32,160},{48,432},{64,192},{80,464},{96,224},{112... | collective-permute-start | bytes 540680 | tf_op jit(solution)/shard_map/ppermute | solution.py:239
  18.7 26.5 %collective-permute-start.1 = (bf16[176,512]{1,0:T(8,128)(2,1)S(1)}, bf16[176,512]{1,0:T(8,128)(2,1)S(1)}, u32[]{:S(2)}, u32[]{:S(2)}) collective-permute-start(bf16[176,512]{1,0:T(8,128)(2,1)S(1)} %pad_maximum_fusion), channel_id=1, source_target_pairs={{0,256},{16,272},{32,288},{48,304},{64,320},{80,336},{96,352},{112... | collective-permute-start | bytes 540680 | tf_op jit(solution)/shard_map/ppermute | solution.py:239
  26.9 18.3 %collective-permute-start.2 = (bf16[176,512]{1,0:T(8,128)(2,1)S(1)}, bf16[176,512]{1,0:T(8,128)(2,1)S(1)}, u32[]{:S(2)}, u32[]{:S(2)}) collective-permute-start(bf16[176,512]{1,0:T(8,128)(2,1)S(1)} %pad_maximum_fusion), channel_id=1, source_target_pairs={{0,384},{16,144},{32,416},{48,176},{64,448},{80,208},{96,480},{112... | collective-permute-start | bytes 540680 | tf_op jit(solution)/shard_map/ppermute | solution.py:239
  45.2 1.1 copy-start.2
  45.3 0.9 copy-start
  46.3 80.7 %all-to-all-start.1 = ((bf16[16,400,256]{2,1,0:T(8,128)(2,1)}), bf16[16,400,256]{2,1,0:T(8,128)(2,1)S(1)}, u32[]{:S(2)}, u32[]{:S(2)}) async-start(bf16[16,400,256]{2,1,0:T(8,128)(2,1)} %pack.1), calls=%async_computation.1 | async-start | bytes 6553600 | tf_op jit(solution)/shard_map/all_to_all | solution.py:235
  53.6 20.9 %collective-permute-start.3 = (bf16[704,512]{1,0:T(8,128)(2,1)}, bf16[704,512]{1,0:T(8,128)(2,1)S(1)}, u32[]{:S(2)}, u32[]{:S(2)}) collective-permute-start(bf16[704,512]{1,0:T(8,128)(2,1)} %copy-done.2), channel_id=1, source_target_pairs={{0,32},{16,112},{32,64},{48,16},{64,96},{80,48},{96,0},{112,80},{1... | collective-permute-start | bytes 2162696 | tf_op jit(solution)/shard_map/ppermute | solution.py:239
  57.0 24.2 %collective-permute-start.5 = (bf16[704,512]{1,0:T(8,128)(2,1)}, bf16[704,512]{1,0:T(8,128)(2,1)S(1)}, u32[]{:S(2)}, u32[]{:S(2)}) collective-permute-start(bf16[704,512]{1,0:T(8,128)(2,1)} %copy-done.2), channel_id=1, source_target_pairs={{0,96},{16,48},{32,0},{48,80},{64,32},{80,112},{96,64},{112,16},{1... | collective-permute-start | bytes 2162696 | tf_op jit(solution)/shard_map/ppermute | solution.py:239
  74.5 13.2 %collective-permute-start.4 = (bf16[704,512]{1,0:T(8,128)(2,1)S(1)}, bf16[704,512]{1,0:T(8,128)(2,1)S(1)}, u32[]{:S(2)}, u32[]{:S(2)}) collective-permute-start(bf16[704,512]{1,0:T(8,128)(2,1)S(1)} %collective-permute-done.3.refs_1_), channel_id=1, source_target_pairs={{0,32},{16,112},{32,64},{48,16},{64,96},{80,48},{96,0},{112,80},{1... | collective-permute-start | bytes 2162696 | tf_op jit(solution)/shard_map/ppermute | solution.py:239
  76.8 13.4 %collective-permute-start.6 = (bf16[704,512]{1,0:T(8,128)(2,1)}, bf16[704,512]{1,0:T(8,128)(2,1)S(1)}, u32[]{:S(2)}, u32[]{:S(2)}) collective-permute-start(bf16[704,512]{1,0:T(8,128)(2,1)} %copy-done.2), channel_id=1, source_target_pairs={{0,16},{16,0},{32,48},{48,32},{64,80},{80,64},{96,112},{112,96},{1... | collective-permute-start | bytes 2162696 | tf_op jit(solution)/shard_map/ppermute | solution.py:239
  78.8 11.4 %collective-permute-start.7 = (bf16[704,512]{1,0:T(8,128)(2,1)S(1)}, bf16[704,512]{1,0:T(8,128)(2,1)S(1)}, u32[]{:S(2)}, u32[]{:S(2)}) collective-permute-start(bf16[704,512]{1,0:T(8,128)(2,1)S(1)} %collective-permute-done.3.refs_1_), channel_id=1, source_target_pairs={{0,16},{16,0},{32,48},{48,32},{64,80},{80,64},{96,112},{112,96},{1... | collective-permute-start | bytes 2162696 | tf_op jit(solution)/shard_map/ppermute | solution.py:239
  81.2 9.0 %collective-permute-start.9 = (bf16[704,512]{1,0:T(8,128)(2,1)S(1)}, bf16[704,512]{1,0:T(8,128)(2,1)S(1)}, u32[]{:S(2)}, u32[]{:S(2)}) collective-permute-start(bf16[704,512]{1,0:T(8,128)(2,1)S(1)} %collective-permute-done.5.refs_3_), channel_id=1, source_target_pairs={{0,16},{16,0},{32,48},{48,32},{64,80},{80,64},{96,112},{112,96},{1... | collective-permute-start | bytes 2162696 | tf_op jit(solution)/shard_map/ppermute | solution.py:239
  87.6 4.1 %collective-permute-start.8 = (bf16[704,512]{1,0:T(8,128)(2,1)S(1)}, bf16[704,512]{1,0:T(8,128)(2,1)S(1)}, u32[]{:S(2)}, u32[]{:S(2)}) collective-permute-start(bf16[704,512]{1,0:T(8,128)(2,1)S(1)} %collective-permute-done.4.refs_2_), channel_id=1, source_target_pairs={{0,16},{16,0},{32,48},{48,32},{64,80},{80,64},{96,112},{112,96},{1... | collective-permute-start | bytes 2162696 | tf_op jit(solution)/shard_map/ppermute | solution.py:239
  91.7 1.1 copy-start.1
  92.8 1.1 copy-start.3

commit v4 on v3

--- a/solution.py
+++ b/solution.py
@@ -10,7 +10,7 @@
 HD = 128
 TPF = 16
 WROWS = 176
-IDROWS = 16
+SIDE = 8
 
 
 def fsdp_perm(move):
@@ -29,17 +29,26 @@
 X_AHEAD = fsdp_perm(lambda z, x, c: (z, x + direction(c), c))
 X_BEHIND = fsdp_perm(lambda z, x, c: (z, x - direction(c), c))
 CORE_SWAP = fsdp_perm(lambda z, x, c: (z, x, 1 - c))
-def pack_kernel(tokens, x_ref, ids_ref, o_ref, held, ids, in_sem, out_sem):
-    planes, _, width = held.shape
+def pack_kernel(x_ref, rows_ref, ids_ref, o_ref, held, side32, side, in_sem, out_sem):
+    planes, tokens, _ = held.shape
     n = o_ref.shape[0]
     loads = [pltpu.make_async_copy(x_ref.at[k], held.at[k], in_sem.at[k]) for k in range(planes)]
     for load in loads:
         load.start()
-    ids[...] = jnp.broadcast_to(ids_ref[...].astype(jnp.float32), (2 * IDROWS, tokens))[0:IDROWS].astype(jnp.bfloat16)
+    x = rows_ref[...].astype(jnp.float32)
+    mean = jnp.mean(x, axis=-1, keepdims=True)
+    centered = x - mean
+    var = jnp.mean(centered * centered, axis=-1, keepdims=True)
+    out = centered * lax.rsqrt(var + 1e-06)
+    r, width = x.shape
+    chunks = width // (2 * HD)
+    for c in range(chunks):
+        side32[c * r : (c + 1) * r, :] = out[:, c * 2 * HD : (c + 1) * 2 * HD]
+    ids = jnp.broadcast_to(ids_ref[...].astype(jnp.float32), (SIDE, tokens))
+    side32[chunks * r :, 0:tokens] = ids
+    side32[chunks * r :, tokens:] = ids
+    side[...] = side32[...].astype(jnp.bfloat16)
     stores = []
-    for d in range(n):
-        rows = o_ref.at[d, pl.ds(planes * tokens, IDROWS), pl.ds(0, tokens)]
-        stores.append(pltpu.make_async_copy(ids, rows, out_sem.at[len(stores)]))
     for k in range(planes):
         loads[k].wait()
         for d in range(n):
@@ -48,50 +57,38 @@
             copy = pltpu.make_async_copy(part, rows, out_sem.at[len(stores)])
             copy.start()
             stores.append(copy)
-    for copy in stores[:n]:
+    for d in range(n):
+        rows = o_ref.at[d, pl.ds(planes * tokens, side.shape[0]), :]
+        copy = pltpu.make_async_copy(side, rows, out_sem.at[len(stores)])
         copy.start()
+        stores.append(copy)
     for copy in stores:
         copy.wait()
 
 
-def pack(video, ids):
+def pack(video, rows, ids):
     planes, tokens, width = video.shape
     n = width // (2 * HD)
-    long = planes * tokens + IDROWS
-    return pl.pallas_call(
-        lambda *refs: pack_kernel(tokens, *refs),
-        out_shape=jax.ShapeDtypeStruct((n, long, 2 * HD), jnp.bfloat16),
-        in_specs=[pl.BlockSpec(memory_space=pl.ANY), pl.BlockSpec(memory_space=pltpu.VMEM)],
+    extra = rows.shape[0] * rows.shape[1] // (2 * HD) + SIDE
+    return pl.pallas_call(
+        pack_kernel,
+        out_shape=jax.ShapeDtypeStruct((n, planes * tokens + extra, 2 * HD), jnp.bfloat16),
+        in_specs=[
+            pl.BlockSpec(memory_space=pl.ANY),
+            pl.BlockSpec(memory_space=pltpu.VMEM),
+            pl.BlockSpec(memory_space=pltpu.VMEM),
+        ],
         out_specs=pl.BlockSpec(memory_space=pl.ANY),
         scratch_shapes=[
             pltpu.VMEM(video.shape, jnp.bfloat16),
-            pltpu.VMEM((IDROWS, tokens), jnp.bfloat16),
+            pltpu.VMEM((extra, 2 * HD), jnp.float32),
+            pltpu.VMEM((extra, 2 * HD), jnp.bfloat16),
             pltpu.SemaphoreType.DMA((planes,)),
             pltpu.SemaphoreType.DMA(((planes + 1) * n,)),
         ],
         cost_estimate=pl.CostEstimate(flops=0, bytes_accessed=6 << 20, transcendentals=0),
         name="pack",
-    )(video, ids)
-
-
-def norm_kernel(x_ref, o_ref):
-    x = x_ref[...].astype(jnp.float32)
-    mean = jnp.mean(x, axis=-1, keepdims=True)
-    centered = x - mean
-    var = jnp.mean(centered * centered, axis=-1, keepdims=True)
-    out = (centered * lax.rsqrt(var + 1e-06)).astype(jnp.bfloat16)
-    for d in range(o_ref.shape[0]):
-        o_ref[d] = out
-
-
-def norm(rows, n):
-    return pl.pallas_call(
-        norm_kernel,
-        out_shape=jax.ShapeDtypeStruct((n,) + rows.shape, jnp.bfloat16),
-        compiler_params=pltpu.CompilerParams(vmem_limit_bytes=4 << 20),
-        cost_estimate=pl.CostEstimate(flops=1 << 10, bytes_accessed=1 << 10, transcendentals=0),
-        name="norm",
-    )(rows)
+    )(video, rows, ids)
 
 
 def ref_kernel(rows_ref, *refs):
@@ -100,9 +97,12 @@
     me = lax.axis_index("fsdp")
     mz, mx, mc = me // 8, me // 2 % 4, me % 2
     kdim = split.shape[2]
-    n, r, _ = rows_ref.shape
+    n, chunk = rows_ref.shape[0], rows_ref.shape[2]
+    r = x.shape[0] // n
     for d in range(n):
-        x[d * r : (d + 1) * r, :] = rows_ref[d].astype(jnp.float32)
+        got = rows_ref[d].astype(jnp.float32)
+        for c in range(x.shape[1] // chunk):
+            x[d * r : (d + 1) * r, c * chunk : (c + 1) * chunk] = got[c * r : (c + 1) * r, :]
     for f in range(32):
         split[f] = x[:, f * kdim : (f + 1) * kdim].astype(jnp.bfloat16)
     total = jnp.zeros(kv_ref.shape, jnp.float32)
@@ -123,9 +123,9 @@
     book_ref[...] = codes[...].astype(jnp.bfloat16)
 
 
-def ref_project(rows, pieces, kdim):
+def ref_project(rows, pieces, kdim, depth):
     n = pieces[0].shape[1]
-    slots = rows.shape[0] * rows.shape[1]
+    slots = rows.shape[0] * (rows.shape[1] - SIDE) * rows.shape[2] // depth
     return pl.pallas_call(
         ref_kernel,
         out_shape=(
@@ -135,7 +135,7 @@
         in_specs=[pl.BlockSpec(memory_space=pltpu.VMEM)] * 9,
         out_specs=(pl.BlockSpec(memory_space=pltpu.VMEM), pl.BlockSpec(memory_space=pltpu.VMEM)),
         scratch_shapes=[
-            pltpu.VMEM((slots, rows.shape[2]), jnp.float32),
+            pltpu.VMEM((slots, depth), jnp.float32),
             pltpu.VMEM((32, slots, kdim), jnp.bfloat16),
             pltpu.VMEM((256, 2 * HD), jnp.float32),
         ],
@@ -178,7 +178,7 @@
         o_ref[b * sub : (b + 1) * sub] = out.astype(jnp.bfloat16).reshape(sub, tokens, HD)
 
 
-def attend(tokens, block, count, book, ref_kv):
+def attend(tokens, block, rows, count, book, ref_kv):
     n = block.shape[0]
     per, sub = 8, 4
     slots = ref_kv.shape[0]
@@ -191,7 +191,7 @@
                 pl.BlockSpec((per, tokens, HD), lambda h, i, c: (i, 0, h)),
                 pl.BlockSpec((n, tokens, HD), lambda h, i, c: (0, 1, h)),
                 pl.BlockSpec((n, tokens, HD), lambda h, i, c: (0, 2, h)),
-                pl.BlockSpec((per, IDROWS, HD), lambda h, i, c: (i, 3 * tokens // IDROWS, 0)),
+                pl.BlockSpec((per, SIDE, HD), lambda h, i, c: (i, rows.shape[1] // SIDE - 1, 0)),
                 pl.BlockSpec((book.shape[0], HD), lambda h, i, c: (0, h)),
                 pl.BlockSpec((slots, HD), lambda h, i, c: (0, h)),
                 pl.BlockSpec((slots, HD), lambda h, i, c: (0, 2 + h)),
@@ -202,7 +202,7 @@
         compiler_params=pltpu.CompilerParams(vmem_limit_bytes=24 << 20),
         cost_estimate=pl.CostEstimate(flops=1 << 10, bytes_accessed=1 << 10, transcendentals=0),
         name="attend",
-    )(count, block, block, block, block, book, ref_kv, ref_kv)
+    )(count, block, block, block, rows, book, ref_kv, ref_kv)
 
 
 def unpack_kernel(r_ref, o_ref, sem):
@@ -244,22 +244,20 @@
 
 
 def shards(video_qkv, reference_rows, kv_weight, pose_table, pose_ids, frame_counts):
+    planes_rows = 3 * video_qkv.shape[1]
     tokens = video_qkv.shape[1]
     depth = kv_weight.shape[0]
-    n = lax.axis_size("seq")
-    rows = exchange(norm(reference_rows[0], n))
+    video = exchange(pack(jnp.transpose(video_qkv[0], (1, 0, 2)), reference_rows[0], pose_ids))
     codes = jnp.pad(pose_table, ((0, WROWS - depth - pose_table.shape[0]), (0, kv_weight.shape[2])))
     packed = jnp.concatenate([kv_weight.reshape(depth, -1), codes], axis=0)
     column = jnp.concatenate([packed] + [move(packed, pairs) for pairs in Z_MOVES], axis=0)
-    sent = pack(jnp.transpose(video_qkv[0], (1, 0, 2)), pose_ids)
-    sent, column, rows = lax.optimization_barrier((sent, column, rows))
-    video = exchange(sent)
     ahead, behind = move(column, X_AHEAD), move(column, X_BEHIND)
     far = move(ahead, X_AHEAD)
     own = [column, ahead, far, behind]
     pieces = own + [move(piece, CORE_SWAP) for piece in own]
-    ref_kv, book = ref_project(rows, pieces, depth)
-    return unpack(exchange(attend(tokens, video, frame_counts, book, ref_kv)))[None]
+    rows = video[:, planes_rows:, :]
+    ref_kv, book = ref_project(rows, pieces, depth, reference_rows.shape[2])
+    return unpack(exchange(attend(tokens, video, rows, frame_counts, book, ref_kv)))[None]
 
 
 def solution(mesh):

time: 181 us -> 164 us (0.906)
  the two profiles are of different devices: /device:TPU:2 before, /device:TPU:12 now
where the time goes in v4:
time: 164 us; the launch traced here: 163 us
  waiting for transfers between devices  52.5 us (32%)
  starting transfers between devices  44.3 us (27%)
  blocking collectives  36.4 us (22%)
  Pallas kernels  27.6 us (17%)
    ppermute x10, waiting for transfers between devices, move(): return lax.ppermute(block, 'fsdp', pairs)  36.7 us
    all_to_all x1, blocking collectives, exchange(): return lax.all_to_all(x, 'seq', 0, 0, tiled=True)  36.4 us
    ppermute x10, starting transfers between devices, move(): return lax.ppermute(block, 'fsdp', pairs)  34.8 us
    pallas_call x1, Pallas kernels, attend(): pl.pallas_call(lambda *refs: attend_kernel(tokens, sub, *refs), grid_spec...  19.1 us
    all_to_all x1, waiting for transfers between devices, exchange(): return lax.all_to_all(x, 'seq', 0, 0, tiled=True)  15.8 us
    all_to_all x1, starting transfers between devices, exchange(): return lax.all_to_all(x, 'seq', 0, 0, tiled=True)  9.51 us
    pallas_call x1, Pallas kernels, pack(): pl.pallas_call(pack_kernel, out_shape=jax.ShapeDtypeStruct((n, planes * t...  4.49 us
  transfers between devices with their start and end apart: 11, of which 5 were waited for; matrix products, arithmetic and copies ran while one was open for 1% of the time, Pallas kernels for 0%

profile of v4, /device:TPU:12, one launch (start us, length us, event | category | flops | bytes accessed | tf_op | source)
XLA Modules:
  0.0 163.0 jit_solution(15020798940704336782)
XLA Ops:
  0.0 4.5 %pack.1 = bf16[16,472,256]{2,1,0:T(8,128)(2,1)} custom-call(bf16[3,128,4096]{2,1,0:T(8,128)(2,1)} %bitcast.7, bf16[4,5120]{1,0:T(4,128)(2,1)} %bitcast.11, s32[1,128]{1,0:T(1,128)} %ids_ref.1), custom_call_target="tpu_custom_call" | custom-call | bytes 6291456 | tf_op jit(solution)/shard_map/pack/pallas_call | solution.py:73
  4.5 0.0 copy-start
  4.5 0.0 copy-start.1
  4.5 9.5 %all-to-all-start = ((bf16[16,472,256]{2,1,0:T(8,128)(2,1)}), bf16[16,472,256]{2,1,0:T(8,128)(2,1)}, u32[]{:S(2)}, u32[]{:S(2)}) async-start(bf16[16,472,256]{2,1,0:T(8,128)(2,1)} %pack.1), calls=%async_computation | async-start | bytes 7733248 | tf_op jit(solution)/shard_map/all_to_all | solution.py:235
  14.0 0.0 copy-done
  14.1 0.0 copy-done.1
  14.1 6.1 %collective-permute-start = (bf16[176,512]{1,0:T(8,128)(2,1)S(1)}, bf16[176,512]{1,0:T(8,128)(2,1)S(1)}, u32[]{:S(2)}, u32[]{:S(2)}) collective-permute-start(bf16[176,512]{1,0:T(8,128)(2,1)S(1)} %pad_maximum_fusion), channel_id=1, source_target_pairs={{0,128},{16,400},{32,160},{48,432},{64,192},{80,464},{96,224},{112... | collective-permute-start | bytes 540680 | tf_op jit(solution)/shard_map/ppermute | solution.py:239
  20.2 8.2 %collective-permute-start.1 = (bf16[176,512]{1,0:T(8,128)(2,1)S(1)}, bf16[176,512]{1,0:T(8,128)(2,1)S(1)}, u32[]{:S(2)}, u32[]{:S(2)}) collective-permute-start(bf16[176,512]{1,0:T(8,128)(2,1)S(1)} %pad_maximum_fusion), channel_id=1, source_target_pairs={{0,256},{16,272},{32,288},{48,304},{64,320},{80,336},{96,352},{112... | collective-permute-start | bytes 540680 | tf_op jit(solution)/shard_map/ppermute | solution.py:239
  28.5 3.7 %collective-permute-start.2 = (bf16[176,512]{1,0:T(8,128)(2,1)S(1)}, bf16[176,512]{1,0:T(8,128)(2,1)S(1)}, u32[]{:S(2)}, u32[]{:S(2)}) collective-permute-start(bf16[176,512]{1,0:T(8,128)(2,1)S(1)} %pad_maximum_fusion), channel_id=1, source_target_pairs={{0,384},{16,144},{32,416},{48,176},{64,448},{80,208},{96,480},{112... | collective-permute-start | bytes 540680 | tf_op jit(solution)/shard_map/ppermute | solution.py:239
  32.1 18.3 %collective-permute-done = bf16[176,512]{1,0:T(8,128)(2,1)S(1)} collective-permute-done((bf16[176,512]{1,0:T(8,128)(2,1)S(1)}, bf16[176,512]{1,0:T(8,128)(2,1)S(1)}, u32[]{:S(2)}, u32[]{:S(2)}) %collective-permute-start) | collective-permute-done | bytes 180256 | tf_op jit(solution)/shard_map/ppermute | solution.py:239
  50.5 1.3 collective-permute-done.1
  51.8 0.0 collective-permute-done.2
  51.8 3.1 %collective-permute-start.3 = (bf16[704,512]{1,0:T(8,128)(2,1)S(1)}, bf16[704,512]{1,0:T(8,128)(2,1)S(1)}, u32[]{:S(2)}, u32[]{:S(2)}) collective-permute-start(bf16[704,512]{1,0:T(8,128)(2,1)S(1)} %constant_dynamic-update-slice_fusion.refs_0_), channel_id=1, source_target_pairs={{0,32},{16,112},{32,64},{48,16},{64,96},{80,48},{96,0},{112,80},{1... | collective-permute-start | bytes 2162696 | tf_op jit(solution)/shard_map/ppermute | solution.py:239
  54.9 2.7 %collective-permute-start.5 = (bf16[704,512]{1,0:T(8,128)(2,1)S(1)}, bf16[704,512]{1,0:T(8,128)(2,1)S(1)}, u32[]{:S(2)}, u32[]{:S(2)}) collective-permute-start(bf16[704,512]{1,0:T(8,128)(2,1)S(1)} %constant_dynamic-update-slice_fusion.refs_0_), channel_id=1, source_target_pairs={{0,96},{16,48},{32,0},{48,80},{64,32},{80,112},{96,64},{112,16},{1... | collective-permute-start | bytes 2162696 | tf_op jit(solution)/shard_map/ppermute | solution.py:239
  57.7 13.0 %collective-permute-done.3.refs_1_ = bf16[704,512]{1,0:T(8,128)(2,1)S(1)} collective-permute-done((bf16[704,512]{1,0:T(8,128)(2,1)S(1)}, bf16[704,512]{1,0:T(8,128)(2,1)S(1)}, u32[]{:S(2)}, u32[]{:S(2)}) %collective-permute-start.3) | collective-permute-done | bytes 720928 | tf_op jit(solution)/shard_map/ppermute | solution.py:239
  70.7 2.8 %collective-permute-start.4 = (bf16[704,512]{1,0:T(8,128)(2,1)S(1)}, bf16[704,512]{1,0:T(8,128)(2,1)S(1)}, u32[]{:S(2)}, u32[]{:S(2)}) collective-permute-start(bf16[704,512]{1,0:T(8,128)(2,1)S(1)} %collective-permute-done.3.refs_1_), channel_id=1, source_target_pairs={{0,32},{16,112},{32,64},{48,16},{64,96},{80,48},{96,0},{112,80},{1... | collective-permute-start | bytes 2162696 | tf_op jit(solution)/shard_map/ppermute | solution.py:239
  73.5 1.9 %collective-permute-start.6 = (bf16[704,512]{1,0:T(8,128)(2,1)S(1)}, bf16[704,512]{1,0:T(8,128)(2,1)}, u32[]{:S(2)}, u32[]{:S(2)}) collective-permute-start(bf16[704,512]{1,0:T(8,128)(2,1)S(1)} %constant_dynamic-update-slice_fusion.refs_0_), channel_id=1, source_target_pairs={{0,16},{16,0},{32,48},{48,32},{64,80},{80,64},{96,112},{112,96},{1... | collective-permute-start | bytes 2162696 | tf_op jit(solution)/shard_map/ppermute | solution.py:239
  75.4 2.4 %collective-permute-start.7 = (bf16[704,512]{1,0:T(8,128)(2,1)S(1)}, bf16[704,512]{1,0:T(8,128)(2,1)}, u32[]{:S(2)}, u32[]{:S(2)}) collective-permute-start(bf16[704,512]{1,0:T(8,128)(2,1)S(1)} %collective-permute-done.3.refs_1_), channel_id=1, source_target_pairs={{0,16},{16,0},{32,48},{48,32},{64,80},{80,64},{96,112},{112,96},{1... | collective-permute-start | bytes 2162696 | tf_op jit(solution)/shard_map/ppermute | solution.py:239
  77.9 0.0 collective-permute-done.5.refs_3_
  77.9 1.9 %collective-permute-start.9 = (bf16[704,512]{1,0:T(8,128)(2,1)S(1)}, bf16[704,512]{1,0:T(8,128)(2,1)}, u32[]{:S(2)}, u32[]{:S(2)}) collective-permute-start(bf16[704,512]{1,0:T(8,128)(2,1)S(1)} %collective-permute-done.5.refs_3_), channel_id=1, source_target_pairs={{0,16},{16,0},{32,48},{48,32},{64,80},{80,64},{96,112},{112,96},{1... | collective-permute-start | bytes 2162696 | tf_op jit(solution)/shard_map/ppermute | solution.py:239
  79.8 4.1 %collective-permute-done.4.refs_2_ = bf16[704,512]{1,0:T(8,128)(2,1)S(1)} collective-permute-done((bf16[704,512]{1,0:T(8,128)(2,1)S(1)}, bf16[704,512]{1,0:T(8,128)(2,1)S(1)}, u32[]{:S(2)}, u32[]{:S(2)}) %collective-permute-start.4) | collective-permute-done | bytes 720928 | tf_op jit(solution)/shard_map/ppermute | solution.py:239
  83.9 1.9 %collective-permute-start.8 = (bf16[704,512]{1,0:T(8,128)(2,1)S(1)}, bf16[704,512]{1,0:T(8,128)(2,1)}, u32[]{:S(2)}, u32[]{:S(2)}) collective-permute-start(bf16[704,512]{1,0:T(8,128)(2,1)S(1)} %collective-permute-done.4.refs_2_), channel_id=1, source_target_pairs={{0,16},{16,0},{32,48},{48,32},{64,80},{80,64},{96,112},{112,96},{1... | collective-permute-start | bytes 2162696 | tf_op jit(solution)/shard_map/ppermute | solution.py:239
  86.4 15.8 %all-to-all-done.refs_1_.refs_2_.refs_3_ = bf16[16,472,256]{2,1,0:T(8,128)(2,1)} async-done(((bf16[16,472,256]{2,1,0:T(8,128)(2,1)}), bf16[16,472,256]{2,1,0:T(8,128)(2,1)}, u32[]{:S(2)}, u32[]{:S(2)}) %all-to-all-start) | async-done | bytes 3866656 | tf_op jit(solution)/shard_map/all_to_all | solution.py:235
  102.2 1.2 slice.4.rows_ref.refs_4_
  103.4 0.0 collective-permute-done.6.refs_4_
  103.4 0.0 collective-permute-done.7.refs_5_
  103.4 0.0 collective-permute-done.9.refs_7_
  103.4 0.0 collective-permute-done.8.refs_6_
  103.4 3.0 %ref_project.1 = (bf16[64,512]{1,0:T(8,128)(2,1)S(1)}, bf16[256,256]{1,0:T(8,128)(2,1)S(1)}) custom-call(bf16[16,88,256]{2,1,0:T(8,128)(2,1)S(1)} %slice.4.rows_ref.refs_4_, bf16[704,512]{1,0:T(8,128)(2,1)S(1)} %constant_dynamic-update-slice_fusion.refs_0_, bf16[704,512]{1,0:T(8,128)(2,1)S(1)} %collective-permute-done.3.refs_1_, ...), custom_call_target="tpu_custom_call" | custom-call | flops 1024 | bytes 1024 | tf_op jit(solution)/shard_map/ref_project/pallas_call | solution.py:129
  106.4 19.1 %attend.1 = bf16[16,128,256]{2,1,0:T(8,128)(2,1)S(1)} custom-call(s32[1]{0:T(128)S(6)} %copy.12.refs_0_, bf16[16,472,256]{2,1,0:T(8,128)(2,1)} %all-to-all-done.refs_1_.refs_2_.refs_3_, bf16[16,472,256]{2,1,0:T(8,128)(2,1)} %all-to-all-done.refs_1_.refs_2_.refs_3_, bf16[16,472,256]{2,1,0:T(8,128)(2,1)} %all-to-all-done.refs_1_.refs_2_.refs_3_, ...), custom_call_target="tpu_custom_call" | custom-call | flops 1024 | bytes 1024 | tf_op jit(solution)/shard_map/attend/pallas_call | solution.py:185
  125.5 36.4 %all_to_all.10.r_ref = bf16[16,128,256]{2,1,0:T(8,128)(2,1)S(1)} all-to-all(bf16[16,128,256]{2,1,0:T(8,128)(2,1)S(1)} %attend.1), channel_id=1, replica_groups=mesh['fsdp'=32,'seq'=16] {'seq'}, dimensions={0} | all-to-all | bytes 2097152 | tf_op jit(solution)/shard_map/all_to_all | solution.py:235
  161.9 1.1 unpack.1
  (7 shorter events, 0.1 us)
Async XLA Ops:
  4.5 9.5 %copy-start = (bf16[160,2,256]{2,1,0:T(2,128)(2,1)S(1)}, bf16[160,2,256]{2,1,0:T(2,128)(2,1)}, u32[]{:S(2)}) copy-start(bf16[160,2,256]{2,1,0:T(2,128)(2,1)} %param.8) | copy-start | bytes 491524
  4.5 9.6 %copy-start.1 = (bf16[8,256]{1,0:T(8,128)(2,1)S(1)}, bf16[8,256]{1,0:T(8,128)(2,1)}, u32[]{:S(2)}) copy-start(bf16[8,256]{1,0:T(8,128)(2,1)} %param.9) | copy-start | bytes 12292
  4.5 97.7 %all-to-all-start = ((bf16[16,472,256]{2,1,0:T(8,128)(2,1)}), bf16[16,472,256]{2,1,0:T(8,128)(2,1)}, u32[]{:S(2)}, u32[]{:S(2)}) async-start(bf16[16,472,256]{2,1,0:T(8,128)(2,1)} %pack.1), calls=%async_computation | async-start | bytes 7733248 | tf_op jit(solution)/shard_map/all_to_all | solution.py:235
  14.1 36.3 %collective-permute-start = (bf16[176,512]{1,0:T(8,128)(2,1)S(1)}, bf16[176,512]{1,0:T(8,128)(2,1)S(1)}, u32[]{:S(2)}, u32[]{:S(2)}) collective-permute-start(bf16[176,512]{1,0:T(8,128)(2,1)S(1)} %pad_maximum_fusion), channel_id=1, source_target_pairs={{0,128},{16,400},{32,160},{48,432},{64,192},{80,464},{96,224},{112... | collective-permute-start | bytes 540680 | tf_op jit(solution)/shard_map/ppermute | solution.py:239
  20.2 31.5 %collective-permute-start.1 = (bf16[176,512]{1,0:T(8,128)(2,1)S(1)}, bf16[176,512]{1,0:T(8,128)(2,1)S(1)}, u32[]{:S(2)}, u32[]{:S(2)}) collective-permute-start(bf16[176,512]{1,0:T(8,128)(2,1)S(1)} %pad_maximum_fusion), channel_id=1, source_target_pairs={{0,256},{16,272},{32,288},{48,304},{64,320},{80,336},{96,352},{112... | collective-permute-start | bytes 540680 | tf_op jit(solution)/shard_map/ppermute | solution.py:239
  28.5 23.3 %collective-permute-start.2 = (bf16[176,512]{1,0:T(8,128)(2,1)S(1)}, bf16[176,512]{1,0:T(8,128)(2,1)S(1)}, u32[]{:S(2)}, u32[]{:S(2)}) collective-permute-start(bf16[176,512]{1,0:T(8,128)(2,1)S(1)} %pad_maximum_fusion), channel_id=1, source_target_pairs={{0,384},{16,144},{32,416},{48,176},{64,448},{80,208},{96,480},{112... | collective-permute-start | bytes 540680 | tf_op jit(solution)/shard_map/ppermute | solution.py:239
  51.8 18.9 %collective-permute-start.3 = (bf16[704,512]{1,0:T(8,128)(2,1)S(1)}, bf16[704,512]{1,0:T(8,128)(2,1)S(1)}, u32[]{:S(2)}, u32[]{:S(2)}) collective-permute-start(bf16[704,512]{1,0:T(8,128)(2,1)S(1)} %constant_dynamic-update-slice_fusion.refs_0_), channel_id=1, source_target_pairs={{0,32},{16,112},{32,64},{48,16},{64,96},{80,48},{96,0},{112,80},{1... | collective-permute-start | bytes 2162696 | tf_op jit(solution)/shard_map/ppermute | solution.py:239
  54.9 22.9 %collective-permute-start.5 = (bf16[704,512]{1,0:T(8,128)(2,1)S(1)}, bf16[704,512]{1,0:T(8,128)(2,1)S(1)}, u32[]{:S(2)}, u32[]{:S(2)}) collective-permute-start(bf16[704,512]{1,0:T(8,128)(2,1)S(1)} %constant_dynamic-update-slice_fusion.refs_0_), channel_id=1, source_target_pairs={{0,96},{16,48},{32,0},{48,80},{64,32},{80,112},{96,64},{112,16},{1... | collective-permute-start | bytes 2162696 | tf_op jit(solution)/shard_map/ppermute | solution.py:239
  70.7 13.2 %collective-permute-start.4 = (bf16[704,512]{1,0:T(8,128)(2,1)S(1)}, bf16[704,512]{1,0:T(8,128)(2,1)S(1)}, u32[]{:S(2)}, u32[]{:S(2)}) collective-permute-start(bf16[704,512]{1,0:T(8,128)(2,1)S(1)} %collective-permute-done.3.refs_1_), channel_id=1, source_target_pairs={{0,32},{16,112},{32,64},{48,16},{64,96},{80,48},{96,0},{112,80},{1... | collective-permute-start | bytes 2162696 | tf_op jit(solution)/shard_map/ppermute | solution.py:239
  73.5 29.9 %collective-permute-start.6 = (bf16[704,512]{1,0:T(8,128)(2,1)S(1)}, bf16[704,512]{1,0:T(8,128)(2,1)}, u32[]{:S(2)}, u32[]{:S(2)}) collective-permute-start(bf16[704,512]{1,0:T(8,128)(2,1)S(1)} %constant_dynamic-update-slice_fusion.refs_0_), channel_id=1, source_target_pairs={{0,16},{16,0},{32,48},{48,32},{64,80},{80,64},{96,112},{112,96},{1... | collective-permute-start | bytes 2162696 | tf_op jit(solution)/shard_map/ppermute | solution.py:239
  75.4 28.0 %collective-permute-start.7 = (bf16[704,512]{1,0:T(8,128)(2,1)S(1)}, bf16[704,512]{1,0:T(8,128)(2,1)}, u32[]{:S(2)}, u32[]{:S(2)}) collective-permute-start(bf16[704,512]{1,0:T(8,128)(2,1)S(1)} %collective-permute-done.3.refs_1_), channel_id=1, source_target_pairs={{0,16},{16,0},{32,48},{48,32},{64,80},{80,64},{96,112},{112,96},{1... | collective-permute-start | bytes 2162696 | tf_op jit(solution)/shard_map/ppermute | solution.py:239
  77.9 25.5 %collective-permute-start.9 = (bf16[704,512]{1,0:T(8,128)(2,1)S(1)}, bf16[704,512]{1,0:T(8,128)(2,1)}, u32[]{:S(2)}, u32[]{:S(2)}) collective-permute-start(bf16[704,512]{1,0:T(8,128)(2,1)S(1)} %collective-permute-done.5.refs_3_), channel_id=1, source_target_pairs={{0,16},{16,0},{32,48},{48,32},{64,80},{80,64},{96,112},{112,96},{1... | collective-permute-start | bytes 2162696 | tf_op jit(solution)/shard_map/ppermute | solution.py:239
  83.9 19.6 %collective-permute-start.8 = (bf16[704,512]{1,0:T(8,128)(2,1)S(1)}, bf16[704,512]{1,0:T(8,128)(2,1)}, u32[]{:S(2)}, u32[]{:S(2)}) collective-permute-start(bf16[704,512]{1,0:T(8,128)(2,1)S(1)} %collective-permute-done.4.refs_2_), channel_id=1, source_target_pairs={{0,16},{16,0},{32,48},{48,32},{64,80},{80,64},{96,112},{112,96},{1... | collective-permute-start | bytes 2162696 | tf_op jit(solution)/shard_map/ppermute | solution.py:239

commit v5 on v4

--- a/solution.py
+++ b/solution.py
@@ -29,12 +29,25 @@
 X_AHEAD = fsdp_perm(lambda z, x, c: (z, x + direction(c), c))
 X_BEHIND = fsdp_perm(lambda z, x, c: (z, x - direction(c), c))
 CORE_SWAP = fsdp_perm(lambda z, x, c: (z, x, 1 - c))
-def pack_kernel(x_ref, rows_ref, ids_ref, o_ref, held, side32, side, in_sem, out_sem):
+def pack_kernel(x_ref, rows_hbm, ids_hbm, o_ref, held, rows_ref, ids_ref, side32, side, in_sem, out_sem):
     planes, tokens, _ = held.shape
     n = o_ref.shape[0]
     loads = [pltpu.make_async_copy(x_ref.at[k], held.at[k], in_sem.at[k]) for k in range(planes)]
+    loads.append(pltpu.make_async_copy(rows_hbm, rows_ref, in_sem.at[planes]))
+    loads.append(pltpu.make_async_copy(ids_hbm, ids_ref, in_sem.at[planes + 1]))
     for load in loads:
         load.start()
+    stores = []
+    for k in range(planes):
+        loads[k].wait()
+        for d in range(n):
+            part = held.at[k, :, pl.ds(d * 2 * HD, 2 * HD)]
+            rows = o_ref.at[d, pl.ds(k * tokens, tokens), :]
+            copy = pltpu.make_async_copy(part, rows, out_sem.at[len(stores)])
+            copy.start()
+            stores.append(copy)
+    loads[planes].wait()
+    loads[planes + 1].wait()
     x = rows_ref[...].astype(jnp.float32)
     mean = jnp.mean(x, axis=-1, keepdims=True)
     centered = x - mean
@@ -48,15 +61,6 @@
     side32[chunks * r :, 0:tokens] = ids
     side32[chunks * r :, tokens:] = ids
     side[...] = side32[...].astype(jnp.bfloat16)
-    stores = []
-    for k in range(planes):
-        loads[k].wait()
-        for d in range(n):
-            part = held.at[k, :, pl.ds(d * 2 * HD, 2 * HD)]
-            rows = o_ref.at[d, pl.ds(k * tokens, tokens), :]
-            copy = pltpu.make_async_copy(part, rows, out_sem.at[len(stores)])
-            copy.start()
-            stores.append(copy)
     for d in range(n):
         rows = o_ref.at[d, pl.ds(planes * tokens, side.shape[0]), :]
         copy = pltpu.make_async_copy(side, rows, out_sem.at[len(stores)])
@@ -73,17 +77,15 @@
     return pl.pallas_call(
         pack_kernel,
         out_shape=jax.ShapeDtypeStruct((n, planes * tokens + extra, 2 * HD), jnp.bfloat16),
-        in_specs=[
-            pl.BlockSpec(memory_space=pl.ANY),
-            pl.BlockSpec(memory_space=pltpu.VMEM),
-            pl.BlockSpec(memory_space=pltpu.VMEM),
-        ],
+        in_specs=[pl.BlockSpec(memory_space=pl.ANY)] * 3,
         out_specs=pl.BlockSpec(memory_space=pl.ANY),
         scratch_shapes=[
             pltpu.VMEM(video.shape, jnp.bfloat16),
+            pltpu.VMEM(rows.shape, jnp.bfloat16),
+            pltpu.VMEM(ids.shape, jnp.int32),
             pltpu.VMEM((extra, 2 * HD), jnp.float32),
             pltpu.VMEM((extra, 2 * HD), jnp.bfloat16),
-            pltpu.SemaphoreType.DMA((planes,)),
+            pltpu.SemaphoreType.DMA((planes + 2,)),
             pltpu.SemaphoreType.DMA(((planes + 1) * n,)),
         ],
         cost_estimate=pl.CostEstimate(flops=0, bytes_accessed=6 << 20, transcendentals=0),
@@ -91,12 +93,18 @@
     )(video, rows, ids)
 
 
-def ref_kernel(rows_ref, *refs):
-    pieces = refs[:8]
-    kv_ref, book_ref, x, split, codes = refs[8:]
+def ref_kernel(block_ref, *refs):
+    kv_ref, book_ref, rows_ref, held, x, split, codes, sem, piece_sem = refs[8:]
+    extra = rows_ref.shape[1]
+    load = pltpu.make_async_copy(block_ref.at[:, pl.ds(block_ref.shape[1] - extra, extra), :], rows_ref, sem)
+    load.start()
+    fetches = [pltpu.make_async_copy(refs[p], held.at[p], piece_sem.at[p]) for p in range(8)]
+    for fetch in fetches:
+        fetch.start()
     me = lax.axis_index("fsdp")
     mz, mx, mc = me // 8, me // 2 % 4, me % 2
     kdim = split.shape[2]
+    load.wait()
     n, chunk = rows_ref.shape[0], rows_ref.shape[2]
     r = x.shape[0] // n
     for d in range(n):
@@ -107,6 +115,7 @@
         split[f] = x[:, f * kdim : (f + 1) * kdim].astype(jnp.bfloat16)
     total = jnp.zeros(kv_ref.shape, jnp.float32)
     for p in range(8):
+        fetches[p].wait()
         core = mc if p < 4 else 1 - mc
         sign = 1 - 2 * core
         kx = p % 4
@@ -114,35 +123,40 @@
             f = (mz - sign * kz + 4) % 4 * 8 + (mx - sign * kx + 4) % 4 * 2 + core
             row = kz * WROWS
             total = total + jnp.dot(
-                split[f], pieces[p][row : row + kdim, :], preferred_element_type=jnp.float32
+                split[f], held[p, row : row + kdim, :], preferred_element_type=jnp.float32
             )
-            codes[pl.ds(pl.multiple_of(f * 8, 8), 8), :] = pieces[p][row + kdim : row + WROWS, 0 : 2 * HD].astype(
+            codes[pl.ds(pl.multiple_of(f * 8, 8), 8), :] = held[p, row + kdim : row + WROWS, 0 : 2 * HD].astype(
                 jnp.float32
             )[0:8]
     kv_ref[...] = total.astype(jnp.bfloat16)
     book_ref[...] = codes[...].astype(jnp.bfloat16)
 
 
-def ref_project(rows, pieces, kdim, depth):
+def ref_project(block, pieces, kdim, r, depth):
     n = pieces[0].shape[1]
-    slots = rows.shape[0] * (rows.shape[1] - SIDE) * rows.shape[2] // depth
+    slots = block.shape[0] * r
+    extra = r * depth // block.shape[2] + SIDE
     return pl.pallas_call(
         ref_kernel,
         out_shape=(
             jax.ShapeDtypeStruct((slots, n), jnp.bfloat16),
             jax.ShapeDtypeStruct((256, 2 * HD), jnp.bfloat16),
         ),
-        in_specs=[pl.BlockSpec(memory_space=pltpu.VMEM)] * 9,
+        in_specs=[pl.BlockSpec(memory_space=pl.ANY)] * 9,
         out_specs=(pl.BlockSpec(memory_space=pltpu.VMEM), pl.BlockSpec(memory_space=pltpu.VMEM)),
         scratch_shapes=[
+            pltpu.VMEM((block.shape[0], extra, block.shape[2]), jnp.bfloat16),
+            pltpu.VMEM((8,) + pieces[0].shape, jnp.bfloat16),
             pltpu.VMEM((slots, depth), jnp.float32),
             pltpu.VMEM((32, slots, kdim), jnp.bfloat16),
             pltpu.VMEM((256, 2 * HD), jnp.float32),
+            pltpu.SemaphoreType.DMA,
+            pltpu.SemaphoreType.DMA((8,)),
         ],
-        compiler_params=pltpu.CompilerParams(vmem_limit_bytes=16 << 20),
+        compiler_params=pltpu.CompilerParams(vmem_limit_bytes=60 << 20),
         cost_estimate=pl.CostEstimate(flops=1 << 10, bytes_accessed=1 << 10, transcendentals=0),
         name="ref_project",
-    )(rows, *pieces)
+    )(block, *pieces)
 
 
 def attend_kernel(tokens, sub, count_ref, q_ref, k_ref, v_ref, ids_ref, book_ref, rk_ref, rv_ref, o_ref):
@@ -178,9 +192,9 @@
         o_ref[b * sub : (b + 1) * sub] = out.astype(jnp.bfloat16).reshape(sub, tokens, HD)
 
 
-def attend(tokens, block, rows, count, book, ref_kv):
+def attend(tokens, block, count, book, ref_kv):
     n = block.shape[0]
-    per, sub = 8, 4
+    per, sub = 16, 8
     slots = ref_kv.shape[0]
     return pl.pallas_call(
         lambda *refs: attend_kernel(tokens, sub, *refs),
@@ -191,7 +205,7 @@
                 pl.BlockSpec((per, tokens, HD), lambda h, i, c: (i, 0, h)),
                 pl.BlockSpec((n, tokens, HD), lambda h, i, c: (0, 1, h)),
                 pl.BlockSpec((n, tokens, HD), lambda h, i, c: (0, 2, h)),
-                pl.BlockSpec((per, SIDE, HD), lambda h, i, c: (i, rows.shape[1] // SIDE - 1, 0)),
+                pl.BlockSpec((per, SIDE, HD), lambda h, i, c: (i, block.shape[1] // SIDE - 1, 0)),
                 pl.BlockSpec((book.shape[0], HD), lambda h, i, c: (0, h)),
                 pl.BlockSpec((slots, HD), lambda h, i, c: (0, h)),
                 pl.BlockSpec((slots, HD), lambda h, i, c: (0, 2 + h)),
@@ -199,10 +213,10 @@
             out_specs=pl.BlockSpec((per, tokens, HD), lambda h, i, c: (i, 0, h)),
         ),
         out_shape=jax.ShapeDtypeStruct((n, tokens, 2 * HD), jnp.bfloat16),
-        compiler_params=pltpu.CompilerParams(vmem_limit_bytes=24 << 20),
+        compiler_params=pltpu.CompilerParams(vmem_limit_bytes=32 << 20),
         cost_estimate=pl.CostEstimate(flops=1 << 10, bytes_accessed=1 << 10, transcendentals=0),
         name="attend",
-    )(count, block, block, block, rows, book, ref_kv, ref_kv)
+    )(count, block, block, block, block, book, ref_kv, ref_kv)
 
 
 def unpack_kernel(r_ref, o_ref, sem):
@@ -244,7 +258,6 @@
 
 
 def shards(video_qkv, reference_rows, kv_weight, pose_table, pose_ids, frame_counts):
-    planes_rows = 3 * video_qkv.shape[1]
     tokens = video_qkv.shape[1]
     depth = kv_weight.shape[0]
     video = exchange(pack(jnp.transpose(video_qkv[0], (1, 0, 2)), reference_rows[0], pose_ids))
@@ -255,9 +268,8 @@
     far = move(ahead, X_AHEAD)
     own = [column, ahead, far, behind]
     pieces = own + [move(piece, CORE_SWAP) for piece in own]
-    rows = video[:, planes_rows:, :]
-    ref_kv, book = ref_project(rows, pieces, depth, reference_rows.shape[2])
-    return unpack(exchange(attend(tokens, video, rows, frame_counts, book, ref_kv)))[None]
+    ref_kv, book = ref_project(video, pieces, depth, *reference_rows.shape[1:])
+    return unpack(exchange(attend(tokens, video, frame_counts, book, ref_kv)))[None]
 
 
 def solution(mesh):

time: 164 us -> 164 us (level)
  the two profiles are of different devices: /device:TPU:12 before, /device:TPU:14 now
where the time goes in v5:
time: 164 us; the launch traced here: 163 us
  waiting for transfers between devices  49.2 us (30%)
  starting transfers between devices  45.5 us (28%)
  blocking collectives  36.4 us (22%)
  Pallas kernels  27.2 us (17%)
  local copies, waits for them, and re-layouts  3.79 us (2%)
    ppermute x10, waiting for transfers between devices, move(): return lax.ppermute(block, 'fsdp', pairs)  36.5 us
    all_to_all x1, blocking collectives, exchange(): return lax.all_to_all(x, 'seq', 0, 0, tiled=True)  36.4 us
    ppermute x10, starting transfers between devices, move(): return lax.ppermute(block, 'fsdp', pairs)  36 us
    pallas_call x1, Pallas kernels, attend(): pl.pallas_call(lambda *refs: attend_kernel(tokens, sub, *refs), grid_spec...  17.6 us
    all_to_all x1, waiting for transfers between devices, exchange(): return lax.all_to_all(x, 'seq', 0, 0, tiled=True)  12.8 us
    all_to_all x1, starting transfers between devices, exchange(): return lax.all_to_all(x, 'seq', 0, 0, tiled=True)  9.51 us
    pallas_call x1, Pallas kernels, ref_project(): pl.pallas_call(ref_kernel, out_shape=(jax.ShapeDtypeStruct((slots, n), jn...  4.88 us
    unnamed x26, local copies, waits for them, and re-layouts  3.77 us
  transfers between devices with their start and end apart: 11, of which 5 were waited for; matrix products, arithmetic and copies ran while one was open for 0% of the time, Pallas kernels for 0%

profile of v5, /device:TPU:14, one launch (start us, length us, event | category | flops | bytes accessed | tf_op | source)
XLA Modules:
  0.0 163.1 jit_solution(7870905441357575637)
XLA Ops:
  0.0 3.7 %pack.1 = bf16[16,472,256]{2,1,0:T(8,128)(2,1)} custom-call(bf16[3,128,4096]{2,1,0:T(8,128)(2,1)} %bitcast.7, bf16[4,5120]{1,0:T(4,128)(2,1)} %bitcast.11, s32[1,128]{1,0:T(1,128)} %ids_hbm.1), custom_call_target="tpu_custom_call" | custom-call | bytes 6291456 | tf_op jit(solution)/shard_map/pack/pallas_call | solution.py:77
  3.7 0.0 copy-start.9
  3.7 0.0 copy-start.10
  3.7 9.5 %all-to-all-start = ((bf16[16,472,256]{2,1,0:T(8,128)(2,1)}), bf16[16,472,256]{2,1,0:T(8,128)(2,1)}, u32[]{:S(2)}, u32[]{:S(2)}) async-start(bf16[16,472,256]{2,1,0:T(8,128)(2,1)} %pack.1), calls=%async_computation | async-start | bytes 7733248 | tf_op jit(solution)/shard_map/all_to_all | solution.py:249
  13.3 0.0 copy-done.9
  13.3 0.0 copy-done.10
  13.4 6.1 %collective-permute-start = (bf16[176,512]{1,0:T(8,128)(2,1)S(1)}, bf16[176,512]{1,0:T(8,128)(2,1)S(1)}, u32[]{:S(2)}, u32[]{:S(2)}) collective-permute-start(bf16[176,512]{1,0:T(8,128)(2,1)S(1)} %pad_maximum_fusion), channel_id=1, source_target_pairs={{0,128},{16,400},{32,160},{48,432},{64,192},{80,464},{96,224},{112... | collective-permute-start | bytes 540680 | tf_op jit(solution)/shard_map/ppermute | solution.py:253
  19.5 8.2 %collective-permute-start.1 = (bf16[176,512]{1,0:T(8,128)(2,1)S(1)}, bf16[176,512]{1,0:T(8,128)(2,1)S(1)}, u32[]{:S(2)}, u32[]{:S(2)}) collective-permute-start(bf16[176,512]{1,0:T(8,128)(2,1)S(1)} %pad_maximum_fusion), channel_id=1, source_target_pairs={{0,256},{16,272},{32,288},{48,304},{64,320},{80,336},{96,352},{112... | collective-permute-start | bytes 540680 | tf_op jit(solution)/shard_map/ppermute | solution.py:253
  27.7 3.7 %collective-permute-start.2 = (bf16[176,512]{1,0:T(8,128)(2,1)S(1)}, bf16[176,512]{1,0:T(8,128)(2,1)S(1)}, u32[]{:S(2)}, u32[]{:S(2)}) collective-permute-start(bf16[176,512]{1,0:T(8,128)(2,1)S(1)} %pad_maximum_fusion), channel_id=1, source_target_pairs={{0,384},{16,144},{32,416},{48,176},{64,448},{80,208},{96,480},{112... | collective-permute-start | bytes 540680 | tf_op jit(solution)/shard_map/ppermute | solution.py:253
  31.4 18.3 %collective-permute-done = bf16[176,512]{1,0:T(8,128)(2,1)S(1)} collective-permute-done((bf16[176,512]{1,0:T(8,128)(2,1)S(1)}, bf16[176,512]{1,0:T(8,128)(2,1)S(1)}, u32[]{:S(2)}, u32[]{:S(2)}) %collective-permute-start) | collective-permute-done | bytes 180256 | tf_op jit(solution)/shard_map/ppermute | solution.py:253
  49.7 1.3 collective-permute-done.1
  51.0 0.0 collective-permute-done.2
  51.0 0.0 copy-start.2
  51.1 2.4 %collective-permute-start.3 = (bf16[704,512]{1,0:T(8,128)(2,1)S(1)}, bf16[704,512]{1,0:T(8,128)(2,1)S(1)}, u32[]{:S(2)}, u32[]{:S(2)}) collective-permute-start(bf16[704,512]{1,0:T(8,128)(2,1)S(1)} %constant_dynamic-update-slice_fusion.refs_0_), channel_id=1, source_target_pairs={{0,32},{16,112},{32,64},{48,16},{64,96},{80,48},{96,0},{112,80},{1... | collective-permute-start | bytes 2162696 | tf_op jit(solution)/shard_map/ppermute | solution.py:253
  53.5 3.4 %collective-permute-start.5 = (bf16[704,512]{1,0:T(8,128)(2,1)S(1)}, bf16[704,512]{1,0:T(8,128)(2,1)S(1)}, u32[]{:S(2)}, u32[]{:S(2)}) collective-permute-start(bf16[704,512]{1,0:T(8,128)(2,1)S(1)} %constant_dynamic-update-slice_fusion.refs_0_), channel_id=1, source_target_pairs={{0,96},{16,48},{32,0},{48,80},{64,32},{80,112},{96,64},{112,16},{1... | collective-permute-start | bytes 2162696 | tf_op jit(solution)/shard_map/ppermute | solution.py:253
  56.9 12.7 %collective-permute-done.3.refs_1_ = bf16[704,512]{1,0:T(8,128)(2,1)S(1)} collective-permute-done((bf16[704,512]{1,0:T(8,128)(2,1)S(1)}, bf16[704,512]{1,0:T(8,128)(2,1)S(1)}, u32[]{:S(2)}, u32[]{:S(2)}) %collective-permute-start.3) | collective-permute-done | bytes 720928 | tf_op jit(solution)/shard_map/ppermute | solution.py:253
  69.6 0.0 copy-start.3
  69.6 1.9 %collective-permute-start.4 = (bf16[704,512]{1,0:T(8,128)(2,1)S(1)}, bf16[704,512]{1,0:T(8,128)(2,1)S(1)}, u32[]{:S(2)}, u32[]{:S(2)}) collective-permute-start(bf16[704,512]{1,0:T(8,128)(2,1)S(1)} %collective-permute-done.3.refs_1_), channel_id=1, source_target_pairs={{0,32},{16,112},{32,64},{48,16},{64,96},{80,48},{96,0},{112,80},{1... | collective-permute-start | bytes 2162696 | tf_op jit(solution)/shard_map/ppermute | solution.py:253
  71.6 2.8 %collective-permute-start.6 = (bf16[704,512]{1,0:T(8,128)(2,1)S(1)}, bf16[704,512]{1,0:T(8,128)(2,1)S(1)}, u32[]{:S(2)}, u32[]{:S(2)}) collective-permute-start(bf16[704,512]{1,0:T(8,128)(2,1)S(1)} %constant_dynamic-update-slice_fusion.refs_0_), channel_id=1, source_target_pairs={{0,16},{16,0},{32,48},{48,32},{64,80},{80,64},{96,112},{112,96},{1... | collective-permute-start | bytes 2162696 | tf_op jit(solution)/shard_map/ppermute | solution.py:253
  74.3 1.9 %collective-permute-start.7 = (bf16[704,512]{1,0:T(8,128)(2,1)S(1)}, bf16[704,512]{1,0:T(8,128)(2,1)S(1)}, u32[]{:S(2)}, u32[]{:S(2)}) collective-permute-start(bf16[704,512]{1,0:T(8,128)(2,1)S(1)} %collective-permute-done.3.refs_1_), channel_id=1, source_target_pairs={{0,16},{16,0},{32,48},{48,32},{64,80},{80,64},{96,112},{112,96},{1... | collective-permute-start | bytes 2162696 | tf_op jit(solution)/shard_map/ppermute | solution.py:253
  76.3 0.0 collective-permute-done.5.refs_3_
  76.3 0.0 copy-start.4
  76.3 2.4 %collective-permute-start.9 = (bf16[704,512]{1,0:T(8,128)(2,1)S(1)}, bf16[704,512]{1,0:T(8,128)(2,1)S(1)}, u32[]{:S(2)}, u32[]{:S(2)}) collective-permute-start(bf16[704,512]{1,0:T(8,128)(2,1)S(1)} %collective-permute-done.5.refs_3_), channel_id=1, source_target_pairs={{0,16},{16,0},{32,48},{48,32},{64,80},{80,64},{96,112},{112,96},{1... | collective-permute-start | bytes 2162696 | tf_op jit(solution)/shard_map/ppermute | solution.py:253
  78.7 4.1 %collective-permute-done.4.refs_2_ = bf16[704,512]{1,0:T(8,128)(2,1)S(1)} collective-permute-done((bf16[704,512]{1,0:T(8,128)(2,1)S(1)}, bf16[704,512]{1,0:T(8,128)(2,1)S(1)}, u32[]{:S(2)}, u32[]{:S(2)}) %collective-permute-start.4) | collective-permute-done | bytes 720928 | tf_op jit(solution)/shard_map/ppermute | solution.py:253
  82.8 0.0 copy-start.5
  82.8 3.2 %collective-permute-start.8 = (bf16[704,512]{1,0:T(8,128)(2,1)S(1)}, bf16[704,512]{1,0:T(8,128)(2,1)}, u32[]{:S(2)}, u32[]{:S(2)}) collective-permute-start(bf16[704,512]{1,0:T(8,128)(2,1)S(1)} %collective-permute-done.4.refs_2_), channel_id=1, source_target_pairs={{0,16},{16,0},{32,48},{48,32},{64,80},{80,64},{96,112},{112,96},{1... | collective-permute-start | bytes 2162696 | tf_op jit(solution)/shard_map/ppermute | solution.py:253
  86.7 0.0 collective-permute-done.6.refs_4_
  86.7 0.0 copy-start.6
  86.7 0.0 collective-permute-done.7.refs_5_
  86.7 0.0 copy-start.7
  86.7 0.0 collective-permute-done.9.refs_7_
  86.7 0.9 copy-done.6
  87.6 0.2 copy-done.7
  87.8 0.0 copy-start.8
  87.8 0.9 copy-done.8
  88.7 0.0 collective-permute-done.8.refs_6_
  88.7 12.8 %all-to-all-done.block_ref.refs_1_.refs_2_.refs_3_.refs_4_ = bf16[16,472,256]{2,1,0:T(8,128)(2,1)} async-done(((bf16[16,472,256]{2,1,0:T(8,128)(2,1)}), bf16[16,472,256]{2,1,0:T(8,128)(2,1)}, u32[]{:S(2)}, u32[]{:S(2)}) %all-to-all-start) | async-done | bytes 3866656 | tf_op jit(solution)/shard_map/all_to_all | solution.py:249
  101.4 0.0 copy-done.2
  101.4 0.0 copy-done.3
  101.4 0.0 copy-done.4
  101.5 0.0 copy-done.5
  101.5 4.9 %ref_project.1 = (bf16[64,512]{1,0:T(8,128)(2,1)}, bf16[256,256]{1,0:T(8,128)(2,1)}) custom-call(bf16[16,472,256]{2,1,0:T(8,128)(2,1)} %all-to-all-done.block_ref.refs_1_.refs_2_.refs_3_.refs_4_, bf16[704,512]{1,0:T(8,128)(2,1)} %copy-done.2, bf16[704,512]{1,0:T(8,128)(2,1)} %copy-done.3, bf16[704,512]{1,0:T(8,128)(2,1)} %copy-done.5, ...), custom_call_target="tpu_custom_call" | custom-call | flops 1024 | bytes 1024 | tf_op jit(solution)/shard_map/ref_project/pallas_call | solution.py:139
  106.3 0.0 copy-start
  106.4 0.8 copy-done
  107.2 0.9 copy-done.1
  108.1 17.6 %attend.1 = bf16[16,128,256]{2,1,0:T(8,128)(2,1)S(1)} custom-call(s32[1]{0:T(128)S(6)} %copy.12.refs_0_, bf16[16,472,256]{2,1,0:T(8,128)(2,1)} %all-to-all-done.block_ref.refs_1_.refs_2_.refs_3_.refs_4_, bf16[16,472,256]{2,1,0:T(8,128)(2,1)} %all-to-all-done.block_ref.refs_1_.refs_2_.refs_3_.refs_4_, ...), custom_call_target="tpu_custom_call" | custom-call | flops 1024 | bytes 1024 | tf_op jit(solution)/shard_map/attend/pallas_call | solution.py:199
  125.7 36.4 %all_to_all.10.r_ref = bf16[16,128,256]{2,1,0:T(8,128)(2,1)S(1)} all-to-all(bf16[16,128,256]{2,1,0:T(8,128)(2,1)S(1)} %attend.1), channel_id=1, replica_groups=mesh['fsdp'=32,'seq'=16] {'seq'}, dimensions={0} | all-to-all | bytes 2097152 | tf_op jit(solution)/shard_map/all_to_all | solution.py:249
  162.0 1.1 unpack.1
  (8 shorter events, 0.1 us)
Async XLA Ops:
  3.7 9.5 %copy-start.9 = (bf16[160,2,256]{2,1,0:T(2,128)(2,1)S(1)}, bf16[160,2,256]{2,1,0:T(2,128)(2,1)}, u32[]{:S(2)}) copy-start(bf16[160,2,256]{2,1,0:T(2,128)(2,1)} %param.8) | copy-start | bytes 491524
  3.7 9.6 %copy-start.10 = (bf16[8,256]{1,0:T(8,128)(2,1)S(1)}, bf16[8,256]{1,0:T(8,128)(2,1)}, u32[]{:S(2)}) copy-start(bf16[8,256]{1,0:T(8,128)(2,1)} %param.9) | copy-start | bytes 12292
  3.7 97.7 %all-to-all-start = ((bf16[16,472,256]{2,1,0:T(8,128)(2,1)}), bf16[16,472,256]{2,1,0:T(8,128)(2,1)}, u32[]{:S(2)}, u32[]{:S(2)}) async-start(bf16[16,472,256]{2,1,0:T(8,128)(2,1)} %pack.1), calls=%async_computation | async-start | bytes 7733248 | tf_op jit(solution)/shard_map/all_to_all | solution.py:249
  13.4 36.3 %collective-permute-start = (bf16[176,512]{1,0:T(8,128)(2,1)S(1)}, bf16[176,512]{1,0:T(8,128)(2,1)S(1)}, u32[]{:S(2)}, u32[]{:S(2)}) collective-permute-start(bf16[176,512]{1,0:T(8,128)(2,1)S(1)} %pad_maximum_fusion), channel_id=1, source_target_pairs={{0,128},{16,400},{32,160},{48,432},{64,192},{80,464},{96,224},{112... | collective-permute-start | bytes 540680 | tf_op jit(solution)/shard_map/ppermute | solution.py:253
  19.5 31.5 %collective-permute-start.1 = (bf16[176,512]{1,0:T(8,128)(2,1)S(1)}, bf16[176,512]{1,0:T(8,128)(2,1)S(1)}, u32[]{:S(2)}, u32[]{:S(2)}) collective-permute-start(bf16[176,512]{1,0:T(8,128)(2,1)S(1)} %pad_maximum_fusion), channel_id=1, source_target_pairs={{0,256},{16,272},{32,288},{48,304},{64,320},{80,336},{96,352},{112... | collective-permute-start | bytes 540680 | tf_op jit(solution)/shard_map/ppermute | solution.py:253
  27.7 23.3 %collective-permute-start.2 = (bf16[176,512]{1,0:T(8,128)(2,1)S(1)}, bf16[176,512]{1,0:T(8,128)(2,1)S(1)}, u32[]{:S(2)}, u32[]{:S(2)}) collective-permute-start(bf16[176,512]{1,0:T(8,128)(2,1)S(1)} %pad_maximum_fusion), channel_id=1, source_target_pairs={{0,384},{16,144},{32,416},{48,176},{64,448},{80,208},{96,480},{112... | collective-permute-start | bytes 540680 | tf_op jit(solution)/shard_map/ppermute | solution.py:253
  51.0 50.4 %copy-start.2 = (bf16[704,512]{1,0:T(8,128)(2,1)}, bf16[704,512]{1,0:T(8,128)(2,1)S(1)}, u32[]{:S(2)}) copy-start(bf16[704,512]{1,0:T(8,128)(2,1)S(1)} %constant_dynamic-update-slice_fusion.refs_0_) | copy-start | bytes 2162692
  51.1 18.6 %collective-permute-start.3 = (bf16[704,512]{1,0:T(8,128)(2,1)S(1)}, bf16[704,512]{1,0:T(8,128)(2,1)S(1)}, u32[]{:S(2)}, u32[]{:S(2)}) collective-permute-start(bf16[704,512]{1,0:T(8,128)(2,1)S(1)} %constant_dynamic-update-slice_fusion.refs_0_), channel_id=1, source_target_pairs={{0,32},{16,112},{32,64},{48,16},{64,96},{80,48},{96,0},{112,80},{1... | collective-permute-start | bytes 2162696 | tf_op jit(solution)/shard_map/ppermute | solution.py:253
  53.5 22.8 %collective-permute-start.5 = (bf16[704,512]{1,0:T(8,128)(2,1)S(1)}, bf16[704,512]{1,0:T(8,128)(2,1)S(1)}, u32[]{:S(2)}, u32[]{:S(2)}) collective-permute-start(bf16[704,512]{1,0:T(8,128)(2,1)S(1)} %constant_dynamic-update-slice_fusion.refs_0_), channel_id=1, source_target_pairs={{0,96},{16,48},{32,0},{48,80},{64,32},{80,112},{96,64},{112,16},{1... | collective-permute-start | bytes 2162696 | tf_op jit(solution)/shard_map/ppermute | solution.py:253
  69.6 31.8 %copy-start.3 = (bf16[704,512]{1,0:T(8,128)(2,1)}, bf16[704,512]{1,0:T(8,128)(2,1)S(1)}, u32[]{:S(2)}) copy-start(bf16[704,512]{1,0:T(8,128)(2,1)S(1)} %collective-permute-done.3.refs_1_) | copy-start | bytes 2162692
  69.6 13.2 %collective-permute-start.4 = (bf16[704,512]{1,0:T(8,128)(2,1)S(1)}, bf16[704,512]{1,0:T(8,128)(2,1)S(1)}, u32[]{:S(2)}, u32[]{:S(2)}) collective-permute-start(bf16[704,512]{1,0:T(8,128)(2,1)S(1)} %collective-permute-done.3.refs_1_), channel_id=1, source_target_pairs={{0,32},{16,112},{32,64},{48,16},{64,96},{80,48},{96,0},{112,80},{1... | collective-permute-start | bytes 2162696 | tf_op jit(solution)/shard_map/ppermute | solution.py:253
  71.6 15.1 %collective-permute-start.6 = (bf16[704,512]{1,0:T(8,128)(2,1)S(1)}, bf16[704,512]{1,0:T(8,128)(2,1)S(1)}, u32[]{:S(2)}, u32[]{:S(2)}) collective-permute-start(bf16[704,512]{1,0:T(8,128)(2,1)S(1)} %constant_dynamic-update-slice_fusion.refs_0_), channel_id=1, source_target_pairs={{0,16},{16,0},{32,48},{48,32},{64,80},{80,64},{96,112},{112,96},{1... | collective-permute-start | bytes 2162696 | tf_op jit(solution)/shard_map/ppermute | solution.py:253
  74.3 12.4 %collective-permute-start.7 = (bf16[704,512]{1,0:T(8,128)(2,1)S(1)}, bf16[704,512]{1,0:T(8,128)(2,1)S(1)}, u32[]{:S(2)}, u32[]{:S(2)}) collective-permute-start(bf16[704,512]{1,0:T(8,128)(2,1)S(1)} %collective-permute-done.3.refs_1_), channel_id=1, source_target_pairs={{0,16},{16,0},{32,48},{48,32},{64,80},{80,64},{96,112},{112,96},{1... | collective-permute-start | bytes 2162696 | tf_op jit(solution)/shard_map/ppermute | solution.py:253
  76.3 25.2 %copy-start.4 = (bf16[704,512]{1,0:T(8,128)(2,1)}, bf16[704,512]{1,0:T(8,128)(2,1)S(1)}, u32[]{:S(2)}) copy-start(bf16[704,512]{1,0:T(8,128)(2,1)S(1)} %collective-permute-done.5.refs_3_) | copy-start | bytes 2162692
  76.3 10.4 %collective-permute-start.9 = (bf16[704,512]{1,0:T(8,128)(2,1)S(1)}, bf16[704,512]{1,0:T(8,128)(2,1)S(1)}, u32[]{:S(2)}, u32[]{:S(2)}) collective-permute-start(bf16[704,512]{1,0:T(8,128)(2,1)S(1)} %collective-permute-done.5.refs_3_), channel_id=1, source_target_pairs={{0,16},{16,0},{32,48},{48,32},{64,80},{80,64},{96,112},{112,96},{1... | collective-permute-start | bytes 2162696 | tf_op jit(solution)/shard_map/ppermute | solution.py:253
  82.8 18.6 %copy-start.5 = (bf16[704,512]{1,0:T(8,128)(2,1)}, bf16[704,512]{1,0:T(8,128)(2,1)S(1)}, u32[]{:S(2)}) copy-start(bf16[704,512]{1,0:T(8,128)(2,1)S(1)} %collective-permute-done.4.refs_2_) | copy-start | bytes 2162692
  82.8 5.9 %collective-permute-start.8 = (bf16[704,512]{1,0:T(8,128)(2,1)S(1)}, bf16[704,512]{1,0:T(8,128)(2,1)}, u32[]{:S(2)}, u32[]{:S(2)}) collective-permute-start(bf16[704,512]{1,0:T(8,128)(2,1)S(1)} %collective-permute-done.4.refs_2_), channel_id=1, source_target_pairs={{0,16},{16,0},{32,48},{48,32},{64,80},{80,64},{96,112},{112,96},{1... | collective-permute-start | bytes 2162696 | tf_op jit(solution)/shard_map/ppermute | solution.py:253
  86.7 0.9 copy-start.6
  86.7 1.1 copy-start.7
  87.8 0.9 copy-start.8
  106.3 0.8 copy-start
  107.2 0.9 copy-start.1

commit v6 on v5

--- a/solution.py
+++ b/solution.py
@@ -93,17 +93,63 @@
     )(video, rows, ids)
 
 
-def ref_kernel(block_ref, *refs):
-    kv_ref, book_ref, rows_ref, held, x, split, codes, sem, piece_sem = refs[8:]
+def assemble_kernel(*refs):
+    pieces = refs[:8]
+    weight_ref, book_ref, codes, sem = refs[8:]
+    me = lax.axis_index("fsdp")
+    mz, mx, mc = me // 8, me // 2 % 4, me % 2
+    kdim = weight_ref.shape[0] // 32
+    copies = []
+    for p in range(8):
+        core = mc if p < 4 else 1 - mc
+        sign = 1 - 2 * core
+        kx = p % 4
+        for kz in range(4):
+            f = (mz - sign * kz + 4) % 4 * 8 + (mx - sign * kx + 4) % 4 * 2 + core
+            row = kz * WROWS
+            copy = pltpu.make_async_copy(
+                pieces[p].at[pl.ds(row, kdim), :],
+                weight_ref.at[pl.ds(pl.multiple_of(f * kdim, 16), kdim), :],
+                sem.at[len(copies)],
+            )
+            copy.start()
+            copies.append(copy)
+            copy = pltpu.make_async_copy(
+                pieces[p].at[pl.ds(row + kdim, WROWS - kdim), pl.ds(0, 2 * HD)],
+                codes.at[pl.ds(pl.multiple_of(f * 16, 16), 16), :],
+                sem.at[len(copies)],
+            )
+            copy.start()
+            copies.append(copy)
+    for copy in copies:
+        copy.wait()
+    for f in range(32):
+        book_ref[f * 8 : (f + 1) * 8, :] = codes[f * 16 : f * 16 + 8, :]
+
+
+def assemble(pieces, kdim):
+    n = pieces[0].shape[1]
+    return pl.pallas_call(
+        assemble_kernel,
+        out_shape=(
+            jax.ShapeDtypeStruct((32 * kdim, n), jnp.bfloat16),
+            jax.ShapeDtypeStruct((256, 2 * HD), jnp.bfloat16),
+        ),
+        in_specs=[pl.BlockSpec(memory_space=pl.ANY)] * 8,
+        out_specs=(pl.BlockSpec(memory_space=pltpu.VMEM), pl.BlockSpec(memory_space=pltpu.VMEM)),
+        scratch_shapes=[pltpu.VMEM((32 * 16, 2 * HD), jnp.bfloat16), pltpu.SemaphoreType.DMA((64,))],
+        compiler_params=pltpu.CompilerParams(vmem_limit_bytes=8 << 20),
+        cost_estimate=pl.CostEstimate(flops=1 << 10, bytes_accessed=1 << 10, transcendentals=0),
+        name="assemble",
+    )(*pieces)
+
+
+def project_kernel(block_ref, weight_hbm, kv_ref, rows_ref, weight_ref, x, sem, weight_sem):
     extra = rows_ref.shape[1]
     load = pltpu.make_async_copy(block_ref.at[:, pl.ds(block_ref.shape[1] - extra, extra), :], rows_ref, sem)
     load.start()
-    fetches = [pltpu.make_async_copy(refs[p], held.at[p], piece_sem.at[p]) for p in range(8)]
-    for fetch in fetches:
-        fetch.start()
-    me = lax.axis_index("fsdp")
-    mz, mx, mc = me // 8, me // 2 % 4, me % 2
-    kdim = split.shape[2]
+    fetch = pltpu.make_async_copy(weight_hbm, weight_ref, weight_sem)
+    fetch.start()
     load.wait()
     n, chunk = rows_ref.shape[0], rows_ref.shape[2]
     r = x.shape[0] // n
@@ -111,52 +157,32 @@
         got = rows_ref[d].astype(jnp.float32)
         for c in range(x.shape[1] // chunk):
             x[d * r : (d + 1) * r, c * chunk : (c + 1) * chunk] = got[c * r : (c + 1) * r, :]
-    for f in range(32):
-        split[f] = x[:, f * kdim : (f + 1) * kdim].astype(jnp.bfloat16)
-    total = jnp.zeros(kv_ref.shape, jnp.float32)
-    for p in range(8):
-        fetches[p].wait()
-        core = mc if p < 4 else 1 - mc
-        sign = 1 - 2 * core
-        kx = p % 4
-        for kz in range(4):
-            f = (mz - sign * kz + 4) % 4 * 8 + (mx - sign * kx + 4) % 4 * 2 + core
-            row = kz * WROWS
-            total = total + jnp.dot(
-                split[f], held[p, row : row + kdim, :], preferred_element_type=jnp.float32
-            )
-            codes[pl.ds(pl.multiple_of(f * 8, 8), 8), :] = held[p, row + kdim : row + WROWS, 0 : 2 * HD].astype(
-                jnp.float32
-            )[0:8]
-    kv_ref[...] = total.astype(jnp.bfloat16)
-    book_ref[...] = codes[...].astype(jnp.bfloat16)
-
-
-def ref_project(block, pieces, kdim, r, depth):
-    n = pieces[0].shape[1]
+    fetch.wait()
+    kv_ref[...] = jnp.dot(
+        x[...].astype(jnp.bfloat16), weight_ref[...], preferred_element_type=jnp.float32
+    ).astype(jnp.bfloat16)
+
+
+def project(block, weight, r):
+    depth, n = weight.shape
     slots = block.shape[0] * r
     extra = r * depth // block.shape[2] + SIDE
     return pl.pallas_call(
-        ref_kernel,
-        out_shape=(
-            jax.ShapeDtypeStruct((slots, n), jnp.bfloat16),
-            jax.ShapeDtypeStruct((256, 2 * HD), jnp.bfloat16),
-        ),
-        in_specs=[pl.BlockSpec(memory_space=pl.ANY)] * 9,
-        out_specs=(pl.BlockSpec(memory_space=pltpu.VMEM), pl.BlockSpec(memory_space=pltpu.VMEM)),
+        project_kernel,
+        out_shape=jax.ShapeDtypeStruct((slots, n), jnp.bfloat16),
+        in_specs=[pl.BlockSpec(memory_space=pl.ANY)] * 2,
+        out_specs=pl.BlockSpec(memory_space=pltpu.VMEM),
         scratch_shapes=[
             pltpu.VMEM((block.shape[0], extra, block.shape[2]), jnp.bfloat16),
-            pltpu.VMEM((8,) + pieces[0].shape, jnp.bfloat16),
+            pltpu.VMEM(weight.shape, jnp.bfloat16),
             pltpu.VMEM((slots, depth), jnp.float32),
-            pltpu.VMEM((32, slots, kdim), jnp.bfloat16),
-            pltpu.VMEM((256, 2 * HD), jnp.float32),
             pltpu.SemaphoreType.DMA,
-            pltpu.SemaphoreType.DMA((8,)),
+            pltpu.SemaphoreType.DMA,
         ],
         compiler_params=pltpu.CompilerParams(vmem_limit_bytes=60 << 20),
         cost_estimate=pl.CostEstimate(flops=1 << 10, bytes_accessed=1 << 10, transcendentals=0),
-        name="ref_project",
-    )(block, *pieces)
+        name="project",
+    )(block, weight)
 
 
 def attend_kernel(tokens, sub, count_ref, q_ref, k_ref, v_ref, ids_ref, book_ref, rk_ref, rv_ref, o_ref):
@@ -268,7 +294,9 @@
     far = move(ahead, X_AHEAD)
     own = [column, ahead, far, behind]
     pieces = own + [move(piece, CORE_SWAP) for piece in own]
-    ref_kv, book = ref_project(video, pieces, depth, *reference_rows.shape[1:])
+    weight, book = assemble(pieces, depth)
+    video, weight = lax.optimization_barrier((video, weight))
+    ref_kv = project(video, weight, reference_rows.shape[1])
     return unpack(exchange(attend(tokens, video, frame_counts, book, ref_kv)))[None]
 
 

time: 164 us -> 165 us (level)
  the two profiles are of different devices: /device:TPU:14 before, /device:TPU:8 now
where the time goes in v6:
time: 165 us
  starting transfers between devices  48.6 us (29%)
  blocking collectives  39.9 us (24%)
  waiting for transfers between devices  37.1 us (22%)
  Pallas kernels  35.1 us (21%)
  local copies, waits for them, and re-layouts  3.21 us (2%)
    all_to_all x1, blocking collectives, exchange(): return lax.all_to_all(x, 'seq', 0, 0, tiled=True)  39.9 us
    ppermute x10, starting transfers between devices, move(): return lax.ppermute(block, 'fsdp', pairs)  38.4 us
    ppermute x10, waiting for transfers between devices, move(): return lax.ppermute(block, 'fsdp', pairs)  34.3 us
    pallas_call x1, Pallas kernels, attend(): pl.pallas_call(lambda *refs: attend_kernel(tokens, sub, *refs), grid_spec...  17.6 us
    all_to_all x1, starting transfers between devices, exchange(): return lax.all_to_all(x, 'seq', 0, 0, tiled=True)  10.2 us
    pallas_call x1, Pallas kernels, assemble(): pl.pallas_call(assemble_kernel, out_shape=(jax.ShapeDtypeStruct((32 * kdi...  8.29 us
    pallas_call x1, Pallas kernels, project(): pl.pallas_call(project_kernel, out_shape=jax.ShapeDtypeStruct((slots, n),...  4.39 us
    pallas_call x1, Pallas kernels, pack(): pl.pallas_call(pack_kernel, out_shape=jax.ShapeDtypeStruct((n, planes * t...  3.72 us
  transfers between devices with their start and end apart: 11, of which 6 were waited for; matrix products, arithmetic and copies ran while one was open for 0% of the time, Pallas kernels for 5%

profile of v6, /device:TPU:8, one launch (start us, length us, event | category | flops | bytes accessed | tf_op | source)
XLA Modules:
  0.0 164.8 jit_solution(2414630344309366566)
XLA Ops:
  0.0 3.7 %pack.1 = bf16[16,472,256]{2,1,0:T(8,128)(2,1)} custom-call(bf16[3,128,4096]{2,1,0:T(8,128)(2,1)} %bitcast.7, bf16[4,5120]{1,0:T(4,128)(2,1)} %bitcast.11, s32[1,128]{1,0:T(1,128)} %ids_hbm.1), custom_call_target="tpu_custom_call" | custom-call | bytes 6291456 | tf_op jit(solution)/shard_map/pack/pallas_call | solution.py:77
  3.7 0.0 copy-start.2
  3.7 0.0 copy-start.3
  3.7 10.2 %all-to-all-start = ((bf16[16,472,256]{2,1,0:T(8,128)(2,1)}), bf16[16,472,256]{2,1,0:T(8,128)(2,1)}, u32[]{:S(2)}, u32[]{:S(2)}) async-start(bf16[16,472,256]{2,1,0:T(8,128)(2,1)} %pack.1), calls=%async_computation | async-start | bytes 7733248 | tf_op jit(solution)/shard_map/all_to_all | solution.py:275
  14.0 0.0 copy-done.2
  14.0 0.0 copy-done.3
  14.1 5.4 %collective-permute-start = (bf16[176,512]{1,0:T(8,128)(2,1)S(1)}, bf16[176,512]{1,0:T(8,128)(2,1)S(1)}, u32[]{:S(2)}, u32[]{:S(2)}) collective-permute-start(bf16[176,512]{1,0:T(8,128)(2,1)S(1)} %pad_maximum_fusion), channel_id=1, source_target_pairs={{0,128},{16,400},{32,160},{48,432},{64,192},{80,464},{96,224},{112... | collective-permute-start | bytes 540680 | tf_op jit(solution)/shard_map/ppermute | solution.py:279
  19.5 8.2 %collective-permute-start.1 = (bf16[176,512]{1,0:T(8,128)(2,1)S(1)}, bf16[176,512]{1,0:T(8,128)(2,1)S(1)}, u32[]{:S(2)}, u32[]{:S(2)}) collective-permute-start(bf16[176,512]{1,0:T(8,128)(2,1)S(1)} %pad_maximum_fusion), channel_id=1, source_target_pairs={{0,256},{16,272},{32,288},{48,304},{64,320},{80,336},{96,352},{112... | collective-permute-start | bytes 540680 | tf_op jit(solution)/shard_map/ppermute | solution.py:279
  27.7 3.7 %collective-permute-start.2 = (bf16[176,512]{1,0:T(8,128)(2,1)S(1)}, bf16[176,512]{1,0:T(8,128)(2,1)S(1)}, u32[]{:S(2)}, u32[]{:S(2)}) collective-permute-start(bf16[176,512]{1,0:T(8,128)(2,1)S(1)} %pad_maximum_fusion), channel_id=1, source_target_pairs={{0,384},{16,144},{32,416},{48,176},{64,448},{80,208},{96,480},{112... | collective-permute-start | bytes 540680 | tf_op jit(solution)/shard_map/ppermute | solution.py:279
  31.4 18.3 %collective-permute-done = bf16[176,512]{1,0:T(8,128)(2,1)S(1)} collective-permute-done((bf16[176,512]{1,0:T(8,128)(2,1)S(1)}, bf16[176,512]{1,0:T(8,128)(2,1)S(1)}, u32[]{:S(2)}, u32[]{:S(2)}) %collective-permute-start) | collective-permute-done | bytes 180256 | tf_op jit(solution)/shard_map/ppermute | solution.py:279
  49.7 1.3 collective-permute-done.1
  51.0 0.0 collective-permute-done.2
  51.1 3.4 %collective-permute-start.3 = (bf16[704,512]{1,0:T(8,128)(2,1)S(1)}, bf16[704,512]{1,0:T(8,128)(2,1)S(1)}, u32[]{:S(2)}, u32[]{:S(2)}) collective-permute-start(bf16[704,512]{1,0:T(8,128)(2,1)S(1)} %constant_dynamic-update-slice_fusion.refs_0_), channel_id=1, source_target_pairs={{0,32},{16,112},{32,64},{48,16},{64,96},{80,48},{96,0},{112,80},{1... | collective-permute-start | bytes 2162696 | tf_op jit(solution)/shard_map/ppermute | solution.py:279
  54.4 3.7 %collective-permute-start.5 = (bf16[704,512]{1,0:T(8,128)(2,1)S(1)}, bf16[704,512]{1,0:T(8,128)(2,1)S(1)}, u32[]{:S(2)}, u32[]{:S(2)}) collective-permute-start(bf16[704,512]{1,0:T(8,128)(2,1)S(1)} %constant_dynamic-update-slice_fusion.refs_0_), channel_id=1, source_target_pairs={{0,96},{16,48},{32,0},{48,80},{64,32},{80,112},{96,64},{112,16},{1... | collective-permute-start | bytes 2162696 | tf_op jit(solution)/shard_map/ppermute | solution.py:279
  58.1 10.8 %collective-permute-done.3.refs_1_ = bf16[704,512]{1,0:T(8,128)(2,1)S(1)} collective-permute-done((bf16[704,512]{1,0:T(8,128)(2,1)S(1)}, bf16[704,512]{1,0:T(8,128)(2,1)S(1)}, u32[]{:S(2)}, u32[]{:S(2)}) %collective-permute-start.3) | collective-permute-done | bytes 720928 | tf_op jit(solution)/shard_map/ppermute | solution.py:279
  68.9 3.4 %collective-permute-start.4 = (bf16[704,512]{1,0:T(8,128)(2,1)S(1)}, bf16[704,512]{1,0:T(8,128)(2,1)S(1)}, u32[]{:S(2)}, u32[]{:S(2)}) collective-permute-start(bf16[704,512]{1,0:T(8,128)(2,1)S(1)} %collective-permute-done.3.refs_1_), channel_id=1, source_target_pairs={{0,32},{16,112},{32,64},{48,16},{64,96},{80,48},{96,0},{112,80},{1... | collective-permute-start | bytes 2162696 | tf_op jit(solution)/shard_map/ppermute | solution.py:279
  72.3 4.4 %collective-permute-start.6 = (bf16[704,512]{1,0:T(8,128)(2,1)S(1)}, bf16[704,512]{1,0:T(8,128)(2,1)S(1)}, u32[]{:S(2)}, u32[]{:S(2)}) collective-permute-start(bf16[704,512]{1,0:T(8,128)(2,1)S(1)} %constant_dynamic-update-slice_fusion.refs_0_), channel_id=1, source_target_pairs={{0,16},{16,0},{32,48},{48,32},{64,80},{80,64},{96,112},{112,96},{1... | collective-permute-start | bytes 2162696 | tf_op jit(solution)/shard_map/ppermute | solution.py:279
  76.8 1.9 %collective-permute-start.7 = (bf16[704,512]{1,0:T(8,128)(2,1)S(1)}, bf16[704,512]{1,0:T(8,128)(2,1)S(1)}, u32[]{:S(2)}, u32[]{:S(2)}) collective-permute-start(bf16[704,512]{1,0:T(8,128)(2,1)S(1)} %collective-permute-done.3.refs_1_), channel_id=1, source_target_pairs={{0,16},{16,0},{32,48},{48,32},{64,80},{80,64},{96,112},{112,96},{1... | collective-permute-start | bytes 2162696 | tf_op jit(solution)/shard_map/ppermute | solution.py:279
  78.7 0.0 collective-permute-done.5.refs_3_
  78.7 2.4 %collective-permute-start.9 = (bf16[704,512]{1,0:T(8,128)(2,1)S(1)}, bf16[704,512]{1,0:T(8,128)(2,1)S(1)}, u32[]{:S(2)}, u32[]{:S(2)}) collective-permute-start(bf16[704,512]{1,0:T(8,128)(2,1)S(1)} %collective-permute-done.5.refs_3_), channel_id=1, source_target_pairs={{0,16},{16,0},{32,48},{48,32},{64,80},{80,64},{96,112},{112,96},{1... | collective-permute-start | bytes 2162696 | tf_op jit(solution)/shard_map/ppermute | solution.py:279
  81.1 2.4 %collective-permute-done.4.refs_2_ = bf16[704,512]{1,0:T(8,128)(2,1)S(1)} collective-permute-done((bf16[704,512]{1,0:T(8,128)(2,1)S(1)}, bf16[704,512]{1,0:T(8,128)(2,1)S(1)}, u32[]{:S(2)}, u32[]{:S(2)}) %collective-permute-start.4) | collective-permute-done | bytes 720928 | tf_op jit(solution)/shard_map/ppermute | solution.py:279
  83.5 1.9 %collective-permute-start.8 = (bf16[704,512]{1,0:T(8,128)(2,1)S(1)}, bf16[704,512]{1,0:T(8,128)(2,1)S(1)}, u32[]{:S(2)}, u32[]{:S(2)}) collective-permute-start(bf16[704,512]{1,0:T(8,128)(2,1)S(1)} %collective-permute-done.4.refs_2_), channel_id=1, source_target_pairs={{0,16},{16,0},{32,48},{48,32},{64,80},{80,64},{96,112},{112,96},{1... | collective-permute-start | bytes 2162696 | tf_op jit(solution)/shard_map/ppermute | solution.py:279
  86.1 0.0 collective-permute-done.6.refs_4_
  86.1 0.0 collective-permute-done.7.refs_5_
  86.1 0.0 collective-permute-done.9.refs_7_
  86.1 1.5 collective-permute-done.8.refs_6_
  87.6 8.3 %assemble.1 = (bf16[5120,512]{1,0:T(8,128)(2,1)S(1)}, bf16[256,256]{1,0:T(8,128)(2,1)S(1)}) custom-call(bf16[704,512]{1,0:T(8,128)(2,1)S(1)} %constant_dynamic-update-slice_fusion.refs_0_, bf16[704,512]{1,0:T(8,128)(2,1)S(1)} %collective-permute-done.3.refs_1_, bf16[704,512]{1,0:T(8,128)(2,1)S(1)} %collective-permute-done.4.refs_2_, ...), custom_call_target="tpu_custom_call" | custom-call | flops 1024 | bytes 1024 | tf_op jit(solution)/shard_map/assemble/pallas_call | solution.py:132
  95.9 0.0 copy-start
  95.9 2.3 %copy-done = bf16[5120,512]{1,0:T(8,128)(2,1)} copy-done((bf16[5120,512]{1,0:T(8,128)(2,1)}, bf16[5120,512]{1,0:T(8,128)(2,1)S(1)}, u32[]{:S(2)}) %copy-start) | copy-done | bytes 5242904
  98.2 2.7 %all-to-all-done.block_ref.refs_1_.refs_2_.refs_3_.refs_4_ = bf16[16,472,256]{2,1,0:T(8,128)(2,1)} async-done(((bf16[16,472,256]{2,1,0:T(8,128)(2,1)}), bf16[16,472,256]{2,1,0:T(8,128)(2,1)}, u32[]{:S(2)}, u32[]{:S(2)}) %all-to-all-start) | async-done | bytes 3866656 | tf_op jit(solution)/shard_map/all_to_all | solution.py:275
  100.9 4.4 %project.1.refs_6_.refs_7_ = bf16[64,512]{1,0:T(8,128)(2,1)} custom-call(bf16[16,472,256]{2,1,0:T(8,128)(2,1)} %all-to-all-done.block_ref.refs_1_.refs_2_.refs_3_.refs_4_, bf16[5120,512]{1,0:T(8,128)(2,1)} %copy-done), custom_call_target="tpu_custom_call" | custom-call | flops 1024 | bytes 1024 | tf_op jit(solution)/shard_map/project/pallas_call | solution.py:170
  105.3 0.0 copy-start.1
  105.3 0.8 copy-done.1
  106.2 17.6 %attend.1 = bf16[16,128,256]{2,1,0:T(8,128)(2,1)S(1)} custom-call(s32[1]{0:T(128)S(6)} %copy.12.refs_0_, bf16[16,472,256]{2,1,0:T(8,128)(2,1)} %all-to-all-done.block_ref.refs_1_.refs_2_.refs_3_.refs_4_, bf16[16,472,256]{2,1,0:T(8,128)(2,1)} %all-to-all-done.block_ref.refs_1_.refs_2_.refs_3_.refs_4_, ...), custom_call_target="tpu_custom_call" | custom-call | flops 1024 | bytes 1024 | tf_op jit(solution)/shard_map/attend/pallas_call | solution.py:225
  123.7 39.9 %all_to_all.10.r_ref = bf16[16,128,256]{2,1,0:T(8,128)(2,1)S(1)} all-to-all(bf16[16,128,256]{2,1,0:T(8,128)(2,1)S(1)} %attend.1), channel_id=1, replica_groups=mesh['fsdp'=32,'seq'=16] {'seq'}, dimensions={0} | all-to-all | bytes 2097152 | tf_op jit(solution)/shard_map/all_to_all | solution.py:275
  163.7 1.1 unpack.1
  (7 shorter events, 0.1 us)
Async XLA Ops:
  3.7 10.3 %copy-start.2 = (bf16[160,2,256]{2,1,0:T(2,128)(2,1)S(1)}, bf16[160,2,256]{2,1,0:T(2,128)(2,1)}, u32[]{:S(2)}) copy-start(bf16[160,2,256]{2,1,0:T(2,128)(2,1)} %param.8) | copy-start | bytes 491524
  3.7 10.3 %copy-start.3 = (bf16[8,256]{1,0:T(8,128)(2,1)S(1)}, bf16[8,256]{1,0:T(8,128)(2,1)}, u32[]{:S(2)}) copy-start(bf16[8,256]{1,0:T(8,128)(2,1)} %param.9) | copy-start | bytes 12292
  3.7 97.2 %all-to-all-start = ((bf16[16,472,256]{2,1,0:T(8,128)(2,1)}), bf16[16,472,256]{2,1,0:T(8,128)(2,1)}, u32[]{:S(2)}, u32[]{:S(2)}) async-start(bf16[16,472,256]{2,1,0:T(8,128)(2,1)} %pack.1), calls=%async_computation | async-start | bytes 7733248 | tf_op jit(solution)/shard_map/all_to_all | solution.py:275
  14.1 35.6 %collective-permute-start = (bf16[176,512]{1,0:T(8,128)(2,1)S(1)}, bf16[176,512]{1,0:T(8,128)(2,1)S(1)}, u32[]{:S(2)}, u32[]{:S(2)}) collective-permute-start(bf16[176,512]{1,0:T(8,128)(2,1)S(1)} %pad_maximum_fusion), channel_id=1, source_target_pairs={{0,128},{16,400},{32,160},{48,432},{64,192},{80,464},{96,224},{112... | collective-permute-start | bytes 540680 | tf_op jit(solution)/shard_map/ppermute | solution.py:279
  19.5 31.5 %collective-permute-start.1 = (bf16[176,512]{1,0:T(8,128)(2,1)S(1)}, bf16[176,512]{1,0:T(8,128)(2,1)S(1)}, u32[]{:S(2)}, u32[]{:S(2)}) collective-permute-start(bf16[176,512]{1,0:T(8,128)(2,1)S(1)} %pad_maximum_fusion), channel_id=1, source_target_pairs={{0,256},{16,272},{32,288},{48,304},{64,320},{80,336},{96,352},{112... | collective-permute-start | bytes 540680 | tf_op jit(solution)/shard_map/ppermute | solution.py:279
  27.7 23.3 %collective-permute-start.2 = (bf16[176,512]{1,0:T(8,128)(2,1)S(1)}, bf16[176,512]{1,0:T(8,128)(2,1)S(1)}, u32[]{:S(2)}, u32[]{:S(2)}) collective-permute-start(bf16[176,512]{1,0:T(8,128)(2,1)S(1)} %pad_maximum_fusion), channel_id=1, source_target_pairs={{0,384},{16,144},{32,416},{48,176},{64,448},{80,208},{96,480},{112... | collective-permute-start | bytes 540680 | tf_op jit(solution)/shard_map/ppermute | solution.py:279
  51.1 17.9 %collective-permute-start.3 = (bf16[704,512]{1,0:T(8,128)(2,1)S(1)}, bf16[704,512]{1,0:T(8,128)(2,1)S(1)}, u32[]{:S(2)}, u32[]{:S(2)}) collective-permute-start(bf16[704,512]{1,0:T(8,128)(2,1)S(1)} %constant_dynamic-update-slice_fusion.refs_0_), channel_id=1, source_target_pairs={{0,32},{16,112},{32,64},{48,16},{64,96},{80,48},{96,0},{112,80},{1... | collective-permute-start | bytes 2162696 | tf_op jit(solution)/shard_map/ppermute | solution.py:279
  54.4 24.3 %collective-permute-start.5 = (bf16[704,512]{1,0:T(8,128)(2,1)S(1)}, bf16[704,512]{1,0:T(8,128)(2,1)S(1)}, u32[]{:S(2)}, u32[]{:S(2)}) collective-permute-start(bf16[704,512]{1,0:T(8,128)(2,1)S(1)} %constant_dynamic-update-slice_fusion.refs_0_), channel_id=1, source_target_pairs={{0,96},{16,48},{32,0},{48,80},{64,32},{80,112},{96,64},{112,16},{1... | collective-permute-start | bytes 2162696 | tf_op jit(solution)/shard_map/ppermute | solution.py:279
  68.9 14.6 %collective-permute-start.4 = (bf16[704,512]{1,0:T(8,128)(2,1)S(1)}, bf16[704,512]{1,0:T(8,128)(2,1)S(1)}, u32[]{:S(2)}, u32[]{:S(2)}) collective-permute-start(bf16[704,512]{1,0:T(8,128)(2,1)S(1)} %collective-permute-done.3.refs_1_), channel_id=1, source_target_pairs={{0,32},{16,112},{32,64},{48,16},{64,96},{80,48},{96,0},{112,80},{1... | collective-permute-start | bytes 2162696 | tf_op jit(solution)/shard_map/ppermute | solution.py:279
  72.3 13.8 %collective-permute-start.6 = (bf16[704,512]{1,0:T(8,128)(2,1)S(1)}, bf16[704,512]{1,0:T(8,128)(2,1)S(1)}, u32[]{:S(2)}, u32[]{:S(2)}) collective-permute-start(bf16[704,512]{1,0:T(8,128)(2,1)S(1)} %constant_dynamic-update-slice_fusion.refs_0_), channel_id=1, source_target_pairs={{0,16},{16,0},{32,48},{48,32},{64,80},{80,64},{96,112},{112,96},{1... | collective-permute-start | bytes 2162696 | tf_op jit(solution)/shard_map/ppermute | solution.py:279
  76.8 9.3 %collective-permute-start.7 = (bf16[704,512]{1,0:T(8,128)(2,1)S(1)}, bf16[704,512]{1,0:T(8,128)(2,1)S(1)}, u32[]{:S(2)}, u32[]{:S(2)}) collective-permute-start(bf16[704,512]{1,0:T(8,128)(2,1)S(1)} %collective-permute-done.3.refs_1_), channel_id=1, source_target_pairs={{0,16},{16,0},{32,48},{48,32},{64,80},{80,64},{96,112},{112,96},{1... | collective-permute-start | bytes 2162696 | tf_op jit(solution)/shard_map/ppermute | solution.py:279
  78.7 7.4 %collective-permute-start.9 = (bf16[704,512]{1,0:T(8,128)(2,1)S(1)}, bf16[704,512]{1,0:T(8,128)(2,1)S(1)}, u32[]{:S(2)}, u32[]{:S(2)}) collective-permute-start(bf16[704,512]{1,0:T(8,128)(2,1)S(1)} %collective-permute-done.5.refs_3_), channel_id=1, source_target_pairs={{0,16},{16,0},{32,48},{48,32},{64,80},{80,64},{96,112},{112,96},{1... | collective-permute-start | bytes 2162696 | tf_op jit(solution)/shard_map/ppermute | solution.py:279
  83.5 4.1 %collective-permute-start.8 = (bf16[704,512]{1,0:T(8,128)(2,1)S(1)}, bf16[704,512]{1,0:T(8,128)(2,1)S(1)}, u32[]{:S(2)}, u32[]{:S(2)}) collective-permute-start(bf16[704,512]{1,0:T(8,128)(2,1)S(1)} %collective-permute-done.4.refs_2_), channel_id=1, source_target_pairs={{0,16},{16,0},{32,48},{48,32},{64,80},{80,64},{96,112},{112,96},{1... | collective-permute-start | bytes 2162696 | tf_op jit(solution)/shard_map/ppermute | solution.py:279
  95.9 2.3 %copy-start = (bf16[5120,512]{1,0:T(8,128)(2,1)}, bf16[5120,512]{1,0:T(8,128)(2,1)S(1)}, u32[]{:S(2)}) copy-start(bf16[5120,512]{1,0:T(8,128)(2,1)S(1)} %get-tuple-element.12.weight_hbm) | copy-start | bytes 15728644
  105.3 0.8 copy-start.1

commit v7 on v4

--- a/solution.py
+++ b/solution.py
@@ -29,12 +29,25 @@
 X_AHEAD = fsdp_perm(lambda z, x, c: (z, x + direction(c), c))
 X_BEHIND = fsdp_perm(lambda z, x, c: (z, x - direction(c), c))
 CORE_SWAP = fsdp_perm(lambda z, x, c: (z, x, 1 - c))
-def pack_kernel(x_ref, rows_ref, ids_ref, o_ref, held, side32, side, in_sem, out_sem):
+def pack_kernel(x_ref, rows_hbm, ids_hbm, o_ref, held, rows_ref, ids_ref, side32, side, in_sem, out_sem):
     planes, tokens, _ = held.shape
     n = o_ref.shape[0]
     loads = [pltpu.make_async_copy(x_ref.at[k], held.at[k], in_sem.at[k]) for k in range(planes)]
+    loads.append(pltpu.make_async_copy(rows_hbm, rows_ref, in_sem.at[planes]))
+    loads.append(pltpu.make_async_copy(ids_hbm, ids_ref, in_sem.at[planes + 1]))
     for load in loads:
         load.start()
+    stores = []
+    for k in range(planes):
+        loads[k].wait()
+        for d in range(n):
+            part = held.at[k, :, pl.ds(d * 2 * HD, 2 * HD)]
+            rows = o_ref.at[d, pl.ds(k * tokens, tokens), :]
+            copy = pltpu.make_async_copy(part, rows, out_sem.at[len(stores)])
+            copy.start()
+            stores.append(copy)
+    loads[planes].wait()
+    loads[planes + 1].wait()
     x = rows_ref[...].astype(jnp.float32)
     mean = jnp.mean(x, axis=-1, keepdims=True)
     centered = x - mean
@@ -48,15 +61,6 @@
     side32[chunks * r :, 0:tokens] = ids
     side32[chunks * r :, tokens:] = ids
     side[...] = side32[...].astype(jnp.bfloat16)
-    stores = []
-    for k in range(planes):
-        loads[k].wait()
-        for d in range(n):
-            part = held.at[k, :, pl.ds(d * 2 * HD, 2 * HD)]
-            rows = o_ref.at[d, pl.ds(k * tokens, tokens), :]
-            copy = pltpu.make_async_copy(part, rows, out_sem.at[len(stores)])
-            copy.start()
-            stores.append(copy)
     for d in range(n):
         rows = o_ref.at[d, pl.ds(planes * tokens, side.shape[0]), :]
         copy = pltpu.make_async_copy(side, rows, out_sem.at[len(stores)])
@@ -73,17 +77,15 @@
     return pl.pallas_call(
         pack_kernel,
         out_shape=jax.ShapeDtypeStruct((n, planes * tokens + extra, 2 * HD), jnp.bfloat16),
-        in_specs=[
-            pl.BlockSpec(memory_space=pl.ANY),
-            pl.BlockSpec(memory_space=pltpu.VMEM),
-            pl.BlockSpec(memory_space=pltpu.VMEM),
-        ],
+        in_specs=[pl.BlockSpec(memory_space=pl.ANY)] * 3,
         out_specs=pl.BlockSpec(memory_space=pl.ANY),
         scratch_shapes=[
             pltpu.VMEM(video.shape, jnp.bfloat16),
+            pltpu.VMEM(rows.shape, jnp.bfloat16),
+            pltpu.VMEM(ids.shape, jnp.int32),
             pltpu.VMEM((extra, 2 * HD), jnp.float32),
             pltpu.VMEM((extra, 2 * HD), jnp.bfloat16),
-            pltpu.SemaphoreType.DMA((planes,)),
+            pltpu.SemaphoreType.DMA((planes + 2,)),
             pltpu.SemaphoreType.DMA(((planes + 1) * n,)),
         ],
         cost_estimate=pl.CostEstimate(flops=0, bytes_accessed=6 << 20, transcendentals=0),
@@ -180,7 +182,7 @@
 
 def attend(tokens, block, rows, count, book, ref_kv):
     n = block.shape[0]
-    per, sub = 8, 4
+    per, sub = 16, 8
     slots = ref_kv.shape[0]
     return pl.pallas_call(
         lambda *refs: attend_kernel(tokens, sub, *refs),

time: 164 us -> 161 us (0.982)
  the two profiles are of different devices: /device:TPU:12 before, /device:TPU:14 now
where the time goes in v7:
time: 161 us
  waiting for transfers between devices  51.3 us (32%)
  starting transfers between devices  45.5 us (28%)
  blocking collectives  36.4 us (23%)
  Pallas kernels  25.4 us (16%)
    ppermute x10, waiting for transfers between devices, move(): return lax.ppermute(block, 'fsdp', pairs)  36.5 us
    all_to_all x1, blocking collectives, exchange(): return lax.all_to_all(x, 'seq', 0, 0, tiled=True)  36.4 us
    ppermute x10, starting transfers between devices, move(): return lax.ppermute(block, 'fsdp', pairs)  36 us
    pallas_call x1, Pallas kernels, attend(): pl.pallas_call(lambda *refs: attend_kernel(tokens, sub, *refs), grid_spec...  17.6 us
    all_to_all x1, waiting for transfers between devices, exchange(): return lax.all_to_all(x, 'seq', 0, 0, tiled=True)  14.8 us
    all_to_all x1, starting transfers between devices, exchange(): return lax.all_to_all(x, 'seq', 0, 0, tiled=True)  9.51 us
    pallas_call x1, Pallas kernels, pack(): pl.pallas_call(pack_kernel, out_shape=jax.ShapeDtypeStruct((n, planes * t...  3.73 us
  transfers between devices with their start and end apart: 11, of which 5 were waited for; matrix products, arithmetic and copies ran while one was open for 1% of the time, Pallas kernels for 0%

profile of v7, /device:TPU:14, one launch (start us, length us, event | category | flops | bytes accessed | tf_op | source)
XLA Modules:
  0.0 160.8 jit_solution(8376998916063409982)
XLA Ops:
  0.0 3.7 %pack.1 = bf16[16,472,256]{2,1,0:T(8,128)(2,1)} custom-call(bf16[3,128,4096]{2,1,0:T(8,128)(2,1)} %bitcast.7, bf16[4,5120]{1,0:T(4,128)(2,1)} %bitcast.11, s32[1,128]{1,0:T(1,128)} %ids_hbm.1), custom_call_target="tpu_custom_call" | custom-call | bytes 6291456 | tf_op jit(solution)/shard_map/pack/pallas_call | solution.py:77
  3.7 0.0 copy-start
  3.8 0.0 copy-start.1
  3.8 9.5 %all-to-all-start = ((bf16[16,472,256]{2,1,0:T(8,128)(2,1)}), bf16[16,472,256]{2,1,0:T(8,128)(2,1)}, u32[]{:S(2)}, u32[]{:S(2)}) async-start(bf16[16,472,256]{2,1,0:T(8,128)(2,1)} %pack.1), calls=%async_computation | async-start | bytes 7733248 | tf_op jit(solution)/shard_map/all_to_all | solution.py:237
  13.3 0.0 copy-done
  13.3 0.0 copy-done.1
  13.4 6.1 %collective-permute-start = (bf16[176,512]{1,0:T(8,128)(2,1)S(1)}, bf16[176,512]{1,0:T(8,128)(2,1)S(1)}, u32[]{:S(2)}, u32[]{:S(2)}) collective-permute-start(bf16[176,512]{1,0:T(8,128)(2,1)S(1)} %pad_maximum_fusion), channel_id=1, source_target_pairs={{0,128},{16,400},{32,160},{48,432},{64,192},{80,464},{96,224},{112... | collective-permute-start | bytes 540680 | tf_op jit(solution)/shard_map/ppermute | solution.py:241
  19.5 8.2 %collective-permute-start.1 = (bf16[176,512]{1,0:T(8,128)(2,1)S(1)}, bf16[176,512]{1,0:T(8,128)(2,1)S(1)}, u32[]{:S(2)}, u32[]{:S(2)}) collective-permute-start(bf16[176,512]{1,0:T(8,128)(2,1)S(1)} %pad_maximum_fusion), channel_id=1, source_target_pairs={{0,256},{16,272},{32,288},{48,304},{64,320},{80,336},{96,352},{112... | collective-permute-start | bytes 540680 | tf_op jit(solution)/shard_map/ppermute | solution.py:241
  27.7 3.7 %collective-permute-start.2 = (bf16[176,512]{1,0:T(8,128)(2,1)S(1)}, bf16[176,512]{1,0:T(8,128)(2,1)S(1)}, u32[]{:S(2)}, u32[]{:S(2)}) collective-permute-start(bf16[176,512]{1,0:T(8,128)(2,1)S(1)} %pad_maximum_fusion), channel_id=1, source_target_pairs={{0,384},{16,144},{32,416},{48,176},{64,448},{80,208},{96,480},{112... | collective-permute-start | bytes 540680 | tf_op jit(solution)/shard_map/ppermute | solution.py:241
  31.4 18.3 %collective-permute-done = bf16[176,512]{1,0:T(8,128)(2,1)S(1)} collective-permute-done((bf16[176,512]{1,0:T(8,128)(2,1)S(1)}, bf16[176,512]{1,0:T(8,128)(2,1)S(1)}, u32[]{:S(2)}, u32[]{:S(2)}) %collective-permute-start) | collective-permute-done | bytes 180256 | tf_op jit(solution)/shard_map/ppermute | solution.py:241
  49.7 1.3 collective-permute-done.1
  51.0 0.0 collective-permute-done.2
  51.1 2.4 %collective-permute-start.3 = (bf16[704,512]{1,0:T(8,128)(2,1)S(1)}, bf16[704,512]{1,0:T(8,128)(2,1)S(1)}, u32[]{:S(2)}, u32[]{:S(2)}) collective-permute-start(bf16[704,512]{1,0:T(8,128)(2,1)S(1)} %constant_dynamic-update-slice_fusion.refs_0_), channel_id=1, source_target_pairs={{0,32},{16,112},{32,64},{48,16},{64,96},{80,48},{96,0},{112,80},{1... | collective-permute-start | bytes 2162696 | tf_op jit(solution)/shard_map/ppermute | solution.py:241
  53.5 3.4 %collective-permute-start.5 = (bf16[704,512]{1,0:T(8,128)(2,1)S(1)}, bf16[704,512]{1,0:T(8,128)(2,1)S(1)}, u32[]{:S(2)}, u32[]{:S(2)}) collective-permute-start(bf16[704,512]{1,0:T(8,128)(2,1)S(1)} %constant_dynamic-update-slice_fusion.refs_0_), channel_id=1, source_target_pairs={{0,96},{16,48},{32,0},{48,80},{64,32},{80,112},{96,64},{112,16},{1... | collective-permute-start | bytes 2162696 | tf_op jit(solution)/shard_map/ppermute | solution.py:241
  56.9 12.7 %collective-permute-done.3.refs_1_ = bf16[704,512]{1,0:T(8,128)(2,1)S(1)} collective-permute-done((bf16[704,512]{1,0:T(8,128)(2,1)S(1)}, bf16[704,512]{1,0:T(8,128)(2,1)S(1)}, u32[]{:S(2)}, u32[]{:S(2)}) %collective-permute-start.3) | collective-permute-done | bytes 720928 | tf_op jit(solution)/shard_map/ppermute | solution.py:241
  69.6 1.9 %collective-permute-start.4 = (bf16[704,512]{1,0:T(8,128)(2,1)S(1)}, bf16[704,512]{1,0:T(8,128)(2,1)S(1)}, u32[]{:S(2)}, u32[]{:S(2)}) collective-permute-start(bf16[704,512]{1,0:T(8,128)(2,1)S(1)} %collective-permute-done.3.refs_1_), channel_id=1, source_target_pairs={{0,32},{16,112},{32,64},{48,16},{64,96},{80,48},{96,0},{112,80},{1... | collective-permute-start | bytes 2162696 | tf_op jit(solution)/shard_map/ppermute | solution.py:241
  71.6 2.8 %collective-permute-start.6 = (bf16[704,512]{1,0:T(8,128)(2,1)S(1)}, bf16[704,512]{1,0:T(8,128)(2,1)}, u32[]{:S(2)}, u32[]{:S(2)}) collective-permute-start(bf16[704,512]{1,0:T(8,128)(2,1)S(1)} %constant_dynamic-update-slice_fusion.refs_0_), channel_id=1, source_target_pairs={{0,16},{16,0},{32,48},{48,32},{64,80},{80,64},{96,112},{112,96},{1... | collective-permute-start | bytes 2162696 | tf_op jit(solution)/shard_map/ppermute | solution.py:241
  74.3 1.9 %collective-permute-start.7 = (bf16[704,512]{1,0:T(8,128)(2,1)S(1)}, bf16[704,512]{1,0:T(8,128)(2,1)}, u32[]{:S(2)}, u32[]{:S(2)}) collective-permute-start(bf16[704,512]{1,0:T(8,128)(2,1)S(1)} %collective-permute-done.3.refs_1_), channel_id=1, source_target_pairs={{0,16},{16,0},{32,48},{48,32},{64,80},{80,64},{96,112},{112,96},{1... | collective-permute-start | bytes 2162696 | tf_op jit(solution)/shard_map/ppermute | solution.py:241
  76.3 0.0 collective-permute-done.5.refs_3_
  76.3 2.4 %collective-permute-start.9 = (bf16[704,512]{1,0:T(8,128)(2,1)S(1)}, bf16[704,512]{1,0:T(8,128)(2,1)}, u32[]{:S(2)}, u32[]{:S(2)}) collective-permute-start(bf16[704,512]{1,0:T(8,128)(2,1)S(1)} %collective-permute-done.5.refs_3_), channel_id=1, source_target_pairs={{0,16},{16,0},{32,48},{48,32},{64,80},{80,64},{96,112},{112,96},{1... | collective-permute-start | bytes 2162696 | tf_op jit(solution)/shard_map/ppermute | solution.py:241
  78.7 4.1 %collective-permute-done.4.refs_2_ = bf16[704,512]{1,0:T(8,128)(2,1)S(1)} collective-permute-done((bf16[704,512]{1,0:T(8,128)(2,1)S(1)}, bf16[704,512]{1,0:T(8,128)(2,1)S(1)}, u32[]{:S(2)}, u32[]{:S(2)}) %collective-permute-start.4) | collective-permute-done | bytes 720928 | tf_op jit(solution)/shard_map/ppermute | solution.py:241
  82.8 3.2 %collective-permute-start.8 = (bf16[704,512]{1,0:T(8,128)(2,1)S(1)}, bf16[704,512]{1,0:T(8,128)(2,1)}, u32[]{:S(2)}, u32[]{:S(2)}) collective-permute-start(bf16[704,512]{1,0:T(8,128)(2,1)S(1)} %collective-permute-done.4.refs_2_), channel_id=1, source_target_pairs={{0,16},{16,0},{32,48},{48,32},{64,80},{80,64},{96,112},{112,96},{1... | collective-permute-start | bytes 2162696 | tf_op jit(solution)/shard_map/ppermute | solution.py:241
  86.7 14.8 %all-to-all-done.refs_1_.refs_2_.refs_3_ = bf16[16,472,256]{2,1,0:T(8,128)(2,1)} async-done(((bf16[16,472,256]{2,1,0:T(8,128)(2,1)}), bf16[16,472,256]{2,1,0:T(8,128)(2,1)}, u32[]{:S(2)}, u32[]{:S(2)}) %all-to-all-start) | async-done | bytes 3866656 | tf_op jit(solution)/shard_map/all_to_all | solution.py:237
  101.5 1.2 slice.4.rows_ref.refs_4_
  102.6 0.0 collective-permute-done.6.refs_4_
  102.6 0.0 collective-permute-done.7.refs_5_
  102.6 0.0 collective-permute-done.9.refs_7_
  102.7 0.0 collective-permute-done.8.refs_6_
  102.7 3.0 %ref_project.1 = (bf16[64,512]{1,0:T(8,128)(2,1)S(1)}, bf16[256,256]{1,0:T(8,128)(2,1)S(1)}) custom-call(bf16[16,88,256]{2,1,0:T(8,128)(2,1)S(1)} %slice.4.rows_ref.refs_4_, bf16[704,512]{1,0:T(8,128)(2,1)S(1)} %constant_dynamic-update-slice_fusion.refs_0_, bf16[704,512]{1,0:T(8,128)(2,1)S(1)} %collective-permute-done.3.refs_1_, ...), custom_call_target="tpu_custom_call" | custom-call | flops 1024 | bytes 1024 | tf_op jit(solution)/shard_map/ref_project/pallas_call | solution.py:131
  105.7 17.6 %attend.1 = bf16[16,128,256]{2,1,0:T(8,128)(2,1)S(1)} custom-call(s32[1]{0:T(128)S(6)} %copy.12.refs_0_, bf16[16,472,256]{2,1,0:T(8,128)(2,1)} %all-to-all-done.refs_1_.refs_2_.refs_3_, bf16[16,472,256]{2,1,0:T(8,128)(2,1)} %all-to-all-done.refs_1_.refs_2_.refs_3_, bf16[16,472,256]{2,1,0:T(8,128)(2,1)} %all-to-all-done.refs_1_.refs_2_.refs_3_, ...), custom_call_target="tpu_custom_call" | custom-call | flops 1024 | bytes 1024 | tf_op jit(solution)/shard_map/attend/pallas_call | solution.py:187
  123.3 36.4 %all_to_all.10.r_ref = bf16[16,128,256]{2,1,0:T(8,128)(2,1)S(1)} all-to-all(bf16[16,128,256]{2,1,0:T(8,128)(2,1)S(1)} %attend.1), channel_id=1, replica_groups=mesh['fsdp'=32,'seq'=16] {'seq'}, dimensions={0} | all-to-all | bytes 2097152 | tf_op jit(solution)/shard_map/all_to_all | solution.py:237
  159.7 1.1 unpack.1
  (7 shorter events, 0.1 us)
Async XLA Ops:
  3.7 9.5 %copy-start = (bf16[160,2,256]{2,1,0:T(2,128)(2,1)S(1)}, bf16[160,2,256]{2,1,0:T(2,128)(2,1)}, u32[]{:S(2)}) copy-start(bf16[160,2,256]{2,1,0:T(2,128)(2,1)} %param.8) | copy-start | bytes 491524
  3.8 9.6 %copy-start.1 = (bf16[8,256]{1,0:T(8,128)(2,1)S(1)}, bf16[8,256]{1,0:T(8,128)(2,1)}, u32[]{:S(2)}) copy-start(bf16[8,256]{1,0:T(8,128)(2,1)} %param.9) | copy-start | bytes 12292
  3.8 97.7 %all-to-all-start = ((bf16[16,472,256]{2,1,0:T(8,128)(2,1)}), bf16[16,472,256]{2,1,0:T(8,128)(2,1)}, u32[]{:S(2)}, u32[]{:S(2)}) async-start(bf16[16,472,256]{2,1,0:T(8,128)(2,1)} %pack.1), calls=%async_computation | async-start | bytes 7733248 | tf_op jit(solution)/shard_map/all_to_all | solution.py:237
  13.4 36.3 %collective-permute-start = (bf16[176,512]{1,0:T(8,128)(2,1)S(1)}, bf16[176,512]{1,0:T(8,128)(2,1)S(1)}, u32[]{:S(2)}, u32[]{:S(2)}) collective-permute-start(bf16[176,512]{1,0:T(8,128)(2,1)S(1)} %pad_maximum_fusion), channel_id=1, source_target_pairs={{0,128},{16,400},{32,160},{48,432},{64,192},{80,464},{96,224},{112... | collective-permute-start | bytes 540680 | tf_op jit(solution)/shard_map/ppermute | solution.py:241
  19.5 31.5 %collective-permute-start.1 = (bf16[176,512]{1,0:T(8,128)(2,1)S(1)}, bf16[176,512]{1,0:T(8,128)(2,1)S(1)}, u32[]{:S(2)}, u32[]{:S(2)}) collective-permute-start(bf16[176,512]{1,0:T(8,128)(2,1)S(1)} %pad_maximum_fusion), channel_id=1, source_target_pairs={{0,256},{16,272},{32,288},{48,304},{64,320},{80,336},{96,352},{112... | collective-permute-start | bytes 540680 | tf_op jit(solution)/shard_map/ppermute | solution.py:241
  27.7 23.3 %collective-permute-start.2 = (bf16[176,512]{1,0:T(8,128)(2,1)S(1)}, bf16[176,512]{1,0:T(8,128)(2,1)S(1)}, u32[]{:S(2)}, u32[]{:S(2)}) collective-permute-start(bf16[176,512]{1,0:T(8,128)(2,1)S(1)} %pad_maximum_fusion), channel_id=1, source_target_pairs={{0,384},{16,144},{32,416},{48,176},{64,448},{80,208},{96,480},{112... | collective-permute-start | bytes 540680 | tf_op jit(solution)/shard_map/ppermute | solution.py:241
  51.1 18.6 %collective-permute-start.3 = (bf16[704,512]{1,0:T(8,128)(2,1)S(1)}, bf16[704,512]{1,0:T(8,128)(2,1)S(1)}, u32[]{:S(2)}, u32[]{:S(2)}) collective-permute-start(bf16[704,512]{1,0:T(8,128)(2,1)S(1)} %constant_dynamic-update-slice_fusion.refs_0_), channel_id=1, source_target_pairs={{0,32},{16,112},{32,64},{48,16},{64,96},{80,48},{96,0},{112,80},{1... | collective-permute-start | bytes 2162696 | tf_op jit(solution)/shard_map/ppermute | solution.py:241
  53.5 22.8 %collective-permute-start.5 = (bf16[704,512]{1,0:T(8,128)(2,1)S(1)}, bf16[704,512]{1,0:T(8,128)(2,1)S(1)}, u32[]{:S(2)}, u32[]{:S(2)}) collective-permute-start(bf16[704,512]{1,0:T(8,128)(2,1)S(1)} %constant_dynamic-update-slice_fusion.refs_0_), channel_id=1, source_target_pairs={{0,96},{16,48},{32,0},{48,80},{64,32},{80,112},{96,64},{112,16},{1... | collective-permute-start | bytes 2162696 | tf_op jit(solution)/shard_map/ppermute | solution.py:241
  69.6 13.2 %collective-permute-start.4 = (bf16[704,512]{1,0:T(8,128)(2,1)S(1)}, bf16[704,512]{1,0:T(8,128)(2,1)S(1)}, u32[]{:S(2)}, u32[]{:S(2)}) collective-permute-start(bf16[704,512]{1,0:T(8,128)(2,1)S(1)} %collective-permute-done.3.refs_1_), channel_id=1, source_target_pairs={{0,32},{16,112},{32,64},{48,16},{64,96},{80,48},{96,0},{112,80},{1... | collective-permute-start | bytes 2162696 | tf_op jit(solution)/shard_map/ppermute | solution.py:241
  71.6 31.1 %collective-permute-start.6 = (bf16[704,512]{1,0:T(8,128)(2,1)S(1)}, bf16[704,512]{1,0:T(8,128)(2,1)}, u32[]{:S(2)}, u32[]{:S(2)}) collective-permute-start(bf16[704,512]{1,0:T(8,128)(2,1)S(1)} %constant_dynamic-update-slice_fusion.refs_0_), channel_id=1, source_target_pairs={{0,16},{16,0},{32,48},{48,32},{64,80},{80,64},{96,112},{112,96},{1... | collective-permute-start | bytes 2162696 | tf_op jit(solution)/shard_map/ppermute | solution.py:241
  74.3 28.3 %collective-permute-start.7 = (bf16[704,512]{1,0:T(8,128)(2,1)S(1)}, bf16[704,512]{1,0:T(8,128)(2,1)}, u32[]{:S(2)}, u32[]{:S(2)}) collective-permute-start(bf16[704,512]{1,0:T(8,128)(2,1)S(1)} %collective-permute-done.3.refs_1_), channel_id=1, source_target_pairs={{0,16},{16,0},{32,48},{48,32},{64,80},{80,64},{96,112},{112,96},{1... | collective-permute-start | bytes 2162696 | tf_op jit(solution)/shard_map/ppermute | solution.py:241
  76.3 26.4 %collective-permute-start.9 = (bf16[704,512]{1,0:T(8,128)(2,1)S(1)}, bf16[704,512]{1,0:T(8,128)(2,1)}, u32[]{:S(2)}, u32[]{:S(2)}) collective-permute-start(bf16[704,512]{1,0:T(8,128)(2,1)S(1)} %collective-permute-done.5.refs_3_), channel_id=1, source_target_pairs={{0,16},{16,0},{32,48},{48,32},{64,80},{80,64},{96,112},{112,96},{1... | collective-permute-start | bytes 2162696 | tf_op jit(solution)/shard_map/ppermute | solution.py:241
  82.8 19.8 %collective-permute-start.8 = (bf16[704,512]{1,0:T(8,128)(2,1)S(1)}, bf16[704,512]{1,0:T(8,128)(2,1)}, u32[]{:S(2)}, u32[]{:S(2)}) collective-permute-start(bf16[704,512]{1,0:T(8,128)(2,1)S(1)} %collective-permute-done.4.refs_2_), channel_id=1, source_target_pairs={{0,16},{16,0},{32,48},{48,32},{64,80},{80,64},{96,112},{112,96},{1... | collective-permute-start | bytes 2162696 | tf_op jit(solution)/shard_map/ppermute | solution.py:241

commit v8 on v7

--- a/solution.py
+++ b/solution.py
@@ -10,6 +10,7 @@
 HD = 128
 TPF = 16
 WROWS = 176
+CUTS = 4
 SIDE = 8
 
 
@@ -32,22 +33,30 @@
 def pack_kernel(x_ref, rows_hbm, ids_hbm, o_ref, held, rows_ref, ids_ref, side32, side, in_sem, out_sem):
     planes, tokens, _ = held.shape
     n = o_ref.shape[0]
-    loads = [pltpu.make_async_copy(x_ref.at[k], held.at[k], in_sem.at[k]) for k in range(planes)]
-    loads.append(pltpu.make_async_copy(rows_hbm, rows_ref, in_sem.at[planes]))
-    loads.append(pltpu.make_async_copy(ids_hbm, ids_ref, in_sem.at[planes + 1]))
+    cut = held.shape[2] // CUTS
+    loads = []
+    for k in range(planes):
+        for q in range(CUTS):
+            cols = pl.ds(q * cut, cut)
+            loads.append(
+                pltpu.make_async_copy(x_ref.at[k, :, cols], held.at[k, :, cols], in_sem.at[len(loads)])
+            )
+    loads.append(pltpu.make_async_copy(rows_hbm, rows_ref, in_sem.at[planes * CUTS]))
+    loads.append(pltpu.make_async_copy(ids_hbm, ids_ref, in_sem.at[planes * CUTS + 1]))
     for load in loads:
         load.start()
     stores = []
     for k in range(planes):
-        loads[k].wait()
         for d in range(n):
+            if d % (n // CUTS) == 0:
+                loads[k * CUTS + d // (n // CUTS)].wait()
             part = held.at[k, :, pl.ds(d * 2 * HD, 2 * HD)]
             rows = o_ref.at[d, pl.ds(k * tokens, tokens), :]
             copy = pltpu.make_async_copy(part, rows, out_sem.at[len(stores)])
             copy.start()
             stores.append(copy)
-    loads[planes].wait()
-    loads[planes + 1].wait()
+    loads[planes * CUTS].wait()
+    loads[planes * CUTS + 1].wait()
     x = rows_ref[...].astype(jnp.float32)
     mean = jnp.mean(x, axis=-1, keepdims=True)
     centered = x - mean
@@ -85,7 +94,7 @@
             pltpu.VMEM(ids.shape, jnp.int32),
             pltpu.VMEM((extra, 2 * HD), jnp.float32),
             pltpu.VMEM((extra, 2 * HD), jnp.bfloat16),
-            pltpu.SemaphoreType.DMA((planes + 2,)),
+            pltpu.SemaphoreType.DMA((planes * CUTS + 2,)),
             pltpu.SemaphoreType.DMA(((planes + 1) * n,)),
         ],
         cost_estimate=pl.CostEstimate(flops=0, bytes_accessed=6 << 20, transcendentals=0),

time: 161 us -> 161 us (level)
  the two profiles are of different devices: /device:TPU:14 before, /device:TPU:12 now
where the time goes in v8:
time: 161 us
  waiting for transfers between devices  52.5 us (33%)
  starting transfers between devices  44.3 us (28%)
  blocking collectives  36.4 us (23%)
  Pallas kernels  25.4 us (16%)
    ppermute x10, waiting for transfers between devices, move(): return lax.ppermute(block, 'fsdp', pairs)  36.7 us
    all_to_all x1, blocking collectives, exchange(): return lax.all_to_all(x, 'seq', 0, 0, tiled=True)  36.4 us
    ppermute x10, starting transfers between devices, move(): return lax.ppermute(block, 'fsdp', pairs)  34.8 us
    pallas_call x1, Pallas kernels, attend(): pl.pallas_call(lambda *refs: attend_kernel(tokens, sub, *refs), grid_spec...  17.6 us
    all_to_all x1, waiting for transfers between devices, exchange(): return lax.all_to_all(x, 'seq', 0, 0, tiled=True)  15.8 us
    all_to_all x1, starting transfers between devices, exchange(): return lax.all_to_all(x, 'seq', 0, 0, tiled=True)  9.51 us
    pallas_call x1, Pallas kernels, pack(): pl.pallas_call(pack_kernel, out_shape=jax.ShapeDtypeStruct((n, planes * t...  3.69 us
  transfers between devices with their start and end apart: 11, of which 5 were waited for; matrix products, arithmetic and copies ran while one was open for 1% of the time, Pallas kernels for 0%

profile of v8, /device:TPU:12, one launch (start us, length us, event | category | flops | bytes accessed | tf_op | source)
XLA Modules:
  0.0 160.7 jit_solution(5246105953761384026)
XLA Ops:
  0.0 3.7 %pack.1 = bf16[16,472,256]{2,1,0:T(8,128)(2,1)} custom-call(bf16[3,128,4096]{2,1,0:T(8,128)(2,1)} %bitcast.7, bf16[4,5120]{1,0:T(4,128)(2,1)} %bitcast.11, s32[1,128]{1,0:T(1,128)} %ids_hbm.1), custom_call_target="tpu_custom_call" | custom-call | bytes 6291456 | tf_op jit(solution)/shard_map/pack/pallas_call | solution.py:86
  3.7 0.0 copy-start
  3.7 0.0 copy-start.1
  3.7 9.5 %all-to-all-start = ((bf16[16,472,256]{2,1,0:T(8,128)(2,1)}), bf16[16,472,256]{2,1,0:T(8,128)(2,1)}, u32[]{:S(2)}, u32[]{:S(2)}) async-start(bf16[16,472,256]{2,1,0:T(8,128)(2,1)} %pack.1), calls=%async_computation | async-start | bytes 7733248 | tf_op jit(solution)/shard_map/all_to_all | solution.py:246
  13.2 0.0 copy-done
  13.3 0.0 copy-done.1
  13.3 6.1 %collective-permute-start = (bf16[176,512]{1,0:T(8,128)(2,1)S(1)}, bf16[176,512]{1,0:T(8,128)(2,1)S(1)}, u32[]{:S(2)}, u32[]{:S(2)}) collective-permute-start(bf16[176,512]{1,0:T(8,128)(2,1)S(1)} %pad_maximum_fusion), channel_id=1, source_target_pairs={{0,128},{16,400},{32,160},{48,432},{64,192},{80,464},{96,224},{112... | collective-permute-start | bytes 540680 | tf_op jit(solution)/shard_map/ppermute | solution.py:250
  19.4 8.2 %collective-permute-start.1 = (bf16[176,512]{1,0:T(8,128)(2,1)S(1)}, bf16[176,512]{1,0:T(8,128)(2,1)S(1)}, u32[]{:S(2)}, u32[]{:S(2)}) collective-permute-start(bf16[176,512]{1,0:T(8,128)(2,1)S(1)} %pad_maximum_fusion), channel_id=1, source_target_pairs={{0,256},{16,272},{32,288},{48,304},{64,320},{80,336},{96,352},{112... | collective-permute-start | bytes 540680 | tf_op jit(solution)/shard_map/ppermute | solution.py:250
  27.7 3.7 %collective-permute-start.2 = (bf16[176,512]{1,0:T(8,128)(2,1)S(1)}, bf16[176,512]{1,0:T(8,128)(2,1)S(1)}, u32[]{:S(2)}, u32[]{:S(2)}) collective-permute-start(bf16[176,512]{1,0:T(8,128)(2,1)S(1)} %pad_maximum_fusion), channel_id=1, source_target_pairs={{0,384},{16,144},{32,416},{48,176},{64,448},{80,208},{96,480},{112... | collective-permute-start | bytes 540680 | tf_op jit(solution)/shard_map/ppermute | solution.py:250
  31.3 18.3 %collective-permute-done = bf16[176,512]{1,0:T(8,128)(2,1)S(1)} collective-permute-done((bf16[176,512]{1,0:T(8,128)(2,1)S(1)}, bf16[176,512]{1,0:T(8,128)(2,1)S(1)}, u32[]{:S(2)}, u32[]{:S(2)}) %collective-permute-start) | collective-permute-done | bytes 180256 | tf_op jit(solution)/shard_map/ppermute | solution.py:250
  49.7 1.3 collective-permute-done.1
  51.0 0.0 collective-permute-done.2
  51.0 3.1 %collective-permute-start.3 = (bf16[704,512]{1,0:T(8,128)(2,1)S(1)}, bf16[704,512]{1,0:T(8,128)(2,1)S(1)}, u32[]{:S(2)}, u32[]{:S(2)}) collective-permute-start(bf16[704,512]{1,0:T(8,128)(2,1)S(1)} %constant_dynamic-update-slice_fusion.refs_0_), channel_id=1, source_target_pairs={{0,32},{16,112},{32,64},{48,16},{64,96},{80,48},{96,0},{112,80},{1... | collective-permute-start | bytes 2162696 | tf_op jit(solution)/shard_map/ppermute | solution.py:250
  54.1 2.7 %collective-permute-start.5 = (bf16[704,512]{1,0:T(8,128)(2,1)S(1)}, bf16[704,512]{1,0:T(8,128)(2,1)S(1)}, u32[]{:S(2)}, u32[]{:S(2)}) collective-permute-start(bf16[704,512]{1,0:T(8,128)(2,1)S(1)} %constant_dynamic-update-slice_fusion.refs_0_), channel_id=1, source_target_pairs={{0,96},{16,48},{32,0},{48,80},{64,32},{80,112},{96,64},{112,16},{1... | collective-permute-start | bytes 2162696 | tf_op jit(solution)/shard_map/ppermute | solution.py:250
  56.9 13.0 %collective-permute-done.3.refs_1_ = bf16[704,512]{1,0:T(8,128)(2,1)S(1)} collective-permute-done((bf16[704,512]{1,0:T(8,128)(2,1)S(1)}, bf16[704,512]{1,0:T(8,128)(2,1)S(1)}, u32[]{:S(2)}, u32[]{:S(2)}) %collective-permute-start.3) | collective-permute-done | bytes 720928 | tf_op jit(solution)/shard_map/ppermute | solution.py:250
  69.9 2.8 %collective-permute-start.4 = (bf16[704,512]{1,0:T(8,128)(2,1)S(1)}, bf16[704,512]{1,0:T(8,128)(2,1)S(1)}, u32[]{:S(2)}, u32[]{:S(2)}) collective-permute-start(bf16[704,512]{1,0:T(8,128)(2,1)S(1)} %collective-permute-done.3.refs_1_), channel_id=1, source_target_pairs={{0,32},{16,112},{32,64},{48,16},{64,96},{80,48},{96,0},{112,80},{1... | collective-permute-start | bytes 2162696 | tf_op jit(solution)/shard_map/ppermute | solution.py:250
  72.7 1.9 %collective-permute-start.6 = (bf16[704,512]{1,0:T(8,128)(2,1)S(1)}, bf16[704,512]{1,0:T(8,128)(2,1)}, u32[]{:S(2)}, u32[]{:S(2)}) collective-permute-start(bf16[704,512]{1,0:T(8,128)(2,1)S(1)} %constant_dynamic-update-slice_fusion.refs_0_), channel_id=1, source_target_pairs={{0,16},{16,0},{32,48},{48,32},{64,80},{80,64},{96,112},{112,96},{1... | collective-permute-start | bytes 2162696 | tf_op jit(solution)/shard_map/ppermute | solution.py:250
  74.6 2.4 %collective-permute-start.7 = (bf16[704,512]{1,0:T(8,128)(2,1)S(1)}, bf16[704,512]{1,0:T(8,128)(2,1)}, u32[]{:S(2)}, u32[]{:S(2)}) collective-permute-start(bf16[704,512]{1,0:T(8,128)(2,1)S(1)} %collective-permute-done.3.refs_1_), channel_id=1, source_target_pairs={{0,16},{16,0},{32,48},{48,32},{64,80},{80,64},{96,112},{112,96},{1... | collective-permute-start | bytes 2162696 | tf_op jit(solution)/shard_map/ppermute | solution.py:250
  77.1 0.0 collective-permute-done.5.refs_3_
  77.1 1.9 %collective-permute-start.9 = (bf16[704,512]{1,0:T(8,128)(2,1)S(1)}, bf16[704,512]{1,0:T(8,128)(2,1)}, u32[]{:S(2)}, u32[]{:S(2)}) collective-permute-start(bf16[704,512]{1,0:T(8,128)(2,1)S(1)} %collective-permute-done.5.refs_3_), channel_id=1, source_target_pairs={{0,16},{16,0},{32,48},{48,32},{64,80},{80,64},{96,112},{112,96},{1... | collective-permute-start | bytes 2162696 | tf_op jit(solution)/shard_map/ppermute | solution.py:250
  79.0 4.1 %collective-permute-done.4.refs_2_ = bf16[704,512]{1,0:T(8,128)(2,1)S(1)} collective-permute-done((bf16[704,512]{1,0:T(8,128)(2,1)S(1)}, bf16[704,512]{1,0:T(8,128)(2,1)S(1)}, u32[]{:S(2)}, u32[]{:S(2)}) %collective-permute-start.4) | collective-permute-done | bytes 720928 | tf_op jit(solution)/shard_map/ppermute | solution.py:250
  83.1 1.9 %collective-permute-start.8 = (bf16[704,512]{1,0:T(8,128)(2,1)S(1)}, bf16[704,512]{1,0:T(8,128)(2,1)}, u32[]{:S(2)}, u32[]{:S(2)}) collective-permute-start(bf16[704,512]{1,0:T(8,128)(2,1)S(1)} %collective-permute-done.4.refs_2_), channel_id=1, source_target_pairs={{0,16},{16,0},{32,48},{48,32},{64,80},{80,64},{96,112},{112,96},{1... | collective-permute-start | bytes 2162696 | tf_op jit(solution)/shard_map/ppermute | solution.py:250
  85.6 15.8 %all-to-all-done.refs_1_.refs_2_.refs_3_ = bf16[16,472,256]{2,1,0:T(8,128)(2,1)} async-done(((bf16[16,472,256]{2,1,0:T(8,128)(2,1)}), bf16[16,472,256]{2,1,0:T(8,128)(2,1)}, u32[]{:S(2)}, u32[]{:S(2)}) %all-to-all-start) | async-done | bytes 3866656 | tf_op jit(solution)/shard_map/all_to_all | solution.py:246
  101.4 1.2 slice.4.rows_ref.refs_4_
  102.6 0.0 collective-permute-done.6.refs_4_
  102.6 0.0 collective-permute-done.7.refs_5_
  102.6 0.0 collective-permute-done.9.refs_7_
  102.6 0.0 collective-permute-done.8.refs_6_
  102.6 3.0 %ref_project.1 = (bf16[64,512]{1,0:T(8,128)(2,1)S(1)}, bf16[256,256]{1,0:T(8,128)(2,1)S(1)}) custom-call(bf16[16,88,256]{2,1,0:T(8,128)(2,1)S(1)} %slice.4.rows_ref.refs_4_, bf16[704,512]{1,0:T(8,128)(2,1)S(1)} %constant_dynamic-update-slice_fusion.refs_0_, bf16[704,512]{1,0:T(8,128)(2,1)S(1)} %collective-permute-done.3.refs_1_, ...), custom_call_target="tpu_custom_call" | custom-call | flops 1024 | bytes 1024 | tf_op jit(solution)/shard_map/ref_project/pallas_call | solution.py:140
  105.6 17.6 %attend.1 = bf16[16,128,256]{2,1,0:T(8,128)(2,1)S(1)} custom-call(s32[1]{0:T(128)S(6)} %copy.12.refs_0_, bf16[16,472,256]{2,1,0:T(8,128)(2,1)} %all-to-all-done.refs_1_.refs_2_.refs_3_, bf16[16,472,256]{2,1,0:T(8,128)(2,1)} %all-to-all-done.refs_1_.refs_2_.refs_3_, bf16[16,472,256]{2,1,0:T(8,128)(2,1)} %all-to-all-done.refs_1_.refs_2_.refs_3_, ...), custom_call_target="tpu_custom_call" | custom-call | flops 1024 | bytes 1024 | tf_op jit(solution)/shard_map/attend/pallas_call | solution.py:196
  123.2 36.4 %all_to_all.10.r_ref = bf16[16,128,256]{2,1,0:T(8,128)(2,1)S(1)} all-to-all(bf16[16,128,256]{2,1,0:T(8,128)(2,1)S(1)} %attend.1), channel_id=1, replica_groups=mesh['fsdp'=32,'seq'=16] {'seq'}, dimensions={0} | all-to-all | bytes 2097152 | tf_op jit(solution)/shard_map/all_to_all | solution.py:246
  159.6 1.1 unpack.1
  (7 shorter events, 0.1 us)
Async XLA Ops:
  3.7 9.5 %copy-start = (bf16[160,2,256]{2,1,0:T(2,128)(2,1)S(1)}, bf16[160,2,256]{2,1,0:T(2,128)(2,1)}, u32[]{:S(2)}) copy-start(bf16[160,2,256]{2,1,0:T(2,128)(2,1)} %param.8) | copy-start | bytes 491524
  3.7 9.6 %copy-start.1 = (bf16[8,256]{1,0:T(8,128)(2,1)S(1)}, bf16[8,256]{1,0:T(8,128)(2,1)}, u32[]{:S(2)}) copy-start(bf16[8,256]{1,0:T(8,128)(2,1)} %param.9) | copy-start | bytes 12292
  3.7 97.7 %all-to-all-start = ((bf16[16,472,256]{2,1,0:T(8,128)(2,1)}), bf16[16,472,256]{2,1,0:T(8,128)(2,1)}, u32[]{:S(2)}, u32[]{:S(2)}) async-start(bf16[16,472,256]{2,1,0:T(8,128)(2,1)} %pack.1), calls=%async_computation | async-start | bytes 7733248 | tf_op jit(solution)/shard_map/all_to_all | solution.py:246
  13.3 36.3 %collective-permute-start = (bf16[176,512]{1,0:T(8,128)(2,1)S(1)}, bf16[176,512]{1,0:T(8,128)(2,1)S(1)}, u32[]{:S(2)}, u32[]{:S(2)}) collective-permute-start(bf16[176,512]{1,0:T(8,128)(2,1)S(1)} %pad_maximum_fusion), channel_id=1, source_target_pairs={{0,128},{16,400},{32,160},{48,432},{64,192},{80,464},{96,224},{112... | collective-permute-start | bytes 540680 | tf_op jit(solution)/shard_map/ppermute | solution.py:250
  19.4 31.5 %collective-permute-start.1 = (bf16[176,512]{1,0:T(8,128)(2,1)S(1)}, bf16[176,512]{1,0:T(8,128)(2,1)S(1)}, u32[]{:S(2)}, u32[]{:S(2)}) collective-permute-start(bf16[176,512]{1,0:T(8,128)(2,1)S(1)} %pad_maximum_fusion), channel_id=1, source_target_pairs={{0,256},{16,272},{32,288},{48,304},{64,320},{80,336},{96,352},{112... | collective-permute-start | bytes 540680 | tf_op jit(solution)/shard_map/ppermute | solution.py:250
  27.7 23.3 %collective-permute-start.2 = (bf16[176,512]{1,0:T(8,128)(2,1)S(1)}, bf16[176,512]{1,0:T(8,128)(2,1)S(1)}, u32[]{:S(2)}, u32[]{:S(2)}) collective-permute-start(bf16[176,512]{1,0:T(8,128)(2,1)S(1)} %pad_maximum_fusion), channel_id=1, source_target_pairs={{0,384},{16,144},{32,416},{48,176},{64,448},{80,208},{96,480},{112... | collective-permute-start | bytes 540680 | tf_op jit(solution)/shard_map/ppermute | solution.py:250
  51.0 18.9 %collective-permute-start.3 = (bf16[704,512]{1,0:T(8,128)(2,1)S(1)}, bf16[704,512]{1,0:T(8,128)(2,1)S(1)}, u32[]{:S(2)}, u32[]{:S(2)}) collective-permute-start(bf16[704,512]{1,0:T(8,128)(2,1)S(1)} %constant_dynamic-update-slice_fusion.refs_0_), channel_id=1, source_target_pairs={{0,32},{16,112},{32,64},{48,16},{64,96},{80,48},{96,0},{112,80},{1... | collective-permute-start | bytes 2162696 | tf_op jit(solution)/shard_map/ppermute | solution.py:250
  54.1 22.9 %collective-permute-start.5 = (bf16[704,512]{1,0:T(8,128)(2,1)S(1)}, bf16[704,512]{1,0:T(8,128)(2,1)S(1)}, u32[]{:S(2)}, u32[]{:S(2)}) collective-permute-start(bf16[704,512]{1,0:T(8,128)(2,1)S(1)} %constant_dynamic-update-slice_fusion.refs_0_), channel_id=1, source_target_pairs={{0,96},{16,48},{32,0},{48,80},{64,32},{80,112},{96,64},{112,16},{1... | collective-permute-start | bytes 2162696 | tf_op jit(solution)/shard_map/ppermute | solution.py:250
  69.9 13.2 %collective-permute-start.4 = (bf16[704,512]{1,0:T(8,128)(2,1)S(1)}, bf16[704,512]{1,0:T(8,128)(2,1)S(1)}, u32[]{:S(2)}, u32[]{:S(2)}) collective-permute-start(bf16[704,512]{1,0:T(8,128)(2,1)S(1)} %collective-permute-done.3.refs_1_), channel_id=1, source_target_pairs={{0,32},{16,112},{32,64},{48,16},{64,96},{80,48},{96,0},{112,80},{1... | collective-permute-start | bytes 2162696 | tf_op jit(solution)/shard_map/ppermute | solution.py:250
  72.7 29.9 %collective-permute-start.6 = (bf16[704,512]{1,0:T(8,128)(2,1)S(1)}, bf16[704,512]{1,0:T(8,128)(2,1)}, u32[]{:S(2)}, u32[]{:S(2)}) collective-permute-start(bf16[704,512]{1,0:T(8,128)(2,1)S(1)} %constant_dynamic-update-slice_fusion.refs_0_), channel_id=1, source_target_pairs={{0,16},{16,0},{32,48},{48,32},{64,80},{80,64},{96,112},{112,96},{1... | collective-permute-start | bytes 2162696 | tf_op jit(solution)/shard_map/ppermute | solution.py:250
  74.6 28.0 %collective-permute-start.7 = (bf16[704,512]{1,0:T(8,128)(2,1)S(1)}, bf16[704,512]{1,0:T(8,128)(2,1)}, u32[]{:S(2)}, u32[]{:S(2)}) collective-permute-start(bf16[704,512]{1,0:T(8,128)(2,1)S(1)} %collective-permute-done.3.refs_1_), channel_id=1, source_target_pairs={{0,16},{16,0},{32,48},{48,32},{64,80},{80,64},{96,112},{112,96},{1... | collective-permute-start | bytes 2162696 | tf_op jit(solution)/shard_map/ppermute | solution.py:250
  77.1 25.5 %collective-permute-start.9 = (bf16[704,512]{1,0:T(8,128)(2,1)S(1)}, bf16[704,512]{1,0:T(8,128)(2,1)}, u32[]{:S(2)}, u32[]{:S(2)}) collective-permute-start(bf16[704,512]{1,0:T(8,128)(2,1)S(1)} %collective-permute-done.5.refs_3_), channel_id=1, source_target_pairs={{0,16},{16,0},{32,48},{48,32},{64,80},{80,64},{96,112},{112,96},{1... | collective-permute-start | bytes 2162696 | tf_op jit(solution)/shard_map/ppermute | solution.py:250
  83.1 19.6 %collective-permute-start.8 = (bf16[704,512]{1,0:T(8,128)(2,1)S(1)}, bf16[704,512]{1,0:T(8,128)(2,1)}, u32[]{:S(2)}, u32[]{:S(2)}) collective-permute-start(bf16[704,512]{1,0:T(8,128)(2,1)S(1)} %collective-permute-done.4.refs_2_), channel_id=1, source_target_pairs={{0,16},{16,0},{32,48},{48,32},{64,80},{80,64},{96,112},{112,96},{1... | collective-permute-start | bytes 2162696 | tf_op jit(solution)/shard_map/ppermute | solution.py:250
